TPU v7x, 32 devices: a whole 2x2x4 slice. The times are simulated.
32 devices in a mesh: rep: 2 (over y), seq: 4 (over z), tp: 2 (over x), sub: 2 (over core).
Axes of the slice: x: 2, y: 2, z: 4, core: 2. Of those that a mesh axis runs over, the one named last changes fastest.
Arguments:
- latents: bfloat16 [3072, 3072], P(('rep', 'seq')), parts along dimension 0, may hold values from -6 to 6
- w_qkv: bfloat16 [3072, 3, 24, 128], P('seq', None, ('tp', 'sub')), may hold values from -0.109375 to 0.109375
- w_out: bfloat16 [24, 128, 3072], P(('tp', 'sub'), None, 'seq'), may hold values from -0.15625 to 0.15625
- query_gain: float32 [128], replicated, may hold values from 1.5 to 20
- key_gain: float32 [128], replicated, may hold values from 1.5 to 20
- mod_shift: float32 [6144], P('rep'), parts along dimension 0, may hold values from -3 to 3
- mod_scale: float32 [6144], P('rep'), parts along dimension 0, may hold values from -0.5 to 0.5
- mod_gate: float32 [6144], P('rep'), parts along dimension 0, may hold values from 0.5 to 1.5
- block_list: int32 [8, 9], P(('rep', 'seq')), parts along dimension 0, may hold values from 0 to 3, as said below
- block_live: int32 [8, 9], P(('rep', 'seq')), parts along dimension 0, may hold values from 0 to 1, as said below
- key_valid: int32 [3072], P(('rep', 'seq')), parts along dimension 0, may hold values from 0 to 1, as said below
Outputs:
- block_out: bfloat16 [3072, 3072], P(('rep', 'seq'), ('tp', 'sub')), parts along dimension 0
There are 2 independent parts, one for each index of `rep`. A program takes and returns all parts, laid end to end along the dimension named above; an argument that names none is the same for every part. Nothing has to cross between parts.
Inputs may be any that keep to these rules, and one draw needn't show every extreme that they name: `block_list`: tiles are numbered frame by frame, 2 tiles to a frame of tiles. Row a lists, in a drawn order, the tiles within 1 frames of tiles and 1 tile column of tile a; entries outside the video or dropped have block_live 0, and those outside the video repeat a. Live entries are distinct, and a itself is always live. `block_live`: see block_list. `key_valid`: within each tile either all tokens are real or the last 144 are padding.
All inputs are finite; a program needn't handle non-finite values.
Results may differ from a plain program's by a relative error of at most 0.012.
The roundings to bfloat16 on the way count: a program that leaves them out, or rounds other values in their place, can miss the bound.
Values may be sent and summed in bfloat16 or wider, within the bound.
No kernel may reach another device: no remote copies, remote signals or barrier semaphores. Data moves between devices by JAX's collectives and lax.ppermute only.
A program may use at most 128 MiB of HBM per device.

v0:
```python
import functools
import math

import jax
import jax.numpy as jnp
from jax import lax
from jax.experimental import pallas as pl
from jax.experimental.pallas import tpu as pltpu
from jax.sharding import PartitionSpec as P


AXES = ("rep", "seq", "tp", "sub")
EPS = 1e-06
NEG = -1e30
F32 = jnp.float32
BF16 = jnp.bfloat16


def norm_kernel(half_ref, x_ref, shift_ref, scale_ref, out_ref):
    x_float = x_ref[...].astype(F32)
    centre = x_float - jnp.mean(x_float, axis=-1, keepdims=True)
    spread = jnp.mean(centre * centre, axis=-1, keepdims=True)
    scaled = centre * lax.rsqrt(spread + EPS) * (1.0 + scale_ref[...])
    out_ref[...] = (scaled + shift_ref[...]).astype(BF16)


def norm_rows(latents, mod_shift, mod_scale, half):
    rows, width = latents.shape
    steps = 4
    block = rows // 2 // steps
    vector = pl.BlockSpec((1, width), lambda i, half_ref: (0, 0))
    return pl.pallas_call(
        norm_kernel,
        out_shape=jax.ShapeDtypeStruct((rows // 2, width), BF16),
        grid_spec=pltpu.PrefetchScalarGridSpec(
            num_scalar_prefetch=1,
            grid=(steps,),
            in_specs=[
                pl.BlockSpec((block, width), lambda i, half_ref: (half_ref[0] * steps + i, 0)),
                vector,
                vector,
            ],
            out_specs=pl.BlockSpec((block, width), lambda i, half_ref: (i, 0)),
        ),
        compiler_params=pltpu.CompilerParams(vmem_limit_bytes=12 << 20),
        cost_estimate=pl.CostEstimate(flops=rows * width * 5, bytes_accessed=rows * width * 2, transcendentals=rows),
        name="norm_rows",
    )(half[None], latents, mod_shift[None], mod_scale[None])


def head_norm(raw, gain):
    square = jnp.mean(raw * raw, axis=-1, keepdims=True)
    return (raw * lax.rsqrt(square + EPS) * gain).astype(BF16)


def qkv_kernel(count, sc_ref, *refs):
    mine, others = refs[:count], refs[count : 2 * count]
    za, ya, ca1, ca2, own_w, own_c, zb, yb, cb1, cb2, gq_ref, gk_ref = refs[2 * count : 2 * count + 12]
    q_ref, kv_ref, tok_ref, acc_ref = refs[2 * count + 12 :]
    half_rows = mine[0].shape[0]
    _, heads, depth, hd = za.shape
    col = sc_ref[5]
    for i in range(count):

        @pl.when(sc_ref[7] == i)
        def _():
            tok_ref[pl.ds(pl.multiple_of(col * half_rows, 64), half_rows), :] = mine[i][...]
            tok_ref[pl.ds(pl.multiple_of((1 - col) * half_rows, 64), half_rows), :] = others[i][...]

    def lanes_of(ref, rows):
        return jnp.concatenate([ref[s, h, rows, :] for s in range(3) for h in range(heads)], axis=1)

    def add(block, halves, fresh=False):
        base = sc_ref[block] * (2 * depth)
        if len(halves) == 2:
            cols = [
                tok_ref[:, pl.ds(pl.multiple_of(base + h * depth, 128), depth)] for h in (sc_ref[4], 1 - sc_ref[4])
            ]
            toks = jnp.concatenate(cols, axis=1)
            w = jnp.concatenate([lanes_of(r, slice(None)) for r in halves], axis=0)
        else:
            toks = tok_ref[:, pl.ds(pl.multiple_of(base, 128), 2 * depth)]
            w = lanes_of(halves[0], slice(None))
        term = jnp.dot(toks, w, preferred_element_type=F32)
        acc_ref[...] = term if fresh else acc_ref[...] + term

    add(0, (za, ya), fresh=True)
    add(1, (ca1, ca2))

    @pl.when(sc_ref[6] == 1)
    def _():
        add(2, (own_w,))
        add(3, (cb1, cb2))

    @pl.when(sc_ref[6] == 0)
    def _():
        add(2, (own_c,))
        add(3, (zb, yb))

    for h in range(heads):
        lanes = slice(h * hd, (h + 1) * hd)
        q_ref[:, lanes] = head_norm(acc_ref[:, lanes], gq_ref[...])
        kv_ref[:, lanes] = head_norm(acc_ref[:, (heads + h) * hd : (heads + h + 1) * hd], gk_ref[...])
    kv_ref[:, heads * hd :] = acc_ref[:, 2 * heads * hd :].astype(BF16)


def qkv_tile(scalars, mine, others, weights, query_gain, key_gain):
    half_rows, width = mine[0].shape
    _, heads, _, hd = weights[0].shape
    rows, out = 2 * half_rows, heads * hd
    smem = pl.BlockSpec(memory_space=pltpu.SMEM)
    vmem = pl.BlockSpec(memory_space=pltpu.VMEM)
    return pl.pallas_call(
        functools.partial(qkv_kernel, len(mine)),
        out_shape=(
            jax.ShapeDtypeStruct((rows, out), BF16),
            jax.ShapeDtypeStruct((rows, 2 * out), BF16),
        ),
        in_specs=[smem] + [vmem] * (2 * len(mine) + len(weights) + 2),
        out_specs=(vmem, vmem),
        scratch_shapes=[pltpu.VMEM((rows, width), BF16), pltpu.VMEM((rows, 3 * out), F32)],
        compiler_params=pltpu.CompilerParams(vmem_limit_bytes=32 << 20),
        cost_estimate=pl.CostEstimate(
            flops=6 * rows * width * out, bytes_accessed=width * 3 * out * 2, transcendentals=0
        ),
        name="qkv_tile",
    )(scalars, *mine, *others, *weights, query_gain[None], key_gain[None])


def attend_kernel(sc_ref, q_ref, kvs0, kvs1, kvs2, kvs3, flags_ref, out_ref):
    kv_refs = (kvs0, kvs1, kvs2, kvs3)
    rows, width = q_ref.shape
    hd = 128
    heads = width // hd
    factor = math.log2(math.e) / math.sqrt(hd)
    flags = flags_ref[...]
    place = lax.broadcasted_iota(jnp.int32, flags.shape, 0)

    def row(d):
        return jnp.sum(jnp.where(place == d, flags, 0), axis=0, keepdims=True)

    hits = row(sc_ref[8])[:, rows:]
    lane = lax.broadcasted_iota(jnp.int32, hits.shape, 1)
    biases = []
    for s in range(4):
        hit = jnp.sum(jnp.where(lane == sc_ref[s], hits, 0), axis=1, keepdims=True)
        valid = row(sc_ref[4 + s])[:, :rows]
        biases.append(jnp.where(valid * hit > 0, 0.0, NEG).astype(F32))
    bias = jnp.concatenate(biases, axis=1)
    for h in range(heads):
        lanes = slice(h * hd, (h + 1) * hd)
        keys = jnp.concatenate([r[:, lanes] for r in kv_refs], axis=0)
        vals = jnp.concatenate([r[:, width + h * hd : width + (h + 1) * hd] for r in kv_refs], axis=0)
        scores = lax.dot_general(
            q_ref[:, lanes], keys, (((1,), (1,)), ((), ())), preferred_element_type=F32
        )
        scores = scores * factor + bias
        weights = jnp.exp2(scores - jnp.max(scores, axis=1, keepdims=True))
        total = jnp.sum(weights, axis=1, keepdims=True)
        added = jnp.dot(weights.astype(BF16), vals, preferred_element_type=F32)
        out_ref[:, lanes] = (added / total).astype(BF16)


def attend(scalars, queries, kvs, flags):
    rows, width = queries.shape
    smem = pl.BlockSpec(memory_space=pltpu.SMEM)
    vmem = pl.BlockSpec(memory_space=pltpu.VMEM)
    keys = 4 * rows
    return pl.pallas_call(
        attend_kernel,
        out_shape=jax.ShapeDtypeStruct((rows, width), BF16),
        in_specs=[smem] + [vmem] * 6,
        out_specs=vmem,
        compiler_params=pltpu.CompilerParams(vmem_limit_bytes=32 << 20),
        cost_estimate=pl.CostEstimate(
            flops=4 * rows * keys * width, bytes_accessed=8 * rows * width * 2, transcendentals=rows * keys * width // 128
        ),
        name="attend",
    )(scalars, queries, *kvs, flags)


def project_kernel(sc_ref, an, bn, ap, bp, f0, f1, wo, c_f, s1, y_f, g_z, y_g, out_ref, att_ref):
    _, width = an.shape
    depth = wo.shape[0]

    def put(place, piece_ref):
        att_ref[:, pl.ds(pl.multiple_of(place * width, 128), width)] = piece_ref[...]

    @pl.when(sc_ref[0] == 1)
    def _():
        put(sc_ref[3], an)
        put(sc_ref[4], ap)

    @pl.when(sc_ref[0] == 0)
    def _():
        put(sc_ref[3], bn)
        put(sc_ref[4], bp)

    put(sc_ref[5], f0)
    put(sc_ref[6], f1)

    def term(group, w_ref):
        part = att_ref[:, pl.ds(pl.multiple_of(group * depth, 128), depth)]
        return jnp.dot(part, w_ref[...], preferred_element_type=F32).astype(BF16).astype(F32)

    def block(group, first, second):
        out_ref[...] = (term(group, first) + term(1 - group, second)).astype(out_ref.dtype)

    @pl.when((sc_ref[7] == 1) & (sc_ref[0] == 1))
    def _():
        block(sc_ref[1], wo, c_f)

    @pl.when((sc_ref[7] == 1) & (sc_ref[0] == 0))
    def _():
        block(sc_ref[2], s1, y_f)

    @pl.when(sc_ref[7] == 0)
    def _():
        block(sc_ref[2], g_z, y_g)


def project(scalars, pieces, weights, dtype):
    rows, _ = pieces[0].shape
    depth, width = weights[0].shape
    smem = pl.BlockSpec(memory_space=pltpu.SMEM)
    vmem = pl.BlockSpec(memory_space=pltpu.VMEM)
    return pl.pallas_call(
        project_kernel,
        out_shape=jax.ShapeDtypeStruct((rows, width), dtype),
        in_specs=[smem] + [vmem] * (len(pieces) + len(weights)),
        out_specs=vmem,
        scratch_shapes=[pltpu.VMEM((rows, 2 * depth), BF16)],
        compiler_params=pltpu.CompilerParams(vmem_limit_bytes=16 << 20),
        cost_estimate=pl.CostEstimate(
            flops=4 * rows * depth * width, bytes_accessed=4 * depth * width * 2, transcendentals=0
        ),
        name="project",
    )(scalars, *pieces, *weights)


def scalars_of(*values):
    return jnp.stack([jnp.asarray(v, jnp.int32) for v in values])


def line_local(
    sizes,
    latents,
    w_qkv,
    w_out,
    query_gain,
    key_gain,
    mod_shift,
    mod_scale,
    mod_gate,
    block_list,
    block_live,
    key_valid,
):
    ny, nz, nx, nc = sizes
    y, z, x, c = (lax.axis_index(a) for a in AXES)

    def move(array, target):
        pairs = []
        for yy in range(ny):
            for zz in range(nz):
                for xx in range(nx):
                    for cc in range(nc):
                        to = target(yy, zz, xx, cc)
                        if to is not None:
                            flat = lambda p: ((p[0] * nz + p[1]) * nx + p[2]) * nc + p[3]
                            pairs.append((flat((yy, zz, xx, cc)), flat(to)))
        return lax.ppermute(array, AXES, pairs)

    def owns(zz, cc):
        return zz % 2 == cc

    def home(zz, cc):
        return zz // 2 == cc

    def mid(zz):
        return zz in (1, 2)

    def to_core(who=lambda zz, cc: True):
        return lambda yy, zz, xx, cc: (yy, zz, xx, 1 - cc) if who(zz, cc) else None

    def to_column(who=lambda zz, cc: True):
        return lambda yy, zz, xx, cc: (yy, zz, 1 - xx, cc) if who(zz, cc) else None

    def to_replica(who=lambda zz, cc: True):
        return lambda yy, zz, xx, cc: (1 - yy, zz, xx, cc) if who(zz, cc) else None

    own = z % 2 == c
    at_home = z // 2 == c
    is_mid = (z == 1) | (z == 2)
    pair = z // 2
    parity = z % 2
    near, far = 2 * pair + c, 2 * (1 - pair) + c
    near_o, far_o = 2 * pair + 1 - c, 2 * (1 - pair) + 1 - c

    depth, _, heads_here, hd = w_qkv.shape
    heads = heads_here * nc // nz
    half = depth // 2
    w_t = jnp.transpose(w_qkv, (1, 2, 0, 3))
    wo = w_out.reshape(heads_here * hd, w_out.shape[2])

    def mid_own(zz, cc):
        return mid(zz) and owns(zz, cc)

    def mid_rest(zz, cc):
        return mid(zz) and not owns(zz, cc)

    def end_own(zz, cc):
        return not mid(zz) and owns(zz, cc)

    def end_rest(zz, cc):
        return not mid(zz) and not owns(zz, cc)

    def across(who):
        return lambda yy, zz, xx, cc: (yy, 3 - zz, xx, cc) if who(zz, cc) else None

    def outward(who):
        return lambda yy, zz, xx, cc: (yy, zz ^ 1, xx, cc) if who(zz, cc) else None

    n_mine = norm_rows(latents, mod_shift, mod_scale, x)
    r1 = move(n_mine, outward(owns))
    r2a = move(n_mine, across(mid_own))

    slot_a = jnp.where(at_home, 1 - parity, parity)
    slot_b = jnp.where(at_home, parity, 1 - parity)
    msg_a = lax.dynamic_slice(w_t, (0, slot_a * heads, y * half, 0), (3, heads, half, hd))
    msg_b = lax.dynamic_slice(w_t, (0, slot_b * heads, y * half, 0), (3, heads, half, hd))
    z_a = move(msg_a, lambda yy, zz, xx, cc: (yy, zz ^ 1, xx, 1) if home(zz, cc) else (yy, zz ^ 2, xx, 0))
    z_b = move(msg_b, lambda yy, zz, xx, cc: None if home(zz, cc) else (yy, zz ^ 3, xx, zz // 2))

    tile_ids = jnp.arange(nz, dtype=jnp.int32)
    hits = jnp.any((block_list[0][:, None] == tile_ids[None]) & (block_live[0][:, None] > 0), axis=0)
    flags = jnp.concatenate([key_valid, jnp.pad(hits.astype(jnp.int32), (0, 128 - nz))])[None]
    flags = jnp.concatenate(
        [flags]
        + [move(flags, lambda yy, zz, xx, cc, d=d: (yy, zz ^ d, xx, cc)) for d in range(1, nz)]
    )

    n_other = norm_rows(latents, mod_shift, mod_scale, 1 - x)
    own_w = lax.dynamic_slice(w_t, (0, parity * heads, 0, 0), (3, heads, depth, hd))

    r2b = move(r1, across(mid_rest))
    x_r1 = move(r1, to_column(lambda zz, cc: not owns(zz, cc)))
    r3a = move(r2a, outward(mid_rest))
    x_r2a = move(r2a, to_column(mid_rest))
    r3b = move(r2b, outward(mid_own))
    x_r2b = move(r2b, to_column(mid_own))
    x_r3a = move(r3a, to_column(end_own))
    x_r3b = move(r3b, to_column(end_rest))

    y_a = move(z_a, to_replica())
    c_a1 = move(z_a, to_core())
    c_own = move(own_w, to_core(home))
    y_b = move(z_b, to_replica(lambda zz, cc: not home(zz, cc)))
    c_b1 = move(z_b, to_core(lambda zz, cc: not home(zz, cc)))
    c_a2 = move(y_a, to_core())
    c_b2 = move(y_b, to_core(lambda zz, cc: not home(zz, cc)))
    weights = (z_a, y_a, c_a1, c_a2, own_w, c_own, z_b, y_b, c_b1, c_b2)
    sources = (
        jnp.where(c == 0, z ^ 2, z ^ 1),
        jnp.where(c == 0, z ^ 1, z ^ 2),
        z,
        z ^ 3,
        y,
        x,
        at_home,
    )

    s1 = move(wo, lambda yy, zz, xx, cc: (yy, zz ^ 1, xx, zz % 2) if cc == yy else None)
    s2a = move(wo, lambda yy, zz, xx, cc: (yy, 3 - zz, xx, zz % 2) if cc == yy and mid(zz) else None)
    c_f = move(wo, to_core(lambda zz, cc: not owns(zz, cc)))
    s2b = move(s1, across(mid_rest))
    y_f = move(s1, to_replica(lambda zz, cc: not owns(zz, cc)))
    s3a = move(s2a, outward(mid_rest))
    s3b = move(s2b, outward(mid_own))
    g_z = jnp.where(is_mid, jnp.where(own, s2b, s2a), jnp.where(own, s3a, s3b))
    y_g = move(g_z, to_replica())

    q_near, kv_near = qkv_tile(
        scalars_of(*sources, jnp.where(own, 0, 1)), (n_mine, r1), (n_other, x_r1), weights, query_gain, key_gain
    )
    kv_near_o = move(kv_near, to_core())
    q_far, kv_far = qkv_tile(
        scalars_of(*sources, jnp.where(is_mid, jnp.where(own, 1, 0), jnp.where(own, 2, 3))),
        (r2a, r2b, r3a, r3b),
        (x_r2a, x_r2b, x_r3a, x_r3b),
        weights,
        query_gain,
        key_gain,
    )
    kv_far_o = move(kv_far, to_core())

    segments = (near, far, near_o, far_o)
    marks = (*segments, *(s ^ z for s in segments))
    kvs = (kv_near, kv_far, kv_near_o, kv_far_o)
    att_far = attend(scalars_of(*marks, far ^ z), q_far, kvs, flags)
    p_far = move(att_far, lambda yy, zz, xx, cc: (yy, 2 * (1 - zz // 2) + cc, xx, zz % 2))
    att_near = attend(scalars_of(*marks, near ^ z), q_near, kvs, flags)
    p_near = move(att_near, outward(lambda zz, cc: not owns(zz, cc)))
    b_near = move(att_near, to_core(owns))
    p_far_o = move(p_far, to_core())
    b_pair = move(p_near, to_core(owns))

    pieces = (att_near, b_near, p_near, b_pair, p_far, p_far_o)
    blocks = (wo, c_f, s1, y_f, g_z, y_g)
    places = (own, c, y, z, z ^ 1, far, far_o)
    send = project(scalars_of(*places, x != pair), pieces, blocks, BF16)
    got = move(send, to_column())
    keep = project(scalars_of(*places, x == pair), pieces, blocks, F32)
    projected = keep + got.astype(F32)
    out_width = projected.shape[1]
    offset = (x * nc + c) * out_width
    latent_cols = lax.dynamic_slice_in_dim(latents, offset, out_width, 1).astype(F32)
    gate_cols = lax.dynamic_slice_in_dim(mod_gate, offset, out_width, 0)
    return (latent_cols + gate_cols * projected).astype(BF16)


def modulate(latents, mod_shift, mod_scale):
    x_float = latents.astype(F32)
    centre = x_float - jnp.mean(x_float, axis=-1, keepdims=True)
    spread = jnp.mean(centre * centre, axis=-1, keepdims=True)
    return (centre * lax.rsqrt(spread + EPS) * (1.0 + mod_scale) + mod_shift).astype(BF16)


def gather_local(
    latents,
    w_qkv,
    w_out,
    query_gain,
    key_gain,
    mod_shift,
    mod_scale,
    mod_gate,
    block_list,
    block_live,
    key_valid,
):
    gather = functools.partial(lax.all_gather, axis_name="seq", tiled=True)
    tok_rows = latents.shape[0]
    tile = tok_rows // block_list.shape[0]
    tiles_all = block_list.shape[0] * lax.axis_size("seq")
    normed = modulate(latents, mod_shift, mod_scale)
    qkv = jnp.einsum("td,dshe->tshe", normed, gather(w_qkv, axis=0), preferred_element_type=F32)
    queries = head_norm(qkv[:, 0], query_gain)
    keys = gather(head_norm(qkv[:, 1], key_gain), axis=0)
    values = gather(qkv[:, 2].astype(BF16), axis=0)
    key_ok = gather(key_valid, axis=0) > 0
    tile_ids = jnp.arange(tiles_all, dtype=jnp.int32)
    hits = jnp.any(
        (block_list[:, :, None] == tile_ids[None, None, :]) & (block_live[:, :, None] > 0), axis=1
    )
    allowed = jnp.repeat(jnp.repeat(hits, tile, axis=0), tile, axis=1) & key_ok[None, :]
    scores = jnp.einsum("qhe,khe->hqk", queries, keys, preferred_element_type=F32) / math.sqrt(
        queries.shape[-1]
    )
    masked = jnp.where(allowed[None], scores, NEG)
    weights = jnp.where(allowed[None], jnp.exp(masked - jnp.max(masked, axis=2, keepdims=True)), 0.0)
    total = jnp.sum(weights, axis=2)
    weighted = jnp.einsum("hqk,khe->qhe", weights.astype(BF16), values, preferred_element_type=F32)
    attended = (weighted / jnp.transpose(total)[:, :, None]).astype(BF16)
    head_terms = jnp.einsum("the,hec->tc", attended, gather(w_out, axis=2), preferred_element_type=F32)
    projected = lax.psum_scatter(
        head_terms.astype(BF16), ("tp", "sub"), scatter_dimension=1, tiled=True
    ).astype(F32)
    out_width = projected.shape[1]
    offset = lax.axis_index(("tp", "sub")) * out_width
    latent_cols = lax.dynamic_slice_in_dim(latents, offset, out_width, 1).astype(F32)
    gate_cols = lax.dynamic_slice_in_dim(mod_gate, offset, out_width, 0)
    return (latent_cols + gate_cols * projected).astype(BF16)


def solution(mesh):
    sizes = tuple(mesh.shape[a] for a in AXES)
    ny, nz, nx, nc = sizes
    line = ny == nx == nc == 2 and nz == nc * 2

    def local(*args):
        heads_here, block_list = args[1].shape[2], args[8]
        if line and heads_here % nc == 0 and block_list.shape[0] == 1:
            return line_local(sizes, *args)
        return gather_local(*args)

    in_specs = (
        P(("rep", "seq"), None),
        P("seq", None, ("tp", "sub"), None),
        P(("tp", "sub"), None, "seq"),
        P(),
        P(),
        P("rep"),
        P("rep"),
        P("rep"),
        P(("rep", "seq"), None),
        P(("rep", "seq"), None),
        P(("rep", "seq")),
    )
    out_specs = P(("rep", "seq"), ("tp", "sub"))
    return jax.shard_map(local, mesh=mesh, in_specs=in_specs, out_specs=out_specs, check_vma=False)
```

profile of v0, /device:TPU:8, one launch (start us, length us, event | category | flops | bytes accessed | tf_op | source)
XLA Modules:
  0.0 214.6 jit_solution(805822811165105515)
XLA Ops:
  0.0 3.0 %dynamic-slice_bitcast_fusion.1 = (bf16[3,3,384,128]{3,2,1,0:T(8,128)(2,1)}, bf16[3,3,384,128]{3,2,1,0:T(8,128)(2,1)}) fusion(bf16[768,3,6,128]{3,0,2,1:T(8,128)(2,1)} %param.12, s32[]{:T(128)S(6)} %select_n.81, s32[]{:T(128)S(6)} %select_n.86, s32[]{:T(128)S(6)} %select_n.83), kind=kLoop, calls=%fused_computation.3 | loop fusion | bytes 3538956 | tf_op jit(solution)/shard_map/dynamic_slice | solution.py:331
  3.0 1.6 collective-permute-start.7
  4.6 2.5 %norm_rows.2.refs_0_ = bf16[192,3072]{1,0:T(8,128)(2,1)} custom-call(s32[1]{0:T(128)} %bitcast.17.half_ref, bf16[384,3072]{1,0:T(8,128)(2,1)S(1)} %copy-done, f32[1,3072]{1,0:T(1,128)S(1)} %bitcast.38, f32[1,3072]{1,0:T(1,128)S(1)} %bitcast.40), custom_call_target="tpu_custom_call" | custom-call | flops 5898240 | bytes 2359296 | tf_op jit(solution)/shard_map/norm_rows/pallas_call | solution.py:32
  8.4 1.3 collective-permute-start.11
  9.7 1.6 dynamic-slice_bitcast_fusion.refs_8_.refs_12_
  11.3 9.3 %collective-permute-start.6 = (bf16[3,3,768,128]{3,2,1,0:T(8,128)(2,1)S(1)}, bf16[3,3,768,128]{3,2,1,0:T(8,128)(2,1)S(1)}, u32[]{:S(2)}, u32[]{:S(2)}) collective-permute-start(bf16[3,3,768,128]{3,2,1,0:T(8,128)(2,1)S(1)} %dynamic-slice_bitcast_fusion.refs_8_.refs_12_), channel_id=1, source_target_pairs={{0,1},{2,3},{4,5},{6,7},{9,8},{11,10},{13,12},{15,14},{16,17},{18,... | collective-permute-start | bytes 5308424 | tf_op jit(solution)/shard_map/ppermute | solution.py:272
  20.6 9.2 %collective-permute-done.2.refs_4_.refs_8_ = bf16[3,3,384,128]{3,2,1,0:T(8,128)(2,1)} collective-permute-done((bf16[3,3,384,128]{3,2,1,0:T(8,128)(2,1)}, bf16[3,3,384,128]{3,2,1,0:T(8,128)(2,1)}, u32[]{:S(2)}, u32[]{:S(2)}) %collective-permute-start.2) | collective-permute-done | bytes 884768 | tf_op jit(solution)/shard_map/ppermute | solution.py:272
  29.8 4.3 %collective-permute-start.30 = (bf16[768,768]{1,0:T(8,128)(2,1)}, bf16[768,768]{1,0:T(8,128)(2,1)S(1)}, u32[]{:S(2)}, u32[]{:S(2)}) collective-permute-start(bf16[768,768]{1,0:T(8,128)(2,1)} %bitcast.32.wo), channel_id=1, source_target_pairs={{0,4},{2,6},{4,1},{6,3},{8,12},{10,14},{12,9},{14,11},{17,20},{19,... | collective-permute-start | bytes 3538952 | tf_op jit(solution)/shard_map/ppermute | solution.py:272
  34.1 1.9 collective-permute-start.33
  36.1 11.3 %collective-permute-done.refs_1_ = bf16[192,3072]{1,0:T(8,128)(2,1)} collective-permute-done((bf16[192,3072]{1,0:T(8,128)(2,1)}, bf16[192,3072]{1,0:T(8,128)(2,1)}, u32[]{:S(2)}, u32[]{:S(2)}) %collective-permute-start) | collective-permute-done | bytes 1179680 | tf_op jit(solution)/shard_map/ppermute | solution.py:272
  47.4 3.7 %collective-permute-start.3 = (bf16[3,3,384,128]{3,2,1,0:T(8,128)(2,1)}, bf16[3,3,384,128]{3,2,1,0:T(8,128)(2,1)S(1)}, u32[]{:S(2)}, u32[]{:S(2)}) collective-permute-start(bf16[3,3,384,128]{3,2,1,0:T(8,128)(2,1)} %collective-permute-done.2.refs_4_.refs_8_), channel_id=1, source_target_pairs={{0,16},{1,17},{2,18},{3,19},{4,20},{5,21},{6,22},{7,23},{8,24},{9,... | collective-permute-start | bytes 2654216 | tf_op jit(solution)/shard_map/ppermute | solution.py:272
  51.1 6.0 %collective-permute-done.11.refs_0_ = bf16[192,3072]{1,0:T(8,128)(2,1)} collective-permute-done((bf16[192,3072]{1,0:T(8,128)(2,1)}, bf16[192,3072]{1,0:T(8,128)(2,1)}, u32[]{:S(2)}, u32[]{:S(2)}) %collective-permute-start.11) | collective-permute-done | bytes 1179680 | tf_op jit(solution)/shard_map/ppermute | solution.py:272
  57.0 12.6 %collective-permute-start.4 = (bf16[3,3,384,128]{3,2,1,0:T(8,128)(2,1)}, bf16[3,3,384,128]{3,2,1,0:T(8,128)(2,1)S(1)}, u32[]{:S(2)}, u32[]{:S(2)}) collective-permute-start(bf16[3,3,384,128]{3,2,1,0:T(8,128)(2,1)} %collective-permute-done.2.refs_4_.refs_8_), channel_id=1, source_target_pairs={{0,1},{1,0},{2,3},{3,2},{4,5},{5,4},{6,7},{7,6},{8,9},{9,8},{10,11... | collective-permute-start | bytes 2654216 | tf_op jit(solution)/shard_map/ppermute | solution.py:272
  69.7 5.3 %collective-permute-start.12 = (bf16[192,3072]{1,0:T(8,128)(2,1)}, bf16[192,3072]{1,0:T(8,128)(2,1)}, u32[]{:S(2)}, u32[]{:S(2)}) collective-permute-start(bf16[192,3072]{1,0:T(8,128)(2,1)} %collective-permute-done.refs_1_), channel_id=1, source_target_pairs={{4,8},{6,10},{9,5},{11,7},{20,24},{22,26},{25,21},{27,23}} | collective-permute-start | bytes 3538952 | tf_op jit(solution)/shard_map/ppermute | solution.py:272
  75.7 1.3 collective-permute-start.9
  78.0 3.4 %collective-permute-start.1 = (bf16[192,3072]{1,0:T(8,128)(2,1)}, bf16[192,3072]{1,0:T(8,128)(2,1)S(1)}, u32[]{:S(2)}, u32[]{:S(2)}) collective-permute-start(bf16[192,3072]{1,0:T(8,128)(2,1)} %collective-permute-done.refs_1_), channel_id=1, source_target_pairs={{1,3},{3,1},{4,6},{6,4},{9,11},{11,9},{12,14},{14,12},{17,19},{19,... | collective-permute-start | bytes 3538952 | tf_op jit(solution)/shard_map/ppermute | solution.py:272
  81.4 2.3 %collective-permute-start.13 = (bf16[192,3072]{1,0:T(8,128)(2,1)}, bf16[192,3072]{1,0:T(8,128)(2,1)}, u32[]{:S(2)}, u32[]{:S(2)}) collective-permute-start(bf16[192,3072]{1,0:T(8,128)(2,1)} %collective-permute-done.11.refs_0_), channel_id=1, source_target_pairs={{4,0},{6,2},{9,13},{11,15},{20,16},{22,18},{25,29},{27,31}} | collective-permute-start | bytes 3538952 | tf_op jit(solution)/shard_map/ppermute | solution.py:272
  83.7 2.4 %collective-permute-start.15 = (bf16[192,3072]{1,0:T(8,128)(2,1)}, bf16[192,3072]{1,0:T(8,128)(2,1)S(1)}, u32[]{:S(2)}, u32[]{:S(2)}) collective-permute-start(bf16[192,3072]{1,0:T(8,128)(2,1)} %collective-permute-done.11.refs_0_), channel_id=1, source_target_pairs={{4,6},{6,4},{9,11},{11,9},{20,22},{22,20},{25,27},{27,25}} | collective-permute-start | bytes 3538952 | tf_op jit(solution)/shard_map/ppermute | solution.py:272
  87.1 6.0 %collective-permute-start.32 = (bf16[768,768]{1,0:T(8,128)(2,1)S(1)}, bf16[768,768]{1,0:T(8,128)(2,1)}, u32[]{:S(2)}, u32[]{:S(2)}) collective-permute-start(bf16[768,768]{1,0:T(8,128)(2,1)S(1)} %collective-permute-done.30.s1), channel_id=1, source_target_pairs={{4,8},{6,10},{9,5},{11,7},{20,24},{22,26},{25,21},{27,23}} | collective-permute-start | bytes 3538952 | tf_op jit(solution)/shard_map/ppermute | solution.py:272
  93.1 1.8 collective-permute-start.14
  94.9 1.4 collective-permute-done.1.refs_3_
  98.2 4.3 %collective-permute-done.13.refs_2_ = bf16[192,3072]{1,0:T(8,128)(2,1)} collective-permute-done((bf16[192,3072]{1,0:T(8,128)(2,1)}, bf16[192,3072]{1,0:T(8,128)(2,1)}, u32[]{:S(2)}, u32[]{:S(2)}) %collective-permute-start.13) | collective-permute-done | bytes 1179680 | tf_op jit(solution)/shard_map/ppermute | solution.py:272
  104.8 4.1 %collective-permute-done.15.refs_4_ = bf16[192,3072]{1,0:T(8,128)(2,1)S(1)} collective-permute-done((bf16[192,3072]{1,0:T(8,128)(2,1)}, bf16[192,3072]{1,0:T(8,128)(2,1)S(1)}, u32[]{:S(2)}, u32[]{:S(2)}) %collective-permute-start.15) | collective-permute-done | bytes 1179680 | tf_op jit(solution)/shard_map/ppermute | solution.py:272
  110.0 1.7 collective-permute-start.16
  111.6 1.7 collective-permute-start.17
  113.3 1.7 collective-permute-start.18
  115.9 2.3 %collective-permute-start.34 = (bf16[768,768]{1,0:T(8,128)(2,1)}, bf16[768,768]{1,0:T(8,128)(2,1)}, u32[]{:S(2)}, u32[]{:S(2)}) collective-permute-start(bf16[768,768]{1,0:T(8,128)(2,1)} %collective-permute-done.33), channel_id=1, source_target_pairs={{4,0},{6,2},{9,13},{11,15},{20,16},{22,18},{25,29},{27,31}} | collective-permute-start | bytes 3538952 | tf_op jit(solution)/shard_map/ppermute | solution.py:272
  119.2 1.7 collective-permute-start.35
  121.6 1.7 copy-done.1
  124.1 1.3 norm_rows.3.refs_2_
  129.6 7.1 %qkv_tile.2 = (bf16[384,384]{1,0:T(8,128)(2,1)S(1)}, bf16[384,768]{1,0:T(8,128)(2,1)}) custom-call(s32[8]{0:T(128)S(1)} %stack.149.sc_ref, bf16[192,3072]{1,0:T(8,128)(2,1)} %norm_rows.2.refs_0_, bf16[192,3072]{1,0:T(8,128)(2,1)} %collective-permute-done.refs_1_, bf16[192,3072]{1,0:T(8,128)(2,1)S(1)} %norm_rows.3.refs_2_, bf16[192,3072]{1,0:T(8,128)(2,1)S(1)} %copy-done.21, ...), custom_call_target="tpu_custom_call" | custom-call | flops 2717908992 | bytes 7077888 | tf_op jit(solution)/shard_map/qkv_tile/pallas_call | solution.py:113
  137.6 3.4 %collective-permute-start.21 = (s32[1,512]{1,0:T(1,128)S(1)}, s32[1,512]{1,0:T(1,128)S(1)}, u32[]{:S(2)}, u32[]{:S(2)}) collective-permute-start(s32[1,512]{1,0:T(1,128)S(1)} %bitcast.48), channel_id=1, source_target_pairs={{0,4},{1,5},{2,6},{3,7},{4,0},{5,1},{6,2},{7,3},{8,12},{9,13},{10,... | collective-permute-start | bytes 6152 | tf_op jit(solution)/shard_map/ppermute | solution.py:272
  141.0 8.9 %qkv_tile.3 = (bf16[384,384]{1,0:T(8,128)(2,1)S(1)}, bf16[384,768]{1,0:T(8,128)(2,1)}) custom-call(s32[8]{0:T(128)S(1)} %copy-done.27, bf16[192,3072]{1,0:T(8,128)(2,1)} %collective-permute-done.11.refs_0_, bf16[192,3072]{1,0:T(8,128)(2,1)} %collective-permute-done.12.refs_1_, bf16[192,3072]{1,0:T(8,128)(2,1)} %collective-permute-done.13.refs_2_, ...), custom_call_target="tpu_custom_call" | custom-call | flops 2717908992 | bytes 7077888 | tf_op jit(solution)/shard_map/qkv_tile/pallas_call | solution.py:113
  149.9 1.9 collective-permute-start.29
  152.4 1.8 select_select_fusion.g_z
  154.2 1.9 collective-permute-start.31
  156.8 2.0 collective-permute-start.36
  160.7 5.6 %attend.2.an = bf16[384,384]{1,0:T(8,128)(2,1)} custom-call(s32[9]{0:T(128)S(1)} %stack.141.sc_ref, bf16[384,384]{1,0:T(8,128)(2,1)S(1)} %copy-done.29, bf16[384,768]{1,0:T(8,128)(2,1)} %get-tuple-element.10.kvs0, bf16[384,768]{1,0:T(8,128)(2,1)} %get-tuple-element.11.kvs1, bf16[384,768]{1,0:T(8,128)(2,1)} %collective-permute-done.19.kvs2, ...), custom_call_target="tpu_custom_call" | custom-call | flops 905969664 | bytes 2359296 | tf_op jit(solution)/shard_map/attend/pallas_call | solution.py:169
  166.3 2.0 collective-permute-start.25
  168.3 4.9 %attend.3 = bf16[384,384]{1,0:T(8,128)(2,1)S(1)} custom-call(s32[9]{0:T(128)S(1)} %stack.152.sc_ref, bf16[384,384]{1,0:T(8,128)(2,1)S(1)} %copy-done.31, bf16[384,768]{1,0:T(8,128)(2,1)} %get-tuple-element.10.kvs0, bf16[384,768]{1,0:T(8,128)(2,1)} %get-tuple-element.11.kvs1, bf16[384,768]{1,0:T(8,128)(2,1)} %collective-permute-done.19.kvs2, ...), custom_call_target="tpu_custom_call" | custom-call | flops 905969664 | bytes 2359296 | tf_op jit(solution)/shard_map/attend/pallas_call | solution.py:169
  173.3 1.3 collective-permute-start.24
  174.6 1.3 collective-permute-start.26
  175.9 10.5 %collective-permute-done.27.f0 = bf16[384,384]{1,0:T(8,128)(2,1)} collective-permute-done((bf16[384,384]{1,0:T(8,128)(2,1)S(1)}, bf16[384,384]{1,0:T(8,128)(2,1)}, u32[]{:S(2)}, u32[]{:S(2)}) %collective-permute-start.27) | collective-permute-done | bytes 294944 | tf_op jit(solution)/shard_map/ppermute | solution.py:272
  186.5 10.9 %collective-permute-done.36.y_g = bf16[768,768]{1,0:T(8,128)(2,1)} collective-permute-done((bf16[768,768]{1,0:T(8,128)(2,1)S(1)}, bf16[768,768]{1,0:T(8,128)(2,1)}, u32[]{:S(2)}, u32[]{:S(2)}) %collective-permute-start.36) | collective-permute-done | bytes 1179680 | tf_op jit(solution)/shard_map/ppermute | solution.py:272
  197.4 4.8 %project.3 = bf16[384,768]{1,0:T(8,128)(2,1)} custom-call(s32[8]{0:T(128)S(1)} %stack.155.sc_ref, bf16[384,384]{1,0:T(8,128)(2,1)} %attend.2.an, bf16[384,384]{1,0:T(8,128)(2,1)} %collective-permute-done.24.bn, bf16[384,384]{1,0:T(8,128)(2,1)} %collective-permute-done.25.ap, bf16[384,384]{1,0:T(8,128)(2,1)} %collective-permute-done.26.bp, ...), custom_call_target="tpu_custom_call" | custom-call | flops 905969664 | bytes 4718592 | tf_op jit(solution)/shard_map/project/pallas_call | solution.py:227
  204.1 3.8 %project.2 = f32[384,768]{1,0:T(8,128)S(1)} custom-call(s32[8]{0:T(128)S(1)} %stack.134.sc_ref, bf16[384,384]{1,0:T(8,128)(2,1)} %attend.2.an, bf16[384,384]{1,0:T(8,128)(2,1)} %collective-permute-done.24.bn, bf16[384,384]{1,0:T(8,128)(2,1)} %collective-permute-done.25.ap, bf16[384,384]{1,0:T(8,128)(2,1)} %collective-permute-done.26.bp, ...), custom_call_target="tpu_custom_call" | custom-call | flops 905969664 | bytes 4718592 | tf_op jit(solution)/shard_map/project/pallas_call | solution.py:227
  207.9 4.5 %collective-permute-done.37 = bf16[384,768]{1,0:T(8,128)(2,1)} collective-permute-done((bf16[384,768]{1,0:T(8,128)(2,1)}, bf16[384,768]{1,0:T(8,128)(2,1)}, u32[]{:S(2)}, u32[]{:S(2)}) %collective-permute-start.37) | collective-permute-done | bytes 589856 | tf_op jit(solution)/shard_map/ppermute | solution.py:272
  212.4 2.3 %add_convert_fusion = bf16[384,768]{1,0:T(8,128)(2,1)} fusion(f32[384,768]{1,0:T(8,128)S(1)} %project.2, bf16[384,768]{1,0:T(8,128)(2,1)} %collective-permute-done.37, f32[768]{0:T(1024)S(1)} %dynamic_slice.16, bf16[384,3072]{1,0:T(8,128)(2,1)} %x_ref.3, s32[]{:T(128)S(6)} %select_n.75), kind=kLoop, calls=%fused_computation.1 | loop fusion | flops 1769472 | bytes 2952196 | tf_op jit(solution)/shard_map/convert_element_type | solution.py:419
  (130 shorter events, 22.6 us)
Async XLA Ops:
  0.0 4.6 %copy-start.22 = (f32[3072]{0:T(1024)S(1)}, f32[3072]{0:T(1024)}, u32[]{:S(2)}) copy-start(f32[3072]{0:T(1024)} %param.16) | copy-start | bytes 36868
  0.0 4.6 %copy-start.23 = (f32[3072]{0:T(1024)S(1)}, f32[3072]{0:T(1024)}, u32[]{:S(2)}) copy-start(f32[3072]{0:T(1024)} %param.17) | copy-start | bytes 36868
  3.0 26.8 %collective-permute-start.2 = (bf16[3,3,384,128]{3,2,1,0:T(8,128)(2,1)}, bf16[3,3,384,128]{3,2,1,0:T(8,128)(2,1)}, u32[]{:S(2)}, u32[]{:S(2)}) collective-permute-start(bf16[3,3,384,128]{3,2,1,0:T(8,128)(2,1)} %get-tuple-element.14), channel_id=1, source_target_pairs={{0,5},{1,8},{2,7},{3,10},{4,1},{5,12},{6,3},{7,14},{8,0},{9,13},{1... | collective-permute-start | bytes 2654216 | tf_op jit(solution)/shard_map/ppermute | solution.py:272
  3.0 31.1 %collective-permute-start.7 = (bf16[3,3,384,128]{3,2,1,0:T(8,128)(2,1)}, bf16[3,3,384,128]{3,2,1,0:T(8,128)(2,1)}, u32[]{:S(2)}, u32[]{:S(2)}) collective-permute-start(bf16[3,3,384,128]{3,2,1,0:T(8,128)(2,1)} %get-tuple-element.13), channel_id=1, source_target_pairs={{1,12},{3,14},{5,8},{7,10},{8,5},{10,7},{12,1},{14,3},{17,28},{19,... | collective-permute-start | bytes 2654216 | tf_op jit(solution)/shard_map/ppermute | solution.py:272
  7.1 40.3 %collective-permute-start = (bf16[192,3072]{1,0:T(8,128)(2,1)}, bf16[192,3072]{1,0:T(8,128)(2,1)}, u32[]{:S(2)}, u32[]{:S(2)}) collective-permute-start(bf16[192,3072]{1,0:T(8,128)(2,1)} %norm_rows.2.refs_0_), channel_id=1, source_target_pairs={{0,4},{2,6},{5,1},{7,3},{8,12},{10,14},{13,9},{15,11},{16,20},{18,... | collective-permute-start | bytes 3538952 | tf_op jit(solution)/shard_map/ppermute | solution.py:272
  8.4 48.6 %collective-permute-start.11 = (bf16[192,3072]{1,0:T(8,128)(2,1)}, bf16[192,3072]{1,0:T(8,128)(2,1)}, u32[]{:S(2)}, u32[]{:S(2)}) collective-permute-start(bf16[192,3072]{1,0:T(8,128)(2,1)} %norm_rows.2.refs_0_), channel_id=1, source_target_pairs={{5,9},{7,11},{8,4},{10,6},{21,25},{23,27},{24,20},{26,22}} | collective-permute-start | bytes 3538952 | tf_op jit(solution)/shard_map/ppermute | solution.py:272
  11.3 70.1 %collective-permute-start.6 = (bf16[3,3,768,128]{3,2,1,0:T(8,128)(2,1)S(1)}, bf16[3,3,768,128]{3,2,1,0:T(8,128)(2,1)S(1)}, u32[]{:S(2)}, u32[]{:S(2)}) collective-permute-start(bf16[3,3,768,128]{3,2,1,0:T(8,128)(2,1)S(1)} %dynamic-slice_bitcast_fusion.refs_8_.refs_12_), channel_id=1, source_target_pairs={{0,1},{2,3},{4,5},{6,7},{9,8},{11,10},{13,12},{15,14},{16,17},{18,... | collective-permute-start | bytes 5308424 | tf_op jit(solution)/shard_map/ppermute | solution.py:272
  29.8 39.9 %collective-permute-start.30 = (bf16[768,768]{1,0:T(8,128)(2,1)}, bf16[768,768]{1,0:T(8,128)(2,1)S(1)}, u32[]{:S(2)}, u32[]{:S(2)}) collective-permute-start(bf16[768,768]{1,0:T(8,128)(2,1)} %bitcast.32.wo), channel_id=1, source_target_pairs={{0,4},{2,6},{4,1},{6,3},{8,12},{10,14},{12,9},{14,11},{17,20},{19,... | collective-permute-start | bytes 3538952 | tf_op jit(solution)/shard_map/ppermute | solution.py:272
  34.1 40.9 %collective-permute-start.33 = (bf16[768,768]{1,0:T(8,128)(2,1)}, bf16[768,768]{1,0:T(8,128)(2,1)}, u32[]{:S(2)}, u32[]{:S(2)}) collective-permute-start(bf16[768,768]{1,0:T(8,128)(2,1)} %bitcast.32.wo), channel_id=1, source_target_pairs={{4,9},{6,11},{8,4},{10,6},{21,25},{23,27},{25,20},{27,22}} | collective-permute-start | bytes 3538952 | tf_op jit(solution)/shard_map/ppermute | solution.py:272
  47.4 28.3 %collective-permute-start.3 = (bf16[3,3,384,128]{3,2,1,0:T(8,128)(2,1)}, bf16[3,3,384,128]{3,2,1,0:T(8,128)(2,1)S(1)}, u32[]{:S(2)}, u32[]{:S(2)}) collective-permute-start(bf16[3,3,384,128]{3,2,1,0:T(8,128)(2,1)} %collective-permute-done.2.refs_4_.refs_8_), channel_id=1, source_target_pairs={{0,16},{1,17},{2,18},{3,19},{4,20},{5,21},{6,22},{7,23},{8,24},{9,... | collective-permute-start | bytes 2654216 | tf_op jit(solution)/shard_map/ppermute | solution.py:272
  57.0 20.0 %collective-permute-start.4 = (bf16[3,3,384,128]{3,2,1,0:T(8,128)(2,1)}, bf16[3,3,384,128]{3,2,1,0:T(8,128)(2,1)S(1)}, u32[]{:S(2)}, u32[]{:S(2)}) collective-permute-start(bf16[3,3,384,128]{3,2,1,0:T(8,128)(2,1)} %collective-permute-done.2.refs_4_.refs_8_), channel_id=1, source_target_pairs={{0,1},{1,0},{2,3},{3,2},{4,5},{5,4},{6,7},{7,6},{8,9},{9,8},{10,11... | collective-permute-start | bytes 2654216 | tf_op jit(solution)/shard_map/ppermute | solution.py:272
  69.7 16.5 %copy-start.2 = (bf16[768,768]{1,0:T(8,128)(2,1)}, bf16[768,768]{1,0:T(8,128)(2,1)S(1)}, u32[]{:S(2)}) copy-start(bf16[768,768]{1,0:T(8,128)(2,1)S(1)} %collective-permute-done.30.s1) | copy-start | bytes 3538948
  69.7 23.4 %collective-permute-start.12 = (bf16[192,3072]{1,0:T(8,128)(2,1)}, bf16[192,3072]{1,0:T(8,128)(2,1)}, u32[]{:S(2)}, u32[]{:S(2)}) collective-permute-start(bf16[192,3072]{1,0:T(8,128)(2,1)} %collective-permute-done.refs_1_), channel_id=1, source_target_pairs={{4,8},{6,10},{9,5},{11,7},{20,24},{22,26},{25,21},{27,23}} | collective-permute-start | bytes 3538952 | tf_op jit(solution)/shard_map/ppermute | solution.py:272
  75.0 8.7 %collective-permute-start.8 = (bf16[3,3,384,128]{3,2,1,0:T(8,128)(2,1)}, bf16[3,3,384,128]{3,2,1,0:T(8,128)(2,1)S(1)}, u32[]{:S(2)}, u32[]{:S(2)}) collective-permute-start(bf16[3,3,384,128]{3,2,1,0:T(8,128)(2,1)} %collective-permute-done.7.refs_10_.refs_14_), channel_id=1, source_target_pairs={{1,17},{3,19},{5,21},{7,23},{8,24},{10,26},{12,28},{14,30},{17,1},... | collective-permute-start | bytes 2654216 | tf_op jit(solution)/shard_map/ppermute | solution.py:272
  75.7 10.4 %collective-permute-start.9 = (bf16[3,3,384,128]{3,2,1,0:T(8,128)(2,1)}, bf16[3,3,384,128]{3,2,1,0:T(8,128)(2,1)S(1)}, u32[]{:S(2)}, u32[]{:S(2)}) collective-permute-start(bf16[3,3,384,128]{3,2,1,0:T(8,128)(2,1)} %collective-permute-done.7.refs_10_.refs_14_), channel_id=1, source_target_pairs={{1,0},{3,2},{5,4},{7,6},{8,9},{10,11},{12,13},{14,15},{17,16},{19,... | collective-permute-start | bytes 2654216 | tf_op jit(solution)/shard_map/ppermute | solution.py:272
  78.0 18.3 %collective-permute-start.1 = (bf16[192,3072]{1,0:T(8,128)(2,1)}, bf16[192,3072]{1,0:T(8,128)(2,1)S(1)}, u32[]{:S(2)}, u32[]{:S(2)}) collective-permute-start(bf16[192,3072]{1,0:T(8,128)(2,1)} %collective-permute-done.refs_1_), channel_id=1, source_target_pairs={{1,3},{3,1},{4,6},{6,4},{9,11},{11,9},{12,14},{14,12},{17,19},{19,... | collective-permute-start | bytes 3538952 | tf_op jit(solution)/shard_map/ppermute | solution.py:272
  81.4 21.1 %collective-permute-start.13 = (bf16[192,3072]{1,0:T(8,128)(2,1)}, bf16[192,3072]{1,0:T(8,128)(2,1)}, u32[]{:S(2)}, u32[]{:S(2)}) collective-permute-start(bf16[192,3072]{1,0:T(8,128)(2,1)} %collective-permute-done.11.refs_0_), channel_id=1, source_target_pairs={{4,0},{6,2},{9,13},{11,15},{20,16},{22,18},{25,29},{27,31}} | collective-permute-start | bytes 3538952 | tf_op jit(solution)/shard_map/ppermute | solution.py:272
  83.7 25.2 %collective-permute-start.15 = (bf16[192,3072]{1,0:T(8,128)(2,1)}, bf16[192,3072]{1,0:T(8,128)(2,1)S(1)}, u32[]{:S(2)}, u32[]{:S(2)}) collective-permute-start(bf16[192,3072]{1,0:T(8,128)(2,1)} %collective-permute-done.11.refs_0_), channel_id=1, source_target_pairs={{4,6},{6,4},{9,11},{11,9},{20,22},{22,20},{25,27},{27,25}} | collective-permute-start | bytes 3538952 | tf_op jit(solution)/shard_map/ppermute | solution.py:272
  87.1 24.5 %collective-permute-start.32 = (bf16[768,768]{1,0:T(8,128)(2,1)S(1)}, bf16[768,768]{1,0:T(8,128)(2,1)}, u32[]{:S(2)}, u32[]{:S(2)}) collective-permute-start(bf16[768,768]{1,0:T(8,128)(2,1)S(1)} %collective-permute-done.30.s1), channel_id=1, source_target_pairs={{4,8},{6,10},{9,5},{11,7},{20,24},{22,26},{25,21},{27,23}} | collective-permute-start | bytes 3538952 | tf_op jit(solution)/shard_map/ppermute | solution.py:272
  93.1 20.2 %collective-permute-start.14 = (bf16[192,3072]{1,0:T(8,128)(2,1)}, bf16[192,3072]{1,0:T(8,128)(2,1)}, u32[]{:S(2)}, u32[]{:S(2)}) collective-permute-start(bf16[192,3072]{1,0:T(8,128)(2,1)} %collective-permute-done.12.refs_1_), channel_id=1, source_target_pairs={{5,1},{7,3},{8,12},{10,14},{21,17},{23,19},{24,28},{26,30}} | collective-permute-start | bytes 3538952 | tf_op jit(solution)/shard_map/ppermute | solution.py:272
  97.3 17.7 %collective-permute-start.5 = (bf16[3,3,384,128]{3,2,1,0:T(8,128)(2,1)S(1)}, bf16[3,3,384,128]{3,2,1,0:T(8,128)(2,1)S(1)}, u32[]{:S(2)}, u32[]{:S(2)}) collective-permute-start(bf16[3,3,384,128]{3,2,1,0:T(8,128)(2,1)S(1)} %collective-permute-done.3.refs_5_.refs_9_), channel_id=1, source_target_pairs={{0,1},{1,0},{2,3},{3,2},{4,5},{5,4},{6,7},{7,6},{8,9},{9,8},{10,11... | collective-permute-start | bytes 2654216 | tf_op jit(solution)/shard_map/ppermute | solution.py:272
  102.5 15.8 %collective-permute-start.10 = (bf16[3,3,384,128]{3,2,1,0:T(8,128)(2,1)S(1)}, bf16[3,3,384,128]{3,2,1,0:T(8,128)(2,1)S(1)}, u32[]{:S(2)}, u32[]{:S(2)}) collective-permute-start(bf16[3,3,384,128]{3,2,1,0:T(8,128)(2,1)S(1)} %collective-permute-done.8.refs_11_.refs_15_), channel_id=1, source_target_pairs={{1,0},{3,2},{5,4},{7,6},{8,9},{10,11},{12,13},{14,15},{17,16},{19,... | collective-permute-start | bytes 2654216 | tf_op jit(solution)/shard_map/ppermute | solution.py:272
  110.0 27.5 %collective-permute-start.16 = (bf16[192,3072]{1,0:T(8,128)(2,1)}, bf16[192,3072]{1,0:T(8,128)(2,1)}, u32[]{:S(2)}, u32[]{:S(2)}) collective-permute-start(bf16[192,3072]{1,0:T(8,128)(2,1)} %collective-permute-done.12.refs_1_), channel_id=1, source_target_pairs={{5,7},{7,5},{8,10},{10,8},{21,23},{23,21},{24,26},{26,24}} | collective-permute-start | bytes 3538952 | tf_op jit(solution)/shard_map/ppermute | solution.py:272
  111.6 25.9 %collective-permute-start.17 = (bf16[192,3072]{1,0:T(8,128)(2,1)}, bf16[192,3072]{1,0:T(8,128)(2,1)}, u32[]{:S(2)}, u32[]{:S(2)}) collective-permute-start(bf16[192,3072]{1,0:T(8,128)(2,1)} %collective-permute-done.13.refs_2_), channel_id=1, source_target_pairs={{0,2},{2,0},{13,15},{15,13},{16,18},{18,16},{29,31},{31,29}} | collective-permute-start | bytes 3538952 | tf_op jit(solution)/shard_map/ppermute | solution.py:272
  113.3 24.2 %collective-permute-start.18 = (bf16[192,3072]{1,0:T(8,128)(2,1)}, bf16[192,3072]{1,0:T(8,128)(2,1)}, u32[]{:S(2)}, u32[]{:S(2)}) collective-permute-start(bf16[192,3072]{1,0:T(8,128)(2,1)} %collective-permute-done.14.refs_3_), channel_id=1, source_target_pairs={{1,3},{3,1},{12,14},{14,12},{17,19},{19,17},{28,30},{30,28}} | collective-permute-start | bytes 3538952 | tf_op jit(solution)/shard_map/ppermute | solution.py:272
  115.9 35.8 %collective-permute-start.34 = (bf16[768,768]{1,0:T(8,128)(2,1)}, bf16[768,768]{1,0:T(8,128)(2,1)}, u32[]{:S(2)}, u32[]{:S(2)}) collective-permute-start(bf16[768,768]{1,0:T(8,128)(2,1)} %collective-permute-done.33), channel_id=1, source_target_pairs={{4,0},{6,2},{9,13},{11,15},{20,16},{22,18},{25,29},{27,31}} | collective-permute-start | bytes 3538952 | tf_op jit(solution)/shard_map/ppermute | solution.py:272
  119.2 32.6 %collective-permute-start.35 = (bf16[768,768]{1,0:T(8,128)(2,1)}, bf16[768,768]{1,0:T(8,128)(2,1)}, u32[]{:S(2)}, u32[]{:S(2)}) collective-permute-start(bf16[768,768]{1,0:T(8,128)(2,1)} %collective-permute-done.32), channel_id=1, source_target_pairs={{5,1},{7,3},{8,12},{10,14},{21,17},{23,19},{24,28},{26,30}} | collective-permute-start | bytes 3538952 | tf_op jit(solution)/shard_map/ppermute | solution.py:272
  125.6 12.0 %copy-start.32 = (s32[512]{0:T(512)}, s32[512]{0:T(512)S(1)}, u32[]{:S(2)}) copy-start(s32[512]{0:T(512)S(1)} %pad_add_fusion.1) | copy-start | bytes 6148
  129.6 11.4 %copy-start.14 = (bf16[3,3,384,128]{3,2,1,0:T(8,128)(2,1)S(1)}, bf16[3,3,384,128]{3,2,1,0:T(8,128)(2,1)}, u32[]{:S(2)}) copy-start(bf16[3,3,384,128]{3,2,1,0:T(8,128)(2,1)} %copy-done.12) | copy-start | bytes 2654212
  129.6 11.4 %copy-start.17 = (bf16[3,3,384,128]{3,2,1,0:T(8,128)(2,1)S(1)}, bf16[3,3,384,128]{3,2,1,0:T(8,128)(2,1)}, u32[]{:S(2)}) copy-start(bf16[3,3,384,128]{3,2,1,0:T(8,128)(2,1)} %copy-done.15) | copy-start | bytes 2654212
  129.6 11.4 %copy-start.19 = (bf16[192,3072]{1,0:T(8,128)(2,1)S(1)}, bf16[192,3072]{1,0:T(8,128)(2,1)}, u32[]{:S(2)}) copy-start(bf16[192,3072]{1,0:T(8,128)(2,1)} %copy-done.18) | copy-start | bytes 3538948
  129.6 11.4 %copy-start.27 = (s32[8]{0:T(128)S(1)}, s32[8]{0:T(128)}, u32[]{:S(2)}) copy-start(s32[8]{0:T(128)} %stack.151.sc_ref) | copy-start | bytes 100
  137.5 12.4 %collective-permute-start.23 = (s32[1,512]{1,0:T(1,128)S(1)}, s32[1,512]{1,0:T(1,128)S(1)}, u32[]{:S(2)}, u32[]{:S(2)}) collective-permute-start(s32[1,512]{1,0:T(1,128)S(1)} %bitcast.46), channel_id=1, source_target_pairs={{0,12},{1,13},{2,14},{3,15},{4,8},{5,9},{6,10},{7,11},{8,4},{9,5},... | collective-permute-start | bytes 6152 | tf_op jit(solution)/shard_map/ppermute | solution.py:272
  137.5 16.7 %collective-permute-start.22 = (s32[1,512]{1,0:T(1,128)S(1)}, s32[1,512]{1,0:T(1,128)S(1)}, u32[]{:S(2)}, u32[]{:S(2)}) collective-permute-start(s32[1,512]{1,0:T(1,128)S(1)} %bitcast.47), channel_id=1, source_target_pairs={{0,8},{1,9},{2,10},{3,11},{4,12},{5,13},{6,14},{7,15},{8,0},{9,1},... | collective-permute-start | bytes 6152 | tf_op jit(solution)/shard_map/ppermute | solution.py:272
  137.6 18.6 %collective-permute-start.21 = (s32[1,512]{1,0:T(1,128)S(1)}, s32[1,512]{1,0:T(1,128)S(1)}, u32[]{:S(2)}, u32[]{:S(2)}) collective-permute-start(s32[1,512]{1,0:T(1,128)S(1)} %bitcast.48), channel_id=1, source_target_pairs={{0,4},{1,5},{2,6},{3,7},{4,0},{5,1},{6,2},{7,3},{8,12},{9,13},{10,... | collective-permute-start | bytes 6152 | tf_op jit(solution)/shard_map/ppermute | solution.py:272
  149.9 23.4 %collective-permute-start.29 = (bf16[768,768]{1,0:T(8,128)(2,1)}, bf16[768,768]{1,0:T(8,128)(2,1)S(1)}, u32[]{:S(2)}, u32[]{:S(2)}) collective-permute-start(bf16[768,768]{1,0:T(8,128)(2,1)} %bitcast.32.wo), channel_id=1, source_target_pairs={{1,0},{3,2},{4,5},{6,7},{9,8},{11,10},{12,13},{14,15},{17,16},{19,... | collective-permute-start | bytes 3538952 | tf_op jit(solution)/shard_map/ppermute | solution.py:272
  151.8 7.9 %collective-permute-start.19 = (bf16[384,768]{1,0:T(8,128)(2,1)}, bf16[384,768]{1,0:T(8,128)(2,1)}, u32[]{:S(2)}, u32[]{:S(2)}) collective-permute-start(bf16[384,768]{1,0:T(8,128)(2,1)} %get-tuple-element.10.kvs0), channel_id=1, source_target_pairs={{0,1},{1,0},{2,3},{3,2},{4,5},{5,4},{6,7},{7,6},{8,9},{9,8},{10,11... | collective-permute-start | bytes 1769480 | tf_op jit(solution)/shard_map/ppermute | solution.py:272
  151.9 7.1 %copy-start.33 = (s32[512]{0:T(512)S(1)}, s32[512]{0:T(512)}, u32[]{:S(2)}) copy-start(s32[512]{0:T(512)} %copy-done.32) | copy-start | bytes 6148
  151.9 7.8 %collective-permute-start.20 = (bf16[384,768]{1,0:T(8,128)(2,1)}, bf16[384,768]{1,0:T(8,128)(2,1)}, u32[]{:S(2)}, u32[]{:S(2)}) collective-permute-start(bf16[384,768]{1,0:T(8,128)(2,1)} %get-tuple-element.11.kvs1), channel_id=1, source_target_pairs={{0,1},{1,0},{2,3},{3,2},{4,5},{5,4},{6,7},{7,6},{8,9},{9,8},{10,11... | collective-permute-start | bytes 1769480 | tf_op jit(solution)/shard_map/ppermute | solution.py:272
  154.2 32.2 %collective-permute-start.31 = (bf16[768,768]{1,0:T(8,128)(2,1)S(1)}, bf16[768,768]{1,0:T(8,128)(2,1)}, u32[]{:S(2)}, u32[]{:S(2)}) collective-permute-start(bf16[768,768]{1,0:T(8,128)(2,1)S(1)} %copy-done.3), channel_id=1, source_target_pairs={{1,17},{3,19},{4,20},{6,22},{9,25},{11,27},{12,28},{14,30},{17,1},... | collective-permute-start | bytes 3538952 | tf_op jit(solution)/shard_map/ppermute | solution.py:272
  156.8 40.6 %collective-permute-start.36 = (bf16[768,768]{1,0:T(8,128)(2,1)S(1)}, bf16[768,768]{1,0:T(8,128)(2,1)}, u32[]{:S(2)}, u32[]{:S(2)}) collective-permute-start(bf16[768,768]{1,0:T(8,128)(2,1)S(1)} %select_select_fusion.g_z), channel_id=1, source_target_pairs={{0,16},{1,17},{2,18},{3,19},{4,20},{5,21},{6,22},{7,23},{8,24},{9,... | collective-permute-start | bytes 3538952 | tf_op jit(solution)/shard_map/ppermute | solution.py:272
  160.7 7.6 %copy-start.31 = (bf16[384,384]{1,0:T(8,128)(2,1)S(1)}, bf16[384,384]{1,0:T(8,128)(2,1)}, u32[]{:S(2)}) copy-start(bf16[384,384]{1,0:T(8,128)(2,1)} %copy-done.30) | copy-start | bytes 884740
  166.3 8.3 %collective-permute-start.25 = (bf16[384,384]{1,0:T(8,128)(2,1)}, bf16[384,384]{1,0:T(8,128)(2,1)}, u32[]{:S(2)}, u32[]{:S(2)}) collective-permute-start(bf16[384,384]{1,0:T(8,128)(2,1)} %attend.2.an), channel_id=1, source_target_pairs={{1,5},{3,7},{4,0},{6,2},{9,13},{11,15},{12,8},{14,10},{17,21},{19,... | collective-permute-start | bytes 884744 | tf_op jit(solution)/shard_map/ppermute | solution.py:272
  173.2 13.2 %collective-permute-start.27 = (bf16[384,384]{1,0:T(8,128)(2,1)S(1)}, bf16[384,384]{1,0:T(8,128)(2,1)}, u32[]{:S(2)}, u32[]{:S(2)}) collective-permute-start(bf16[384,384]{1,0:T(8,128)(2,1)S(1)} %attend.3), channel_id=1, source_target_pairs={{0,8},{1,12},{2,10},{3,14},{4,9},{5,13},{6,11},{7,15},{8,0},{9,4},... | collective-permute-start | bytes 884744 | tf_op jit(solution)/shard_map/ppermute | solution.py:272
  173.3 24.1 %collective-permute-start.24 = (bf16[384,384]{1,0:T(8,128)(2,1)}, bf16[384,384]{1,0:T(8,128)(2,1)}, u32[]{:S(2)}, u32[]{:S(2)}) collective-permute-start(bf16[384,384]{1,0:T(8,128)(2,1)} %attend.2.an), channel_id=1, source_target_pairs={{0,1},{2,3},{5,4},{7,6},{8,9},{10,11},{13,12},{15,14},{16,17},{18,... | collective-permute-start | bytes 884744 | tf_op jit(solution)/shard_map/ppermute | solution.py:272
  174.6 22.8 %collective-permute-start.26 = (bf16[384,384]{1,0:T(8,128)(2,1)}, bf16[384,384]{1,0:T(8,128)(2,1)}, u32[]{:S(2)}, u32[]{:S(2)}) collective-permute-start(bf16[384,384]{1,0:T(8,128)(2,1)} %collective-permute-done.25.ap), channel_id=1, source_target_pairs={{0,1},{2,3},{5,4},{7,6},{8,9},{10,11},{13,12},{15,14},{16,17},{18,... | collective-permute-start | bytes 884744 | tf_op jit(solution)/shard_map/ppermute | solution.py:272
  186.4 11.0 %collective-permute-start.28 = (bf16[384,384]{1,0:T(8,128)(2,1)}, bf16[384,384]{1,0:T(8,128)(2,1)}, u32[]{:S(2)}, u32[]{:S(2)}) collective-permute-start(bf16[384,384]{1,0:T(8,128)(2,1)} %collective-permute-done.27.f0), channel_id=1, source_target_pairs={{0,1},{1,0},{2,3},{3,2},{4,5},{5,4},{6,7},{7,6},{8,9},{9,8},{10,11... | collective-permute-start | bytes 884744 | tf_op jit(solution)/shard_map/ppermute | solution.py:272
  202.2 10.2 %collective-permute-start.37 = (bf16[384,768]{1,0:T(8,128)(2,1)}, bf16[384,768]{1,0:T(8,128)(2,1)}, u32[]{:S(2)}, u32[]{:S(2)}) collective-permute-start(bf16[384,768]{1,0:T(8,128)(2,1)} %project.3), channel_id=1, source_target_pairs={{0,2},{1,3},{2,0},{3,1},{4,6},{5,7},{6,4},{7,5},{8,10},{9,11},{10,... | collective-permute-start | bytes 1769480 | tf_op jit(solution)/shard_map/ppermute | solution.py:272
  (29 other events, 44.4 us)
where the time goes:
time: 216 us; the launch traced here: 215 us
  starting transfers between devices  85.1 us (39%)
  waiting for transfers between devices  62.2 us (29%)
  Pallas kernels  38.9 us (18%)
  local copies, waits for them, and re-layouts  22.9 us (11%)
  other arithmetic  4.95 us (2%)
    ppermute x38, starting transfers between devices, move(): return lax.ppermute(array, AXES, pairs)  85.1 us
    ppermute x38, waiting for transfers between devices, move(): return lax.ppermute(array, AXES, pairs)  62.2 us
    unnamed x78, local copies, waits for them, and re-layouts  16.5 us
    pallas_call x2, Pallas kernels, qkv_tile(): pl.pallas_call(functools.partial(qkv_kernel, len(mine)), out_shape=(jax.S...  16 us
    pallas_call x2, Pallas kernels, attend(): pl.pallas_call(attend_kernel, out_shape=jax.ShapeDtypeStruct((rows, width...  10.5 us
    pallas_call x2, Pallas kernels, project(): pl.pallas_call(project_kernel, out_shape=jax.ShapeDtypeStruct((rows, widt...  8.56 us
  transfers between devices with their start and end apart: 38, of which 9 were waited for; matrix products, arithmetic and copies ran while one was open for 3% of the time, Pallas kernels for 16%

commit v1 on v0

--- a/solution.py
+++ b/solution.py
@@ -42,7 +42,6 @@
             ],
             out_specs=pl.BlockSpec((block, width), lambda i, half_ref: (i, 0)),
         ),
-        compiler_params=pltpu.CompilerParams(vmem_limit_bytes=12 << 20),
         cost_estimate=pl.CostEstimate(flops=rows * width * 5, bytes_accessed=rows * width * 2, transcendentals=rows),
         name="norm_rows",
     )(half[None], latents, mod_shift[None], mod_scale[None])
@@ -53,183 +52,238 @@
     return (raw * lax.rsqrt(square + EPS) * gain).astype(BF16)
 
 
-def qkv_kernel(count, sc_ref, *refs):
-    mine, others = refs[:count], refs[count : 2 * count]
-    za, ya, ca1, ca2, own_w, own_c, zb, yb, cb1, cb2, gq_ref, gk_ref = refs[2 * count : 2 * count + 12]
-    q_ref, kv_ref, tok_ref, acc_ref = refs[2 * count + 12 :]
-    half_rows = mine[0].shape[0]
+def qkv_kernel(counts, sc_ref, *refs):
+    tiles = []
+    for count in counts:
+        tiles.append((refs[:count], refs[count : 2 * count]))
+        refs = refs[2 * count :]
+    za, ya, ca1, ca2, own_w, own_c, zb, yb, cb1, cb2, gq_ref, gk_ref = refs[:12]
+    q_ref, kv_ref, tok_ref, w_ref, acc_ref, gain_ref, tok_sem, w_sem, gain_sem = refs[12:]
+    half_rows = tiles[0][0][0].shape[0]
     _, heads, depth, hd = za.shape
-    col = sc_ref[5]
-    for i in range(count):
-
-        @pl.when(sc_ref[7] == i)
+    col, rep, at_home = sc_ref[5], sc_ref[4], sc_ref[6] == 1
+    bases = [pl.multiple_of(sc_ref[i] * (2 * depth), 128) for i in range(4)]
+
+    def tok_copy(ref, block, tile, i):
+        start = pl.multiple_of((col if i == 0 else 1 - col) * half_rows, 64)
+        cols = pl.ds(bases[block], 2 * depth)
+        dst = tok_ref.at[tile, pl.ds(start, half_rows), cols]
+        return pltpu.make_async_copy(ref.at[:, cols], dst, tok_sem.at[block, tile, i])
+
+    def w_copy(ref, block, i):
+        if i is None:
+            start, size, sem = bases[block], 2 * depth, w_sem.at[2 * block]
+        else:
+            start, size, sem = bases[block] + (rep if i == 0 else 1 - rep) * depth, depth, w_sem.at[2 * block + i]
+        return pltpu.make_async_copy(ref, w_ref.at[:, :, pl.ds(pl.multiple_of(start, 128), size), :], sem)
+
+    def when_home(home, away):
+        @pl.when(at_home)
         def _():
-            tok_ref[pl.ds(pl.multiple_of(col * half_rows, 64), half_rows), :] = mine[i][...]
-            tok_ref[pl.ds(pl.multiple_of((1 - col) * half_rows, 64), half_rows), :] = others[i][...]
-
-    def lanes_of(ref, rows):
-        return jnp.concatenate([ref[s, h, rows, :] for s in range(3) for h in range(heads)], axis=1)
-
-    def add(block, halves, fresh=False):
-        base = sc_ref[block] * (2 * depth)
-        if len(halves) == 2:
-            cols = [
-                tok_ref[:, pl.ds(pl.multiple_of(base + h * depth, 128), depth)] for h in (sc_ref[4], 1 - sc_ref[4])
-            ]
-            toks = jnp.concatenate(cols, axis=1)
-            w = jnp.concatenate([lanes_of(r, slice(None)) for r in halves], axis=0)
-        else:
-            toks = tok_ref[:, pl.ds(pl.multiple_of(base, 128), 2 * depth)]
-            w = lanes_of(halves[0], slice(None))
-        term = jnp.dot(toks, w, preferred_element_type=F32)
-        acc_ref[...] = term if fresh else acc_ref[...] + term
-
-    add(0, (za, ya), fresh=True)
-    add(1, (ca1, ca2))
-
-    @pl.when(sc_ref[6] == 1)
-    def _():
-        add(2, (own_w,))
-        add(3, (cb1, cb2))
-
-    @pl.when(sc_ref[6] == 0)
-    def _():
-        add(2, (own_c,))
-        add(3, (zb, yb))
-
-    for h in range(heads):
-        lanes = slice(h * hd, (h + 1) * hd)
-        q_ref[:, lanes] = head_norm(acc_ref[:, lanes], gq_ref[...])
-        kv_ref[:, lanes] = head_norm(acc_ref[:, (heads + h) * hd : (heads + h + 1) * hd], gk_ref[...])
-    kv_ref[:, heads * hd :] = acc_ref[:, 2 * heads * hd :].astype(BF16)
-
-
-def qkv_tile(scalars, mine, others, weights, query_gain, key_gain):
-    half_rows, width = mine[0].shape
+            for copy in home:
+                copy.start()
+
+        @pl.when(jnp.logical_not(at_home))
+        def _():
+            for copy in away:
+                copy.start()
+
+        return home
+
+    def fetch_weights(block):
+        if block == 2:
+            return when_home([w_copy(own_w, 2, None)], [w_copy(own_c, 2, None)])
+        if block == 3:
+            return when_home([w_copy(cb1, 3, 0), w_copy(cb2, 3, 1)], [w_copy(zb, 3, 0), w_copy(yb, 3, 1)])
+        pair = (za, ya) if block == 0 else (ca1, ca2)
+        copies = [w_copy(pair[0], block, 0), w_copy(pair[1], block, 1)]
+        for copy in copies:
+            copy.start()
+        return copies
+
+    def fetch(block):
+        for tile, (mine, others) in enumerate(tiles):
+            for i in range(counts[tile]):
+
+                @pl.when(sc_ref[7 + tile] == i)
+                def _():
+                    tok_copy(mine[i], block, tile, 0).start()
+                    tok_copy(others[i], block, tile, 1).start()
+
+        waits = fetch_weights(block)
+        return waits + [tok_copy(pairs[0], block, tile, i) for tile, t in enumerate(tiles) for i, pairs in enumerate(t)]
+
+    gains = [pltpu.make_async_copy(r, gain_ref.at[i], gain_sem.at[i]) for i, r in enumerate((gq_ref, gk_ref))]
+    waits = {0: fetch(0), 1: fetch(1)}
+    for copy in gains:
+        copy.start()
+    for block in range(4):
+        for copy in waits[block]:
+            copy.wait()
+        if block + 2 < 4:
+            waits[block + 2] = fetch(block + 2)
+        part = pl.ds(bases[block], 2 * depth)
+        w = jnp.concatenate([w_ref[s, h, part, :] for s in range(3) for h in range(heads)], axis=1)
+        for tile in range(2):
+            term = jnp.dot(tok_ref[tile, :, part], w, preferred_element_type=F32)
+            acc_ref[tile] = term if block == 0 else acc_ref[tile] + term
+
+    for copy in gains:
+        copy.wait()
+    for tile in range(2):
+        for h in range(heads):
+            lanes = slice(h * hd, (h + 1) * hd)
+            q_ref[tile, :, lanes] = head_norm(acc_ref[tile, :, lanes], gain_ref[0])
+            kv_ref[tile, :, lanes] = head_norm(acc_ref[tile, :, (heads + h) * hd : (heads + h + 1) * hd], gain_ref[1])
+        kv_ref[tile, :, heads * hd :] = acc_ref[tile, :, 2 * heads * hd :].astype(BF16)
+
+
+def qkv_tiles(scalars, candidates, weights, query_gain, key_gain):
+    half_rows, width = candidates[0][0][0].shape
     _, heads, _, hd = weights[0].shape
     rows, out = 2 * half_rows, heads * hd
+    counts = tuple(len(mine) for mine, _ in candidates)
+    tokens = [t for mine, others in candidates for t in (*mine, *others)]
     smem = pl.BlockSpec(memory_space=pltpu.SMEM)
     vmem = pl.BlockSpec(memory_space=pltpu.VMEM)
+    anywhere = pl.BlockSpec(memory_space=pl.ANY)
     return pl.pallas_call(
-        functools.partial(qkv_kernel, len(mine)),
+        functools.partial(qkv_kernel, counts),
         out_shape=(
-            jax.ShapeDtypeStruct((rows, out), BF16),
-            jax.ShapeDtypeStruct((rows, 2 * out), BF16),
+            jax.ShapeDtypeStruct((2, rows, out), BF16),
+            jax.ShapeDtypeStruct((2, rows, 2 * out), BF16),
         ),
-        in_specs=[smem] + [vmem] * (2 * len(mine) + len(weights) + 2),
+        in_specs=[smem] + [anywhere] * (len(tokens) + len(weights) + 2),
         out_specs=(vmem, vmem),
-        scratch_shapes=[pltpu.VMEM((rows, width), BF16), pltpu.VMEM((rows, 3 * out), F32)],
-        compiler_params=pltpu.CompilerParams(vmem_limit_bytes=32 << 20),
+        scratch_shapes=[
+            pltpu.VMEM((2, rows, width), BF16),
+            pltpu.VMEM((3, heads, width, hd), BF16),
+            pltpu.VMEM((2, rows, 3 * out), F32),
+            pltpu.VMEM((2, 1, hd), F32),
+            pltpu.SemaphoreType.DMA((4, 2, 2)),
+            pltpu.SemaphoreType.DMA((8,)),
+            pltpu.SemaphoreType.DMA((2,)),
+        ],
         cost_estimate=pl.CostEstimate(
-            flops=6 * rows * width * out, bytes_accessed=width * 3 * out * 2, transcendentals=0
+            flops=12 * rows * width * out, bytes_accessed=width * 3 * out * 2, transcendentals=0
         ),
-        name="qkv_tile",
-    )(scalars, *mine, *others, *weights, query_gain[None], key_gain[None])
-
-
-def attend_kernel(sc_ref, q_ref, kvs0, kvs1, kvs2, kvs3, flags_ref, out_ref):
-    kv_refs = (kvs0, kvs1, kvs2, kvs3)
-    rows, width = q_ref.shape
+        name="qkv_tiles",
+    )(scalars, *tokens, *weights, query_gain[None], key_gain[None])
+
+
+def attend_kernel(sc_ref, q_ref, kv0, kv1, flags_ref, near_ref, far_ref):
+    _, rows, width = q_ref.shape
     hd = 128
     heads = width // hd
     factor = math.log2(math.e) / math.sqrt(hd)
     flags = flags_ref[...]
     place = lax.broadcasted_iota(jnp.int32, flags.shape, 0)
+    segments = ((kv0, 0), (kv0, 1), (kv1, 0), (kv1, 1))
 
     def row(d):
         return jnp.sum(jnp.where(place == d, flags, 0), axis=0, keepdims=True)
 
-    hits = row(sc_ref[8])[:, rows:]
-    lane = lax.broadcasted_iota(jnp.int32, hits.shape, 1)
+    rows_of = [row(sc_ref[4 + s]) for s in range(4)]
     biases = []
-    for s in range(4):
-        hit = jnp.sum(jnp.where(lane == sc_ref[s], hits, 0), axis=1, keepdims=True)
-        valid = row(sc_ref[4 + s])[:, :rows]
-        biases.append(jnp.where(valid * hit > 0, 0.0, NEG).astype(F32))
-    bias = jnp.concatenate(biases, axis=1)
-    for h in range(heads):
-        lanes = slice(h * hd, (h + 1) * hd)
-        keys = jnp.concatenate([r[:, lanes] for r in kv_refs], axis=0)
-        vals = jnp.concatenate([r[:, width + h * hd : width + (h + 1) * hd] for r in kv_refs], axis=0)
-        scores = lax.dot_general(
-            q_ref[:, lanes], keys, (((1,), (1,)), ((), ())), preferred_element_type=F32
-        )
-        scores = scores * factor + bias
-        weights = jnp.exp2(scores - jnp.max(scores, axis=1, keepdims=True))
-        total = jnp.sum(weights, axis=1, keepdims=True)
-        added = jnp.dot(weights.astype(BF16), vals, preferred_element_type=F32)
-        out_ref[:, lanes] = (added / total).astype(BF16)
-
-
-def attend(scalars, queries, kvs, flags):
-    rows, width = queries.shape
+    for t in range(2):
+        hits = rows_of[t][:, rows:]
+        lane = lax.broadcasted_iota(jnp.int32, hits.shape, 1)
+        bias = []
+        for s in range(4):
+            hit = jnp.sum(jnp.where(lane == sc_ref[s], hits, 0), axis=1, keepdims=True)
+            bias.append(jnp.where(rows_of[s][:, :rows] * hit > 0, 0.0, NEG).astype(F32))
+        biases.append(jnp.concatenate(bias, axis=1))
+    for t, out_ref in ((1, far_ref), (0, near_ref)):
+        for h in range(heads):
+            lanes = slice(h * hd, (h + 1) * hd)
+            keys = jnp.concatenate([r[s, :, lanes] for r, s in segments], axis=0)
+            vals = jnp.concatenate([r[s, :, width + h * hd : width + (h + 1) * hd] for r, s in segments], axis=0)
+            scores = lax.dot_general(
+                q_ref[t, :, lanes], keys, (((1,), (1,)), ((), ())), preferred_element_type=F32
+            )
+            scores = scores * factor + biases[t]
+            weights = jnp.exp2(scores - jnp.max(scores, axis=1, keepdims=True))
+            total = jnp.sum(weights, axis=1, keepdims=True)
+            added = jnp.dot(weights.astype(BF16), vals, preferred_element_type=F32)
+            out_ref[:, lanes] = (added / total).astype(BF16)
+
+
+def attend(scalars, queries, kv, kv_other, flags):
+    _, rows, width = queries.shape
     smem = pl.BlockSpec(memory_space=pltpu.SMEM)
     vmem = pl.BlockSpec(memory_space=pltpu.VMEM)
     keys = 4 * rows
+    shape = jax.ShapeDtypeStruct((rows, width), BF16)
     return pl.pallas_call(
         attend_kernel,
-        out_shape=jax.ShapeDtypeStruct((rows, width), BF16),
-        in_specs=[smem] + [vmem] * 6,
-        out_specs=vmem,
-        compiler_params=pltpu.CompilerParams(vmem_limit_bytes=32 << 20),
+        out_shape=(shape, shape),
+        in_specs=[smem] + [vmem] * 4,
+        out_specs=(vmem, vmem),
+        compiler_params=pltpu.CompilerParams(vmem_limit_bytes=24 << 20),
         cost_estimate=pl.CostEstimate(
-            flops=4 * rows * keys * width, bytes_accessed=8 * rows * width * 2, transcendentals=rows * keys * width // 128
+            flops=8 * rows * keys * width, bytes_accessed=8 * rows * width * 2, transcendentals=2 * rows * keys * width // 128
         ),
         name="attend",
-    )(scalars, queries, *kvs, flags)
-
-
-def project_kernel(sc_ref, an, bn, ap, bp, f0, f1, wo, c_f, s1, y_f, g_z, y_g, out_ref, att_ref):
+    )(scalars, queries, kv, kv_other, flags)
+
+
+def project_kernel(sc_ref, an, bn, ap, bp, f0, f1, *refs):
+    firsts, seconds = refs[0:12:2], refs[1:12:2]
+    out_ref, att_ref, w_ref, att_sem, w_sem = refs[12:]
     _, width = an.shape
-    depth = wo.shape[0]
-
-    def put(place, piece_ref):
-        att_ref[:, pl.ds(pl.multiple_of(place * width, 128), width)] = piece_ref[...]
+    depth = w_ref.shape[1]
+
+    def piece_copy(ref, i):
+        lanes = pl.ds(pl.multiple_of(sc_ref[1 + i] * width, 128), width)
+        return pltpu.make_async_copy(ref, att_ref.at[:, lanes], att_sem.at[i])
 
     @pl.when(sc_ref[0] == 1)
     def _():
-        put(sc_ref[3], an)
-        put(sc_ref[4], ap)
+        piece_copy(an, 0).start()
+        piece_copy(ap, 1).start()
 
     @pl.when(sc_ref[0] == 0)
     def _():
-        put(sc_ref[3], bn)
-        put(sc_ref[4], bp)
-
-    put(sc_ref[5], f0)
-    put(sc_ref[6], f1)
-
-    def term(group, w_ref):
+        piece_copy(bn, 0).start()
+        piece_copy(bp, 1).start()
+
+    piece_copy(f0, 2).start()
+    piece_copy(f1, 3).start()
+    for i in range(6):
+
+        @pl.when(sc_ref[5] == i)
+        def _():
+            pltpu.make_async_copy(firsts[i], w_ref.at[0], w_sem.at[0]).start()
+            pltpu.make_async_copy(seconds[i], w_ref.at[1], w_sem.at[1]).start()
+
+    for i in range(4):
+        piece_copy(f0, i).wait()
+    terms = []
+    for i in range(2):
+        group = sc_ref[6] if i == 0 else 1 - sc_ref[6]
+        pltpu.make_async_copy(firsts[0], w_ref.at[i], w_sem.at[i]).wait()
         part = att_ref[:, pl.ds(pl.multiple_of(group * depth, 128), depth)]
-        return jnp.dot(part, w_ref[...], preferred_element_type=F32).astype(BF16).astype(F32)
-
-    def block(group, first, second):
-        out_ref[...] = (term(group, first) + term(1 - group, second)).astype(out_ref.dtype)
-
-    @pl.when((sc_ref[7] == 1) & (sc_ref[0] == 1))
-    def _():
-        block(sc_ref[1], wo, c_f)
-
-    @pl.when((sc_ref[7] == 1) & (sc_ref[0] == 0))
-    def _():
-        block(sc_ref[2], s1, y_f)
-
-    @pl.when(sc_ref[7] == 0)
-    def _():
-        block(sc_ref[2], g_z, y_g)
+        terms.append(jnp.dot(part, w_ref[i], preferred_element_type=F32).astype(BF16).astype(F32))
+    out_ref[...] = (terms[0] + terms[1]).astype(out_ref.dtype)
 
 
 def project(scalars, pieces, weights, dtype):
-    rows, _ = pieces[0].shape
+    rows = pieces[0].shape[0]
     depth, width = weights[0].shape
     smem = pl.BlockSpec(memory_space=pltpu.SMEM)
     vmem = pl.BlockSpec(memory_space=pltpu.VMEM)
+    anywhere = pl.BlockSpec(memory_space=pl.ANY)
     return pl.pallas_call(
         project_kernel,
         out_shape=jax.ShapeDtypeStruct((rows, width), dtype),
-        in_specs=[smem] + [vmem] * (len(pieces) + len(weights)),
+        in_specs=[smem] + [anywhere] * (len(pieces) + len(weights)),
         out_specs=vmem,
-        scratch_shapes=[pltpu.VMEM((rows, 2 * depth), BF16)],
+        scratch_shapes=[
+            pltpu.VMEM((rows, 2 * depth), BF16),
+            pltpu.VMEM((2, depth, width), BF16),
+            pltpu.SemaphoreType.DMA((4,)),
+            pltpu.SemaphoreType.DMA((2,)),
+        ],
         compiler_params=pltpu.CompilerParams(vmem_limit_bytes=16 << 20),
         cost_estimate=pl.CostEstimate(
             flops=4 * rows * depth * width, bytes_accessed=4 * depth * width * 2, transcendentals=0
@@ -377,40 +431,43 @@
     y_f = move(s1, to_replica(lambda zz, cc: not owns(zz, cc)))
     s3a = move(s2a, outward(mid_rest))
     s3b = move(s2b, outward(mid_own))
-    g_z = jnp.where(is_mid, jnp.where(own, s2b, s2a), jnp.where(own, s3a, s3b))
-    y_g = move(g_z, to_replica())
-
-    q_near, kv_near = qkv_tile(
-        scalars_of(*sources, jnp.where(own, 0, 1)), (n_mine, r1), (n_other, x_r1), weights, query_gain, key_gain
-    )
-    kv_near_o = move(kv_near, to_core())
-    q_far, kv_far = qkv_tile(
-        scalars_of(*sources, jnp.where(is_mid, jnp.where(own, 1, 0), jnp.where(own, 2, 3))),
-        (r2a, r2b, r3a, r3b),
-        (x_r2a, x_r2b, x_r3a, x_r3b),
+    y_2a = move(s2a, to_replica(mid_rest))
+    y_2b = move(s2b, to_replica(mid_own))
+    y_3a = move(s3a, to_replica(end_own))
+    y_3b = move(s3b, to_replica(end_rest))
+
+    picks = (jnp.where(own, 0, 1), jnp.where(is_mid, jnp.where(own, 1, 0), jnp.where(own, 2, 3)))
+    queries, kv = qkv_tiles(
+        scalars_of(*sources, *picks),
+        (((n_mine, r1), (n_other, x_r1)), ((r2a, r2b, r3a, r3b), (x_r2a, x_r2b, x_r3a, x_r3b))),
         weights,
         query_gain,
         key_gain,
     )
-    kv_far_o = move(kv_far, to_core())
+    kv_other = move(kv, to_core())
 
     segments = (near, far, near_o, far_o)
-    marks = (*segments, *(s ^ z for s in segments))
-    kvs = (kv_near, kv_far, kv_near_o, kv_far_o)
-    att_far = attend(scalars_of(*marks, far ^ z), q_far, kvs, flags)
+    att_near, att_far = attend(scalars_of(*segments, *(s ^ z for s in segments)), queries, kv, kv_other, flags)
     p_far = move(att_far, lambda yy, zz, xx, cc: (yy, 2 * (1 - zz // 2) + cc, xx, zz % 2))
-    att_near = attend(scalars_of(*marks, near ^ z), q_near, kvs, flags)
     p_near = move(att_near, outward(lambda zz, cc: not owns(zz, cc)))
     b_near = move(att_near, to_core(owns))
     p_far_o = move(p_far, to_core())
     b_pair = move(p_near, to_core(owns))
 
     pieces = (att_near, b_near, p_near, b_pair, p_far, p_far_o)
-    blocks = (wo, c_f, s1, y_f, g_z, y_g)
-    places = (own, c, y, z, z ^ 1, far, far_o)
-    send = project(scalars_of(*places, x != pair), pieces, blocks, BF16)
+    blocks = (wo, c_f, s1, y_f, s2a, y_2a, s2b, y_2b, s3a, y_3a, s3b, y_3b)
+    places = (own, z, z ^ 1, far, far_o)
+    from_near = (jnp.where(own, 0, 1), jnp.where(own, c, y))
+    from_far = (2 + jnp.where(is_mid, jnp.where(own, 1, 0), jnp.where(own, 2, 3)), y)
+    near_stays = x == pair
+
+    def project_block(near_block):
+        chosen = [jnp.where(near_block, n, f) for n, f in zip(from_near, from_far)]
+        return scalars_of(*places, *chosen)
+
+    send = project(project_block(jnp.logical_not(near_stays)), pieces, blocks, BF16)
     got = move(send, to_column())
-    keep = project(scalars_of(*places, x == pair), pieces, blocks, F32)
+    keep = project(project_block(near_stays), pieces, blocks, F32)
     projected = keep + got.astype(F32)
     out_width = projected.shape[1]
     offset = (x * nc + c) * out_width

time: 216 us -> 248 us (1.15)
  the two profiles are of different devices: /device:TPU:8 before, /device:TPU:14 now
where the time goes in v1:
time: 248 us; the launch traced here: 247 us
  waiting for transfers between devices  130 us (52%)
  starting transfers between devices  64.3 us (26%)
  Pallas kernels  34.8 us (14%)
  local copies, waits for them, and re-layouts  14 us (6%)
  other arithmetic  3.1 us (1%)
    ppermute x40, waiting for transfers between devices, move(): return lax.ppermute(array, AXES, pairs)  130 us
    ppermute x40, starting transfers between devices, move(): return lax.ppermute(array, AXES, pairs)  64.3 us
    pallas_call x1, Pallas kernels, qkv_tiles(): pl.pallas_call(functools.partial(qkv_kernel, counts), out_shape=(jax.Shap...  11.8 us
    pallas_call x2, Pallas kernels, norm_rows(): pl.pallas_call(norm_kernel, out_shape=jax.ShapeDtypeStruct((rows // 2, wi...  8.26 us
    unnamed x36, local copies, waits for them, and re-layouts  8.21 us
    pallas_call x2, Pallas kernels, project(): pl.pallas_call(project_kernel, out_shape=jax.ShapeDtypeStruct((rows, widt...  7.57 us
    pallas_call x1, Pallas kernels, attend(): pl.pallas_call(attend_kernel, out_shape=(shape, shape), in_specs=[smem] +...  7.13 us
  transfers between devices with their start and end apart: 40, of which 15 were waited for; matrix products, arithmetic and copies ran while one was open for 2% of the time, Pallas kernels for 12%

profile of v1, /device:TPU:14, one launch (start us, length us, event | category | flops | bytes accessed | tf_op | source)
XLA Modules:
  0.0 246.9 jit_solution(4573254730824558634)
XLA Ops:
  0.0 2.5 %dynamic-slice_bitcast_fusion.1 = (bf16[3,3,384,128]{3,2,1,0:T(8,128)(2,1)}, bf16[3,3,384,128]{3,2,1,0:T(8,128)(2,1)S(1)}) fusion(bf16[768,3,6,128]{3,0,2,1:T(8,128)(2,1)} %param.12, s32[]{:T(128)S(6)} %select_n.88, s32[]{:T(128)S(6)} %select_n.93, s32[]{:T(128)S(6)} %select_n.90), kind=kLoop, calls=%fused_computation.2 | loop fusion | bytes 3538956 | tf_op jit(solution)/shard_map/dynamic_slice | solution.py:385
  2.5 4.2 %norm_rows.2.refs_0_ = bf16[192,3072]{1,0:T(8,128)(2,1)} custom-call(s32[1]{0:T(128)} %bitcast.17.half_ref, bf16[384,3072]{1,0:T(8,128)(2,1)} %x_ref.3, f32[1,3072]{1,0:T(1,128)} %bitcast.44, f32[1,3072]{1,0:T(1,128)} %bitcast.46), custom_call_target="tpu_custom_call" | custom-call | flops 5898240 | bytes 2359296 | tf_op jit(solution)/shard_map/norm_rows/pallas_call | solution.py:32
  8.0 1.7 collective-permute-start.15
  11.0 1.3 collective-permute-start.29
  12.3 17.5 %collective-permute-done.10.refs_12_ = bf16[3,3,384,128]{3,2,1,0:T(8,128)(2,1)} collective-permute-done((bf16[3,3,384,128]{3,2,1,0:T(8,128)(2,1)S(1)}, bf16[3,3,384,128]{3,2,1,0:T(8,128)(2,1)}, u32[]{:S(2)}, u32[]{:S(2)}) %collective-permute-start.10) | collective-permute-done | bytes 884768 | tf_op jit(solution)/shard_map/ppermute | solution.py:326
  31.1 3.6 %collective-permute-start.11 = (bf16[3,3,384,128]{3,2,1,0:T(8,128)(2,1)}, bf16[3,3,384,128]{3,2,1,0:T(8,128)(2,1)S(1)}, u32[]{:S(2)}, u32[]{:S(2)}) collective-permute-start(bf16[3,3,384,128]{3,2,1,0:T(8,128)(2,1)} %collective-permute-done.10.refs_12_), channel_id=1, source_target_pairs={{0,16},{1,17},{2,18},{3,19},{4,20},{5,21},{6,22},{7,23},{8,24},{9,... | collective-permute-start | bytes 2654216 | tf_op jit(solution)/shard_map/ppermute | solution.py:326
  34.7 1.6 dynamic-slice_bitcast_fusion.refs_16_
  36.3 12.6 %collective-permute-done.refs_1_ = bf16[192,3072]{1,0:T(8,128)(2,1)} collective-permute-done((bf16[192,3072]{1,0:T(8,128)(2,1)}, bf16[192,3072]{1,0:T(8,128)(2,1)}, u32[]{:S(2)}, u32[]{:S(2)}) %collective-permute-start) | collective-permute-done | bytes 1179680 | tf_op jit(solution)/shard_map/ppermute | solution.py:326
  48.9 4.0 %collective-permute-start.14 = (bf16[3,3,768,128]{3,2,1,0:T(8,128)(2,1)S(1)}, bf16[3,3,768,128]{3,2,1,0:T(8,128)(2,1)}, u32[]{:S(2)}, u32[]{:S(2)}) collective-permute-start(bf16[3,3,768,128]{3,2,1,0:T(8,128)(2,1)S(1)} %dynamic-slice_bitcast_fusion.refs_16_), channel_id=1, source_target_pairs={{0,1},{2,3},{4,5},{6,7},{9,8},{11,10},{13,12},{15,14},{16,17},{18,... | collective-permute-start | bytes 5308424 | tf_op jit(solution)/shard_map/ppermute | solution.py:326
  52.8 20.3 %collective-permute-done.2.refs_4_ = bf16[192,3072]{1,0:T(8,128)(2,1)} collective-permute-done((bf16[192,3072]{1,0:T(8,128)(2,1)}, bf16[192,3072]{1,0:T(8,128)(2,1)}, u32[]{:S(2)}, u32[]{:S(2)}) %collective-permute-start.2) | collective-permute-done | bytes 1179680 | tf_op jit(solution)/shard_map/ppermute | solution.py:326
  73.1 2.5 %collective-permute-start.3 = (bf16[192,3072]{1,0:T(8,128)(2,1)}, bf16[192,3072]{1,0:T(8,128)(2,1)}, u32[]{:S(2)}, u32[]{:S(2)}) collective-permute-start(bf16[192,3072]{1,0:T(8,128)(2,1)} %collective-permute-done.refs_1_), channel_id=1, source_target_pairs={{4,8},{6,10},{9,5},{11,7},{20,24},{22,26},{25,21},{27,23}} | collective-permute-start | bytes 3538952 | tf_op jit(solution)/shard_map/ppermute | solution.py:326
  75.6 1.6 collective-permute-start.16
  77.2 1.3 collective-permute-start.17
  78.5 2.3 collective-permute-start.4
  80.8 2.4 collective-permute-start.1
  83.3 5.3 %collective-permute-done.3.refs_5_ = bf16[192,3072]{1,0:T(8,128)(2,1)} collective-permute-done((bf16[192,3072]{1,0:T(8,128)(2,1)}, bf16[192,3072]{1,0:T(8,128)(2,1)}, u32[]{:S(2)}, u32[]{:S(2)}) %collective-permute-start.3) | collective-permute-done | bytes 1179680 | tf_op jit(solution)/shard_map/ppermute | solution.py:326
  88.6 1.7 collective-permute-start.5
  90.3 2.4 collective-permute-start.6
  92.7 4.0 %collective-permute-start.33 = (bf16[768,768]{1,0:T(8,128)(2,1)S(1)}, bf16[768,768]{1,0:T(8,128)(2,1)S(1)}, u32[]{:S(2)}, u32[]{:S(2)}) collective-permute-start(bf16[768,768]{1,0:T(8,128)(2,1)S(1)} %collective-permute-done.29.refs_2_), channel_id=1, source_target_pairs={{4,8},{6,10},{9,5},{11,7},{20,24},{22,26},{25,21},{27,23}} | collective-permute-start | bytes 3538952 | tf_op jit(solution)/shard_map/ppermute | solution.py:326
  96.7 1.7 collective-permute-start.7
  99.2 1.7 collective-permute-start.8
  100.9 1.7 collective-permute-start.9
  102.6 21.8 %collective-permute-done.6.refs_8_ = bf16[192,3072]{1,0:T(8,128)(2,1)S(1)} collective-permute-done((bf16[192,3072]{1,0:T(8,128)(2,1)}, bf16[192,3072]{1,0:T(8,128)(2,1)S(1)}, u32[]{:S(2)}, u32[]{:S(2)}) %collective-permute-start.6) | collective-permute-done | bytes 1179680 | tf_op jit(solution)/shard_map/ppermute | solution.py:326
  124.4 1.3 collective-permute-start.18
  127.8 3.9 %collective-permute-start.28 = (bf16[768,768]{1,0:T(8,128)(2,1)S(1)}, bf16[768,768]{1,0:T(8,128)(2,1)}, u32[]{:S(2)}, u32[]{:S(2)}) collective-permute-start(bf16[768,768]{1,0:T(8,128)(2,1)S(1)} %bitcast.41), channel_id=1, source_target_pairs={{1,0},{3,2},{4,5},{6,7},{9,8},{11,10},{12,13},{14,15},{17,16},{19,... | collective-permute-start | bytes 3538952 | tf_op jit(solution)/shard_map/ppermute | solution.py:326
  132.4 4.1 %norm_rows.3.refs_2_ = bf16[192,3072]{1,0:T(8,128)(2,1)} custom-call(s32[1]{0:T(128)} %bitcast.23.half_ref, bf16[384,3072]{1,0:T(8,128)(2,1)} %x_ref.3, f32[1,3072]{1,0:T(1,128)} %bitcast.45, f32[1,3072]{1,0:T(1,128)} %bitcast.47), custom_call_target="tpu_custom_call" | custom-call | flops 5898240 | bytes 2359296 | tf_op jit(solution)/shard_map/norm_rows/pallas_call | solution.py:32
  136.5 2.3 collective-permute-start.35
  138.8 1.8 collective-permute-start.37
  140.6 11.8 %qkv_tiles.1 = (bf16[2,384,384]{2,1,0:T(8,128)(2,1)}, bf16[2,384,768]{2,1,0:T(8,128)(2,1)}) custom-call(s32[9]{0:T(128)} %stack.120.sc_ref, bf16[192,3072]{1,0:T(8,128)(2,1)} %norm_rows.2.refs_0_, bf16[192,3072]{1,0:T(8,128)(2,1)} %collective-permute-done.refs_1_, bf16[192,3072]{1,0:T(8,128)(2,1)} %norm_rows.3.refs_2_, bf16[192,3072]{1,0:T(8,128)(2,1)} %copy-done.9, ...), custom_call_target="tpu_custom_call" | custom-call | flops 5435817984 | bytes 7077888 | tf_op jit(solution)/shard_map/qkv_tiles/pallas_call | solution.py:150
  152.8 11.0 %collective-permute-done.20 = s32[1,512]{1,0:T(1,128)S(1)} collective-permute-done((s32[1,512]{1,0:T(1,128)S(1)}, s32[1,512]{1,0:T(1,128)S(1)}, u32[]{:S(2)}, u32[]{:S(2)}) %collective-permute-start.20) | collective-permute-done | bytes 2080 | tf_op jit(solution)/shard_map/ppermute | solution.py:326
  163.7 4.5 %collective-permute-done.21 = s32[1,512]{1,0:T(1,128)S(1)} collective-permute-done((s32[1,512]{1,0:T(1,128)S(1)}, s32[1,512]{1,0:T(1,128)S(1)}, u32[]{:S(2)}, u32[]{:S(2)}) %collective-permute-start.21) | collective-permute-done | bytes 2080 | tf_op jit(solution)/shard_map/ppermute | solution.py:326
  169.3 2.5 %collective-permute-done.22 = s32[1,512]{1,0:T(1,128)S(1)} collective-permute-done((s32[1,512]{1,0:T(1,128)S(1)}, s32[1,512]{1,0:T(1,128)S(1)}, u32[]{:S(2)}, u32[]{:S(2)}) %collective-permute-start.22) | collective-permute-done | bytes 2080 | tf_op jit(solution)/shard_map/ppermute | solution.py:326
  171.8 2.1 collective-permute-start.30
  173.9 3.8 %collective-permute-start.32 = (bf16[768,768]{1,0:T(8,128)(2,1)S(1)}, bf16[768,768]{1,0:T(8,128)(2,1)}, u32[]{:S(2)}, u32[]{:S(2)}) collective-permute-start(bf16[768,768]{1,0:T(8,128)(2,1)S(1)} %collective-permute-done.31.refs_4_), channel_id=1, source_target_pairs={{4,20},{6,22},{9,25},{11,27},{20,4},{22,6},{25,9},{27,11}} | collective-permute-start | bytes 3538952 | tf_op jit(solution)/shard_map/ppermute | solution.py:326
  177.7 1.7 collective-permute-start.34
  179.4 1.7 collective-permute-start.36
  182.2 1.7 collective-permute-start.38
  188.2 7.1 %attend.1 = (bf16[384,384]{1,0:T(8,128)(2,1)}, bf16[384,384]{1,0:T(8,128)(2,1)S(1)}) custom-call(s32[8]{0:T(128)S(1)} %stack.110.sc_ref, bf16[2,384,384]{2,1,0:T(8,128)(2,1)S(1)} %copy-done.7, bf16[2,384,768]{2,1,0:T(8,128)(2,1)S(1)} %copy-done.4, bf16[2,384,768]{2,1,0:T(8,128)(2,1)S(1)} %copy-done.6, s32[4,512]{1,0:T(4,128)S(1)} %pad_add_fusion.flags_ref), custom_call_target="tpu_custom_call" | custom-call | flops 1811939328 | bytes 2359296 | tf_op jit(solution)/shard_map/attend/pallas_call | solution.py:217
  195.3 7.2 %collective-permute-done.30.refs_3_ = bf16[768,768]{1,0:T(8,128)(2,1)} collective-permute-done((bf16[768,768]{1,0:T(8,128)(2,1)S(1)}, bf16[768,768]{1,0:T(8,128)(2,1)}, u32[]{:S(2)}, u32[]{:S(2)}) %collective-permute-start.30) | collective-permute-done | bytes 1179680 | tf_op jit(solution)/shard_map/ppermute | solution.py:326
  202.5 2.0 collective-permute-start.24
  204.5 10.8 %collective-permute-done.32.refs_5_ = bf16[768,768]{1,0:T(8,128)(2,1)} collective-permute-done((bf16[768,768]{1,0:T(8,128)(2,1)S(1)}, bf16[768,768]{1,0:T(8,128)(2,1)}, u32[]{:S(2)}, u32[]{:S(2)}) %collective-permute-start.32) | collective-permute-done | bytes 1179680 | tf_op jit(solution)/shard_map/ppermute | solution.py:326
  216.6 1.3 collective-permute-start.25
  217.9 3.6 %collective-permute-done.26.f0 = bf16[384,384]{1,0:T(8,128)(2,1)} collective-permute-done((bf16[384,384]{1,0:T(8,128)(2,1)S(1)}, bf16[384,384]{1,0:T(8,128)(2,1)}, u32[]{:S(2)}, u32[]{:S(2)}) %collective-permute-start.26) | collective-permute-done | bytes 294944 | tf_op jit(solution)/shard_map/ppermute | solution.py:326
  221.7 1.8 collective-permute-done.27.f1
  224.7 4.2 %project.3 = bf16[384,768]{1,0:T(8,128)(2,1)} custom-call(s32[7]{0:T(128)S(1)} %stack.123.sc_ref, bf16[384,384]{1,0:T(8,128)(2,1)} %get-tuple-element.11.an, bf16[384,384]{1,0:T(8,128)(2,1)} %collective-permute-done.23.bn, bf16[384,384]{1,0:T(8,128)(2,1)} %collective-permute-done.24.ap, bf16[384,384]{1,0:T(8,128)(2,1)} %collective-permute-done.25.bp, ...), custom_call_target="tpu_custom_call" | custom-call | flops 905969664 | bytes 4718592 | tf_op jit(solution)/shard_map/project/pallas_call | solution.py:276
  231.7 3.4 %project.2 = f32[384,768]{1,0:T(8,128)S(1)} custom-call(s32[7]{0:T(128)S(1)} %stack.103.sc_ref, bf16[384,384]{1,0:T(8,128)(2,1)} %get-tuple-element.11.an, bf16[384,384]{1,0:T(8,128)(2,1)} %collective-permute-done.23.bn, bf16[384,384]{1,0:T(8,128)(2,1)} %collective-permute-done.24.ap, bf16[384,384]{1,0:T(8,128)(2,1)} %collective-permute-done.25.bp, ...), custom_call_target="tpu_custom_call" | custom-call | flops 905969664 | bytes 4718592 | tf_op jit(solution)/shard_map/project/pallas_call | solution.py:276
  235.0 9.6 %collective-permute-done.39 = bf16[384,768]{1,0:T(8,128)(2,1)} collective-permute-done((bf16[384,768]{1,0:T(8,128)(2,1)}, bf16[384,768]{1,0:T(8,128)(2,1)}, u32[]{:S(2)}, u32[]{:S(2)}) %collective-permute-start.39) | collective-permute-done | bytes 589856 | tf_op jit(solution)/shard_map/ppermute | solution.py:326
  244.7 2.3 add_convert_fusion
  (87 shorter events, 19.7 us)
Async XLA Ops:
  2.5 27.3 %collective-permute-start.10 = (bf16[3,3,384,128]{3,2,1,0:T(8,128)(2,1)S(1)}, bf16[3,3,384,128]{3,2,1,0:T(8,128)(2,1)}, u32[]{:S(2)}, u32[]{:S(2)}) collective-permute-start(bf16[3,3,384,128]{3,2,1,0:T(8,128)(2,1)S(1)} %get-tuple-element.14), channel_id=1, source_target_pairs={{0,5},{1,8},{2,7},{3,10},{4,1},{5,12},{6,3},{7,14},{8,0},{9,13},{1... | collective-permute-start | bytes 2654216 | tf_op jit(solution)/shard_map/ppermute | solution.py:326
  6.7 42.2 %collective-permute-start = (bf16[192,3072]{1,0:T(8,128)(2,1)}, bf16[192,3072]{1,0:T(8,128)(2,1)}, u32[]{:S(2)}, u32[]{:S(2)}) collective-permute-start(bf16[192,3072]{1,0:T(8,128)(2,1)} %norm_rows.2.refs_0_), channel_id=1, source_target_pairs={{0,4},{2,6},{5,1},{7,3},{8,12},{10,14},{13,9},{15,11},{16,20},{18,... | collective-permute-start | bytes 3538952 | tf_op jit(solution)/shard_map/ppermute | solution.py:326
  8.0 23.1 %collective-permute-start.15 = (bf16[3,3,384,128]{3,2,1,0:T(8,128)(2,1)}, bf16[3,3,384,128]{3,2,1,0:T(8,128)(2,1)}, u32[]{:S(2)}, u32[]{:S(2)}) collective-permute-start(bf16[3,3,384,128]{3,2,1,0:T(8,128)(2,1)} %get-tuple-element.13), channel_id=1, source_target_pairs={{1,12},{3,14},{5,8},{7,10},{8,5},{10,7},{12,1},{14,3},{17,28},{19,... | collective-permute-start | bytes 2654216 | tf_op jit(solution)/shard_map/ppermute | solution.py:326
  9.7 63.5 %collective-permute-start.2 = (bf16[192,3072]{1,0:T(8,128)(2,1)}, bf16[192,3072]{1,0:T(8,128)(2,1)}, u32[]{:S(2)}, u32[]{:S(2)}) collective-permute-start(bf16[192,3072]{1,0:T(8,128)(2,1)} %norm_rows.2.refs_0_), channel_id=1, source_target_pairs={{5,9},{7,11},{8,4},{10,6},{21,25},{23,27},{24,20},{26,22}} | collective-permute-start | bytes 3538952 | tf_op jit(solution)/shard_map/ppermute | solution.py:326
  11.0 64.6 %collective-permute-start.29 = (bf16[768,768]{1,0:T(8,128)(2,1)S(1)}, bf16[768,768]{1,0:T(8,128)(2,1)S(1)}, u32[]{:S(2)}, u32[]{:S(2)}) collective-permute-start(bf16[768,768]{1,0:T(8,128)(2,1)S(1)} %bitcast.39), channel_id=1, source_target_pairs={{0,4},{2,6},{4,1},{6,3},{8,12},{10,14},{12,9},{14,11},{17,20},{19,... | collective-permute-start | bytes 3538952 | tf_op jit(solution)/shard_map/ppermute | solution.py:326
  29.8 47.4 %collective-permute-start.31 = (bf16[768,768]{1,0:T(8,128)(2,1)S(1)}, bf16[768,768]{1,0:T(8,128)(2,1)S(1)}, u32[]{:S(2)}, u32[]{:S(2)}) collective-permute-start(bf16[768,768]{1,0:T(8,128)(2,1)S(1)} %bitcast.40), channel_id=1, source_target_pairs={{4,9},{6,11},{8,4},{10,6},{21,25},{23,27},{25,20},{27,22}} | collective-permute-start | bytes 3538952 | tf_op jit(solution)/shard_map/ppermute | solution.py:326
  31.1 46.1 %collective-permute-start.11 = (bf16[3,3,384,128]{3,2,1,0:T(8,128)(2,1)}, bf16[3,3,384,128]{3,2,1,0:T(8,128)(2,1)S(1)}, u32[]{:S(2)}, u32[]{:S(2)}) collective-permute-start(bf16[3,3,384,128]{3,2,1,0:T(8,128)(2,1)} %collective-permute-done.10.refs_12_), channel_id=1, source_target_pairs={{0,16},{1,17},{2,18},{3,19},{4,20},{5,21},{6,22},{7,23},{8,24},{9,... | collective-permute-start | bytes 2654216 | tf_op jit(solution)/shard_map/ppermute | solution.py:326
  36.3 90.6 %copy-start.8 = (bf16[3,3,768,128]{3,2,1,0:T(8,128)(2,1)}, bf16[3,3,768,128]{3,2,1,0:T(8,128)(2,1)S(1)}, u32[]{:S(2)}) copy-start(bf16[3,3,768,128]{3,2,1,0:T(8,128)(2,1)S(1)} %dynamic-slice_bitcast_fusion.refs_16_) | copy-start | bytes 5308420
  48.9 43.9 %collective-permute-start.14 = (bf16[3,3,768,128]{3,2,1,0:T(8,128)(2,1)S(1)}, bf16[3,3,768,128]{3,2,1,0:T(8,128)(2,1)}, u32[]{:S(2)}, u32[]{:S(2)}) collective-permute-start(bf16[3,3,768,128]{3,2,1,0:T(8,128)(2,1)S(1)} %dynamic-slice_bitcast_fusion.refs_16_), channel_id=1, source_target_pairs={{0,1},{2,3},{4,5},{6,7},{9,8},{11,10},{13,12},{15,14},{16,17},{18,... | collective-permute-start | bytes 5308424 | tf_op jit(solution)/shard_map/ppermute | solution.py:326
  73.1 15.5 %collective-permute-start.3 = (bf16[192,3072]{1,0:T(8,128)(2,1)}, bf16[192,3072]{1,0:T(8,128)(2,1)}, u32[]{:S(2)}, u32[]{:S(2)}) collective-permute-start(bf16[192,3072]{1,0:T(8,128)(2,1)} %collective-permute-done.refs_1_), channel_id=1, source_target_pairs={{4,8},{6,10},{9,5},{11,7},{20,24},{22,26},{25,21},{27,23}} | collective-permute-start | bytes 3538952 | tf_op jit(solution)/shard_map/ppermute | solution.py:326
  75.6 2.9 %collective-permute-start.16 = (bf16[3,3,384,128]{3,2,1,0:T(8,128)(2,1)}, bf16[3,3,384,128]{3,2,1,0:T(8,128)(2,1)}, u32[]{:S(2)}, u32[]{:S(2)}) collective-permute-start(bf16[3,3,384,128]{3,2,1,0:T(8,128)(2,1)} %collective-permute-done.15.refs_18_), channel_id=1, source_target_pairs={{1,17},{3,19},{5,21},{7,23},{8,24},{10,26},{12,28},{14,30},{17,1},... | collective-permute-start | bytes 2654216 | tf_op jit(solution)/shard_map/ppermute | solution.py:326
  77.2 3.7 %collective-permute-start.12 = (bf16[3,3,384,128]{3,2,1,0:T(8,128)(2,1)}, bf16[3,3,384,128]{3,2,1,0:T(8,128)(2,1)S(1)}, u32[]{:S(2)}, u32[]{:S(2)}) collective-permute-start(bf16[3,3,384,128]{3,2,1,0:T(8,128)(2,1)} %collective-permute-done.10.refs_12_), channel_id=1, source_target_pairs={{0,1},{1,0},{2,3},{3,2},{4,5},{5,4},{6,7},{7,6},{8,9},{9,8},{10,11... | collective-permute-start | bytes 2654216 | tf_op jit(solution)/shard_map/ppermute | solution.py:326
  77.2 49.7 %copy-start.11 = (bf16[3,3,384,128]{3,2,1,0:T(8,128)(2,1)}, bf16[3,3,384,128]{3,2,1,0:T(8,128)(2,1)S(1)}, u32[]{:S(2)}) copy-start(bf16[3,3,384,128]{3,2,1,0:T(8,128)(2,1)S(1)} %collective-permute-done.11.refs_13_) | copy-start | bytes 2654212
  77.2 13.1 %collective-permute-start.17 = (bf16[3,3,384,128]{3,2,1,0:T(8,128)(2,1)}, bf16[3,3,384,128]{3,2,1,0:T(8,128)(2,1)}, u32[]{:S(2)}, u32[]{:S(2)}) collective-permute-start(bf16[3,3,384,128]{3,2,1,0:T(8,128)(2,1)} %collective-permute-done.15.refs_18_), channel_id=1, source_target_pairs={{1,0},{3,2},{5,4},{7,6},{8,9},{10,11},{12,13},{14,15},{17,16},{19,... | collective-permute-start | bytes 2654216 | tf_op jit(solution)/shard_map/ppermute | solution.py:326
  78.5 18.2 %collective-permute-start.4 = (bf16[192,3072]{1,0:T(8,128)(2,1)}, bf16[192,3072]{1,0:T(8,128)(2,1)}, u32[]{:S(2)}, u32[]{:S(2)}) collective-permute-start(bf16[192,3072]{1,0:T(8,128)(2,1)} %collective-permute-done.2.refs_4_), channel_id=1, source_target_pairs={{4,0},{6,2},{9,13},{11,15},{20,16},{22,18},{25,29},{27,31}} | collective-permute-start | bytes 3538952 | tf_op jit(solution)/shard_map/ppermute | solution.py:326
  80.8 11.9 %copy-start.12 = (bf16[3,3,384,128]{3,2,1,0:T(8,128)(2,1)}, bf16[3,3,384,128]{3,2,1,0:T(8,128)(2,1)S(1)}, u32[]{:S(2)}) copy-start(bf16[3,3,384,128]{3,2,1,0:T(8,128)(2,1)S(1)} %collective-permute-done.12.refs_14_) | copy-start | bytes 2654212
  80.8 18.4 %collective-permute-start.1 = (bf16[192,3072]{1,0:T(8,128)(2,1)}, bf16[192,3072]{1,0:T(8,128)(2,1)S(1)}, u32[]{:S(2)}, u32[]{:S(2)}) collective-permute-start(bf16[192,3072]{1,0:T(8,128)(2,1)} %collective-permute-done.refs_1_), channel_id=1, source_target_pairs={{1,3},{3,1},{4,6},{6,4},{9,11},{11,9},{12,14},{14,12},{17,19},{19,... | collective-permute-start | bytes 3538952 | tf_op jit(solution)/shard_map/ppermute | solution.py:326
  88.6 12.3 %collective-permute-start.5 = (bf16[192,3072]{1,0:T(8,128)(2,1)}, bf16[192,3072]{1,0:T(8,128)(2,1)}, u32[]{:S(2)}, u32[]{:S(2)}) collective-permute-start(bf16[192,3072]{1,0:T(8,128)(2,1)} %collective-permute-done.3.refs_5_), channel_id=1, source_target_pairs={{5,1},{7,3},{8,12},{10,14},{21,17},{23,19},{24,28},{26,30}} | collective-permute-start | bytes 3538952 | tf_op jit(solution)/shard_map/ppermute | solution.py:326
  90.3 34.1 %collective-permute-start.6 = (bf16[192,3072]{1,0:T(8,128)(2,1)}, bf16[192,3072]{1,0:T(8,128)(2,1)S(1)}, u32[]{:S(2)}, u32[]{:S(2)}) collective-permute-start(bf16[192,3072]{1,0:T(8,128)(2,1)} %collective-permute-done.2.refs_4_), channel_id=1, source_target_pairs={{4,6},{6,4},{9,11},{11,9},{20,22},{22,20},{25,27},{27,25}} | collective-permute-start | bytes 3538952 | tf_op jit(solution)/shard_map/ppermute | solution.py:326
  92.7 31.7 %collective-permute-start.33 = (bf16[768,768]{1,0:T(8,128)(2,1)S(1)}, bf16[768,768]{1,0:T(8,128)(2,1)S(1)}, u32[]{:S(2)}, u32[]{:S(2)}) collective-permute-start(bf16[768,768]{1,0:T(8,128)(2,1)S(1)} %collective-permute-done.29.refs_2_), channel_id=1, source_target_pairs={{4,8},{6,10},{9,5},{11,7},{20,24},{22,26},{25,21},{27,23}} | collective-permute-start | bytes 3538952 | tf_op jit(solution)/shard_map/ppermute | solution.py:326
  96.7 42.0 %collective-permute-start.7 = (bf16[192,3072]{1,0:T(8,128)(2,1)}, bf16[192,3072]{1,0:T(8,128)(2,1)}, u32[]{:S(2)}, u32[]{:S(2)}) collective-permute-start(bf16[192,3072]{1,0:T(8,128)(2,1)} %collective-permute-done.3.refs_5_), channel_id=1, source_target_pairs={{5,7},{7,5},{8,10},{10,8},{21,23},{23,21},{24,26},{26,24}} | collective-permute-start | bytes 3538952 | tf_op jit(solution)/shard_map/ppermute | solution.py:326
  99.2 27.6 %copy-start.9 = (bf16[192,3072]{1,0:T(8,128)(2,1)}, bf16[192,3072]{1,0:T(8,128)(2,1)S(1)}, u32[]{:S(2)}) copy-start(bf16[192,3072]{1,0:T(8,128)(2,1)S(1)} %collective-permute-done.1.refs_3_) | copy-start | bytes 3538948
  99.2 41.3 %collective-permute-start.8 = (bf16[192,3072]{1,0:T(8,128)(2,1)}, bf16[192,3072]{1,0:T(8,128)(2,1)}, u32[]{:S(2)}, u32[]{:S(2)}) collective-permute-start(bf16[192,3072]{1,0:T(8,128)(2,1)} %collective-permute-done.4.refs_6_), channel_id=1, source_target_pairs={{0,2},{2,0},{13,15},{15,13},{16,18},{18,16},{29,31},{31,29}} | collective-permute-start | bytes 3538952 | tf_op jit(solution)/shard_map/ppermute | solution.py:326
  100.9 39.7 %collective-permute-start.9 = (bf16[192,3072]{1,0:T(8,128)(2,1)}, bf16[192,3072]{1,0:T(8,128)(2,1)}, u32[]{:S(2)}, u32[]{:S(2)}) collective-permute-start(bf16[192,3072]{1,0:T(8,128)(2,1)} %collective-permute-done.5.refs_7_), channel_id=1, source_target_pairs={{1,3},{3,1},{12,14},{14,12},{17,19},{19,17},{28,30},{30,28}} | collective-permute-start | bytes 3538952 | tf_op jit(solution)/shard_map/ppermute | solution.py:326
  124.4 2.4 collective-permute-start.13
  124.4 12.0 %collective-permute-start.18 = (bf16[3,3,384,128]{3,2,1,0:T(8,128)(2,1)}, bf16[3,3,384,128]{3,2,1,0:T(8,128)(2,1)}, u32[]{:S(2)}, u32[]{:S(2)}) collective-permute-start(bf16[3,3,384,128]{3,2,1,0:T(8,128)(2,1)} %collective-permute-done.16.refs_19_), channel_id=1, source_target_pairs={{1,0},{3,2},{5,4},{7,6},{8,9},{10,11},{12,13},{14,15},{17,16},{19,... | collective-permute-start | bytes 2654216 | tf_op jit(solution)/shard_map/ppermute | solution.py:326
  127.8 46.1 %collective-permute-start.28 = (bf16[768,768]{1,0:T(8,128)(2,1)S(1)}, bf16[768,768]{1,0:T(8,128)(2,1)}, u32[]{:S(2)}, u32[]{:S(2)}) collective-permute-start(bf16[768,768]{1,0:T(8,128)(2,1)S(1)} %bitcast.41), channel_id=1, source_target_pairs={{1,0},{3,2},{4,5},{6,7},{9,8},{11,10},{12,13},{14,15},{17,16},{19,... | collective-permute-start | bytes 3538952 | tf_op jit(solution)/shard_map/ppermute | solution.py:326
  136.5 41.2 %collective-permute-start.35 = (bf16[768,768]{1,0:T(8,128)(2,1)S(1)}, bf16[768,768]{1,0:T(8,128)(2,1)}, u32[]{:S(2)}, u32[]{:S(2)}) collective-permute-start(bf16[768,768]{1,0:T(8,128)(2,1)S(1)} %collective-permute-done.31.refs_4_), channel_id=1, source_target_pairs={{4,0},{6,2},{9,13},{11,15},{20,16},{22,18},{25,29},{27,31}} | collective-permute-start | bytes 3538952 | tf_op jit(solution)/shard_map/ppermute | solution.py:326
  138.8 40.6 %collective-permute-start.37 = (bf16[768,768]{1,0:T(8,128)(2,1)}, bf16[768,768]{1,0:T(8,128)(2,1)}, u32[]{:S(2)}, u32[]{:S(2)}) collective-permute-start(bf16[768,768]{1,0:T(8,128)(2,1)} %copy-done.1), channel_id=1, source_target_pairs={{5,1},{7,3},{8,12},{10,14},{21,17},{23,19},{24,28},{26,30}} | collective-permute-start | bytes 3538952 | tf_op jit(solution)/shard_map/ppermute | solution.py:326
  140.5 12.0 %copy-start.16 = (s32[1,9]{1,0:T(1,128)S(1)}, s32[1,9]{1,0:T(1,128)}, u32[]{:S(2)}) copy-start(s32[1,9]{1,0:T(1,128)} %param.20) | copy-start | bytes 112
  140.6 12.0 %copy-start.17 = (s32[1,9]{1,0:T(1,128)S(1)}, s32[1,9]{1,0:T(1,128)}, u32[]{:S(2)}) copy-start(s32[1,9]{1,0:T(1,128)} %param.19) | copy-start | bytes 112
  140.6 12.1 %copy-start.14 = (s32[384]{0:T(512)S(1)}, s32[384]{0:T(512)}, u32[]{:S(2)}) copy-start(s32[384]{0:T(512)} %param.21) | copy-start | bytes 4612
  152.4 28.6 %collective-permute-start.19 = (bf16[2,384,768]{2,1,0:T(8,128)(2,1)}, bf16[2,384,768]{2,1,0:T(8,128)(2,1)S(1)}, u32[]{:S(2)}, u32[]{:S(2)}) collective-permute-start(bf16[2,384,768]{2,1,0:T(8,128)(2,1)} %get-tuple-element.10.kv0), channel_id=1, source_target_pairs={{0,1},{1,0},{2,3},{3,2},{4,5},{5,4},{6,7},{7,6},{8,9},{9,8},{10,11... | collective-permute-start | bytes 3538952 | tf_op jit(solution)/shard_map/ppermute | solution.py:326
  152.7 11.1 %collective-permute-start.20 = (s32[1,512]{1,0:T(1,128)S(1)}, s32[1,512]{1,0:T(1,128)S(1)}, u32[]{:S(2)}, u32[]{:S(2)}) collective-permute-start(s32[1,512]{1,0:T(1,128)S(1)} %bitcast.48), channel_id=1, source_target_pairs={{0,4},{1,5},{2,6},{3,7},{4,0},{5,1},{6,2},{7,3},{8,12},{9,13},{10,... | collective-permute-start | bytes 6152 | tf_op jit(solution)/shard_map/ppermute | solution.py:326
  163.7 4.5 %collective-permute-start.21 = (s32[1,512]{1,0:T(1,128)S(1)}, s32[1,512]{1,0:T(1,128)S(1)}, u32[]{:S(2)}, u32[]{:S(2)}) collective-permute-start(s32[1,512]{1,0:T(1,128)S(1)} %bitcast.49), channel_id=1, source_target_pairs={{0,8},{1,9},{2,10},{3,11},{4,12},{5,13},{6,14},{7,15},{8,0},{9,1},... | collective-permute-start | bytes 6152 | tf_op jit(solution)/shard_map/ppermute | solution.py:326
  168.2 3.6 %collective-permute-start.22 = (s32[1,512]{1,0:T(1,128)S(1)}, s32[1,512]{1,0:T(1,128)S(1)}, u32[]{:S(2)}, u32[]{:S(2)}) collective-permute-start(s32[1,512]{1,0:T(1,128)S(1)} %bitcast.50), channel_id=1, source_target_pairs={{0,12},{1,13},{2,14},{3,15},{4,8},{5,9},{6,10},{7,11},{8,4},{9,5},... | collective-permute-start | bytes 6152 | tf_op jit(solution)/shard_map/ppermute | solution.py:326
  171.8 9.3 %copy-start.15 = (s32[1,512]{1,0:T(1,128)}, s32[1,512]{1,0:T(1,128)S(1)}, u32[]{:S(2)}) copy-start(s32[1,512]{1,0:T(1,128)S(1)} %collective-permute-done.22) | copy-start | bytes 6148
  171.8 30.7 %collective-permute-start.30 = (bf16[768,768]{1,0:T(8,128)(2,1)S(1)}, bf16[768,768]{1,0:T(8,128)(2,1)}, u32[]{:S(2)}, u32[]{:S(2)}) collective-permute-start(bf16[768,768]{1,0:T(8,128)(2,1)S(1)} %collective-permute-done.29.refs_2_), channel_id=1, source_target_pairs={{1,17},{3,19},{4,20},{6,22},{9,25},{11,27},{12,28},{14,30},{17,1},... | collective-permute-start | bytes 3538952 | tf_op jit(solution)/shard_map/ppermute | solution.py:326
  173.9 41.4 %collective-permute-start.32 = (bf16[768,768]{1,0:T(8,128)(2,1)S(1)}, bf16[768,768]{1,0:T(8,128)(2,1)}, u32[]{:S(2)}, u32[]{:S(2)}) collective-permute-start(bf16[768,768]{1,0:T(8,128)(2,1)S(1)} %collective-permute-done.31.refs_4_), channel_id=1, source_target_pairs={{4,20},{6,22},{9,25},{11,27},{20,4},{22,6},{25,9},{27,11}} | collective-permute-start | bytes 3538952 | tf_op jit(solution)/shard_map/ppermute | solution.py:326
  177.7 37.6 %collective-permute-start.34 = (bf16[768,768]{1,0:T(8,128)(2,1)}, bf16[768,768]{1,0:T(8,128)(2,1)}, u32[]{:S(2)}, u32[]{:S(2)}) collective-permute-start(bf16[768,768]{1,0:T(8,128)(2,1)} %copy-done.1), channel_id=1, source_target_pairs={{5,21},{7,23},{8,24},{10,26},{21,5},{23,7},{24,8},{26,10}} | collective-permute-start | bytes 3538952 | tf_op jit(solution)/shard_map/ppermute | solution.py:326
  179.4 42.2 %collective-permute-start.36 = (bf16[768,768]{1,0:T(8,128)(2,1)}, bf16[768,768]{1,0:T(8,128)(2,1)}, u32[]{:S(2)}, u32[]{:S(2)}) collective-permute-start(bf16[768,768]{1,0:T(8,128)(2,1)} %collective-permute-done.35.refs_8_), channel_id=1, source_target_pairs={{0,16},{2,18},{13,29},{15,31},{16,0},{18,2},{29,13},{31,15}} | collective-permute-start | bytes 3538952 | tf_op jit(solution)/shard_map/ppermute | solution.py:326
  182.2 39.5 %collective-permute-start.38 = (bf16[768,768]{1,0:T(8,128)(2,1)}, bf16[768,768]{1,0:T(8,128)(2,1)}, u32[]{:S(2)}, u32[]{:S(2)}) collective-permute-start(bf16[768,768]{1,0:T(8,128)(2,1)} %collective-permute-done.37.refs_10_), channel_id=1, source_target_pairs={{1,17},{3,19},{12,28},{14,30},{17,1},{19,3},{28,12},{30,14}} | collective-permute-start | bytes 3538952 | tf_op jit(solution)/shard_map/ppermute | solution.py:326
  202.5 14.1 %collective-permute-start.24 = (bf16[384,384]{1,0:T(8,128)(2,1)}, bf16[384,384]{1,0:T(8,128)(2,1)}, u32[]{:S(2)}, u32[]{:S(2)}) collective-permute-start(bf16[384,384]{1,0:T(8,128)(2,1)} %get-tuple-element.11.an), channel_id=1, source_target_pairs={{1,5},{3,7},{4,0},{6,2},{9,13},{11,15},{12,8},{14,10},{17,21},{19,... | collective-permute-start | bytes 884744 | tf_op jit(solution)/shard_map/ppermute | solution.py:326
  215.3 6.3 %collective-permute-start.26 = (bf16[384,384]{1,0:T(8,128)(2,1)S(1)}, bf16[384,384]{1,0:T(8,128)(2,1)}, u32[]{:S(2)}, u32[]{:S(2)}) collective-permute-start(bf16[384,384]{1,0:T(8,128)(2,1)S(1)} %get-tuple-element.12), channel_id=1, source_target_pairs={{0,8},{1,12},{2,10},{3,14},{4,9},{5,13},{6,11},{7,15},{8,0},{9,4},... | collective-permute-start | bytes 884744 | tf_op jit(solution)/shard_map/ppermute | solution.py:326
  215.3 6.3 %collective-permute-start.23 = (bf16[384,384]{1,0:T(8,128)(2,1)}, bf16[384,384]{1,0:T(8,128)(2,1)}, u32[]{:S(2)}, u32[]{:S(2)}) collective-permute-start(bf16[384,384]{1,0:T(8,128)(2,1)} %get-tuple-element.11.an), channel_id=1, source_target_pairs={{0,1},{2,3},{5,4},{7,6},{8,9},{10,11},{13,12},{15,14},{16,17},{18,... | collective-permute-start | bytes 884744 | tf_op jit(solution)/shard_map/ppermute | solution.py:326
  216.6 5.1 %collective-permute-start.25 = (bf16[384,384]{1,0:T(8,128)(2,1)}, bf16[384,384]{1,0:T(8,128)(2,1)}, u32[]{:S(2)}, u32[]{:S(2)}) collective-permute-start(bf16[384,384]{1,0:T(8,128)(2,1)} %collective-permute-done.24.ap), channel_id=1, source_target_pairs={{0,1},{2,3},{5,4},{7,6},{8,9},{10,11},{13,12},{15,14},{16,17},{18,... | collective-permute-start | bytes 884744 | tf_op jit(solution)/shard_map/ppermute | solution.py:326
  221.5 1.9 collective-permute-start.27
  228.9 15.7 %collective-permute-start.39 = (bf16[384,768]{1,0:T(8,128)(2,1)}, bf16[384,768]{1,0:T(8,128)(2,1)}, u32[]{:S(2)}, u32[]{:S(2)}) collective-permute-start(bf16[384,768]{1,0:T(8,128)(2,1)} %project.3), channel_id=1, source_target_pairs={{0,2},{1,3},{2,0},{3,1},{4,6},{5,7},{6,4},{7,5},{8,10},{9,11},{10,... | collective-permute-start | bytes 1769480 | tf_op jit(solution)/shard_map/ppermute | solution.py:326
  (10 other events, 20.4 us)

commit v2 on v1

--- a/solution.py
+++ b/solution.py
@@ -146,7 +146,7 @@
     tokens = [t for mine, others in candidates for t in (*mine, *others)]
     smem = pl.BlockSpec(memory_space=pltpu.SMEM)
     vmem = pl.BlockSpec(memory_space=pltpu.VMEM)
-    anywhere = pl.BlockSpec(memory_space=pl.ANY)
+    anywhere = pl.BlockSpec(memory_space=pltpu.HBM)
     return pl.pallas_call(
         functools.partial(qkv_kernel, counts),
         out_shape=(
@@ -164,6 +164,7 @@
             pltpu.SemaphoreType.DMA((8,)),
             pltpu.SemaphoreType.DMA((2,)),
         ],
+        compiler_params=pltpu.CompilerParams(vmem_limit_bytes=28 << 20),
         cost_estimate=pl.CostEstimate(
             flops=12 * rows * width * out, bytes_accessed=width * 3 * out * 2, transcendentals=0
         ),
@@ -227,9 +228,9 @@
     )(scalars, queries, kv, kv_other, flags)
 
 
-def project_kernel(sc_ref, an, bn, ap, bp, f0, f1, *refs):
-    firsts, seconds = refs[0:12:2], refs[1:12:2]
-    out_ref, att_ref, w_ref, att_sem, w_sem = refs[12:]
+def project_kernel(sc_ref, an, pn, bp, f0, f1, *refs):
+    firsts, seconds = refs[0:10:2], refs[1:10:2]
+    out_ref, att_ref, w_ref, att_sem, w_sem = refs[10:]
     _, width = an.shape
     depth = w_ref.shape[1]
 
@@ -240,24 +241,29 @@
     @pl.when(sc_ref[0] == 1)
     def _():
         piece_copy(an, 0).start()
-        piece_copy(ap, 1).start()
+        piece_copy(pn, 1).start()
 
     @pl.when(sc_ref[0] == 0)
     def _():
-        piece_copy(bn, 0).start()
+        piece_copy(pn, 0).start()
         piece_copy(bp, 1).start()
 
     piece_copy(f0, 2).start()
     piece_copy(f1, 3).start()
-    for i in range(6):
+    for i in range(5):
 
         @pl.when(sc_ref[5] == i)
         def _():
             pltpu.make_async_copy(firsts[i], w_ref.at[0], w_sem.at[0]).start()
-            pltpu.make_async_copy(seconds[i], w_ref.at[1], w_sem.at[1]).start()
 
     for i in range(4):
         piece_copy(f0, i).wait()
+    for i in range(5):
+
+        @pl.when(sc_ref[5] == i)
+        def _():
+            pltpu.make_async_copy(seconds[i], w_ref.at[1], w_sem.at[1]).start()
+
     terms = []
     for i in range(2):
         group = sc_ref[6] if i == 0 else 1 - sc_ref[6]
@@ -272,7 +278,7 @@
     depth, width = weights[0].shape
     smem = pl.BlockSpec(memory_space=pltpu.SMEM)
     vmem = pl.BlockSpec(memory_space=pltpu.VMEM)
-    anywhere = pl.BlockSpec(memory_space=pl.ANY)
+    anywhere = pl.BlockSpec(memory_space=pltpu.HBM)
     return pl.pallas_call(
         project_kernel,
         out_shape=jax.ShapeDtypeStruct((rows, width), dtype),
@@ -334,14 +340,23 @@
     def mid(zz):
         return zz in (1, 2)
 
-    def to_core(who=lambda zz, cc: True):
-        return lambda yy, zz, xx, cc: (yy, zz, xx, 1 - cc) if who(zz, cc) else None
+    def to_core(yy, zz, xx, cc):
+        return (yy, zz, xx, 1 - cc)
 
     def to_column(who=lambda zz, cc: True):
         return lambda yy, zz, xx, cc: (yy, zz, 1 - xx, cc) if who(zz, cc) else None
 
     def to_replica(who=lambda zz, cc: True):
         return lambda yy, zz, xx, cc: (1 - yy, zz, xx, cc) if who(zz, cc) else None
+
+    def else_core(real, left_out=lambda zz, cc: False):
+        def target(yy, zz, xx, cc):
+            to = real(yy, zz, xx, cc)
+            if to is None and not left_out(zz, cc):
+                return to_core(yy, zz, xx, cc)
+            return to
+
+        return target
 
     own = z % 2 == c
     at_home = z // 2 == c
@@ -376,8 +391,8 @@
         return lambda yy, zz, xx, cc: (yy, zz ^ 1, xx, cc) if who(zz, cc) else None
 
     n_mine = norm_rows(latents, mod_shift, mod_scale, x)
-    r1 = move(n_mine, outward(owns))
-    r2a = move(n_mine, across(mid_own))
+    r1 = move(n_mine, else_core(outward(owns)))
+    r2a = move(n_mine, else_core(across(mid_own)))
 
     slot_a = jnp.where(at_home, 1 - parity, parity)
     slot_b = jnp.where(at_home, parity, 1 - parity)
@@ -394,25 +409,30 @@
         + [move(flags, lambda yy, zz, xx, cc, d=d: (yy, zz ^ d, xx, cc)) for d in range(1, nz)]
     )
 
-    n_other = norm_rows(latents, mod_shift, mod_scale, 1 - x)
     own_w = lax.dynamic_slice(w_t, (0, parity * heads, 0, 0), (3, heads, depth, hd))
 
-    r2b = move(r1, across(mid_rest))
-    x_r1 = move(r1, to_column(lambda zz, cc: not owns(zz, cc)))
-    r3a = move(r2a, outward(mid_rest))
-    x_r2a = move(r2a, to_column(mid_rest))
-    r3b = move(r2b, outward(mid_own))
-    x_r2b = move(r2b, to_column(mid_own))
-    x_r3a = move(r3a, to_column(end_own))
-    x_r3b = move(r3b, to_column(end_rest))
+    def mids(zz, cc):
+        return mid(zz)
+
+    def ends(zz, cc):
+        return not mid(zz)
+
+    r2b = move(r1, else_core(across(mid_rest)))
+    x_r1 = move(r1, to_column())
+    r3a = move(r2a, else_core(outward(mid_rest), end_rest))
+    x_r2a = move(r2a, else_core(to_column(mid_rest), mids))
+    r3b = move(r2b, else_core(outward(mid_own), end_own))
+    x_r2b = move(r2b, else_core(to_column(mid_own), mids))
+    x_r3a = move(r3a, else_core(to_column(end_own), ends))
+    x_r3b = move(r3b, else_core(to_column(end_rest), ends))
 
     y_a = move(z_a, to_replica())
-    c_a1 = move(z_a, to_core())
-    c_own = move(own_w, to_core(home))
+    c_a1 = move(z_a, to_core)
+    c_own = move(own_w, to_core)
     y_b = move(z_b, to_replica(lambda zz, cc: not home(zz, cc)))
-    c_b1 = move(z_b, to_core(lambda zz, cc: not home(zz, cc)))
-    c_a2 = move(y_a, to_core())
-    c_b2 = move(y_b, to_core(lambda zz, cc: not home(zz, cc)))
+    c_b1 = move(z_b, to_core)
+    c_a2 = move(y_a, to_core)
+    c_b2 = move(y_b, to_core)
     weights = (z_a, y_a, c_a1, c_a2, own_w, c_own, z_b, y_b, c_b1, c_b2)
     sources = (
         jnp.where(c == 0, z ^ 2, z ^ 1),
@@ -424,41 +444,52 @@
         at_home,
     )
 
-    s1 = move(wo, lambda yy, zz, xx, cc: (yy, zz ^ 1, xx, zz % 2) if cc == yy else None)
-    s2a = move(wo, lambda yy, zz, xx, cc: (yy, 3 - zz, xx, zz % 2) if cc == yy and mid(zz) else None)
-    c_f = move(wo, to_core(lambda zz, cc: not owns(zz, cc)))
-    s2b = move(s1, across(mid_rest))
-    y_f = move(s1, to_replica(lambda zz, cc: not owns(zz, cc)))
-    s3a = move(s2a, outward(mid_rest))
-    s3b = move(s2b, outward(mid_own))
-    y_2a = move(s2a, to_replica(mid_rest))
-    y_2b = move(s2b, to_replica(mid_own))
-    y_3a = move(s3a, to_replica(end_own))
-    y_3b = move(s3b, to_replica(end_rest))
-
-    picks = (jnp.where(own, 0, 1), jnp.where(is_mid, jnp.where(own, 1, 0), jnp.where(own, 2, 3)))
+    def spread(step):
+        def target(yy, zz, xx, cc):
+            if cc == yy:
+                return (yy, zz ^ step, xx, zz % 2)
+            reached = (zz ^ step) % 2
+            return None if cc != reached else to_core(yy, zz, xx, cc)
+
+        return target
+
+    s1 = move(wo, spread(1))
+
+    def to_mids(yy, zz, xx, cc):
+        if cc == yy:
+            return (yy, 3 - zz if mid(zz) else zz ^ 2, xx, zz % 2)
+        return None if mid(zz) else to_core(yy, zz, xx, cc)
+
+    s2 = move(wo, to_mids)
+    s3 = move(s2, outward(mids))
+    c_f = move(wo, to_core)
+    y_1 = move(s1, to_replica(lambda zz, cc: not owns(zz, cc)))
+    y_2 = move(s2, else_core(to_replica(mids), lambda zz, cc: False))
+    y_3 = move(s3, else_core(to_replica(end_own), ends))
+    s4 = move(y_2, outward(mid_own))
+
+    picks = (0, jnp.where(is_mid, jnp.where(own, 1, 0), jnp.where(own, 2, 3)))
     queries, kv = qkv_tiles(
         scalars_of(*sources, *picks),
-        (((n_mine, r1), (n_other, x_r1)), ((r2a, r2b, r3a, r3b), (x_r2a, x_r2b, x_r3a, x_r3b))),
+        (((r1,), (x_r1,)), ((r2a, r2b, r3a, r3b), (x_r2a, x_r2b, x_r3a, x_r3b))),
         weights,
         query_gain,
         key_gain,
     )
-    kv_other = move(kv, to_core())
+    kv_other = move(kv, to_core)
 
     segments = (near, far, near_o, far_o)
     att_near, att_far = attend(scalars_of(*segments, *(s ^ z for s in segments)), queries, kv, kv_other, flags)
     p_far = move(att_far, lambda yy, zz, xx, cc: (yy, 2 * (1 - zz // 2) + cc, xx, zz % 2))
-    p_near = move(att_near, outward(lambda zz, cc: not owns(zz, cc)))
-    b_near = move(att_near, to_core(owns))
-    p_far_o = move(p_far, to_core())
-    b_pair = move(p_near, to_core(owns))
-
-    pieces = (att_near, b_near, p_near, b_pair, p_far, p_far_o)
-    blocks = (wo, c_f, s1, y_f, s2a, y_2a, s2b, y_2b, s3a, y_3a, s3b, y_3b)
+    p_near = move(att_near, else_core(outward(lambda zz, cc: not owns(zz, cc))))
+    p_far_o = move(p_far, to_core)
+    b_pair = move(p_near, to_core)
+
+    pieces = (att_near, p_near, b_pair, p_far, p_far_o)
+    blocks = (wo, c_f, s1, y_1, s2, y_2, s3, y_3, s3, s4)
     places = (own, z, z ^ 1, far, far_o)
     from_near = (jnp.where(own, 0, 1), jnp.where(own, c, y))
-    from_far = (2 + jnp.where(is_mid, jnp.where(own, 1, 0), jnp.where(own, 2, 3)), y)
+    from_far = (jnp.where(is_mid, 2, jnp.where(own, 3, 4)), y)
     near_stays = x == pair
 
     def project_block(near_block):

time: 248 us -> 286 us (1.15)
  the two profiles are of different devices: /device:TPU:14 before, /device:TPU:0 now
where the time goes in v2:
time: 286 us; the launch traced here: 285 us
  starting transfers between devices  133 us (47%)
  waiting for transfers between devices  94.2 us (33%)
  Pallas kernels  31.1 us (11%)
  local copies, waits for them, and re-layouts  22.8 us (8%)
  other arithmetic  3.08 us (1%)
    ppermute x36, starting transfers between devices, move(): return lax.ppermute(array, AXES, pairs)  133 us
    ppermute x36, waiting for transfers between devices, move(): return lax.ppermute(array, AXES, pairs)  94.2 us
    unnamed x48, local copies, waits for them, and re-layouts  18.5 us
    pallas_call x1, Pallas kernels, qkv_tiles(): pl.pallas_call(functools.partial(qkv_kernel, counts), out_shape=(jax.Shap...  11.3 us
    pallas_call x2, Pallas kernels, project(): pl.pallas_call(project_kernel, out_shape=jax.ShapeDtypeStruct((rows, widt...  8.59 us
    pallas_call x1, Pallas kernels, attend(): pl.pallas_call(attend_kernel, out_shape=(shape, shape), in_specs=[smem] +...  7.12 us
  transfers between devices with their start and end apart: 36, of which 11 were waited for; matrix products, arithmetic and copies ran while one was open for 1% of the time, Pallas kernels for 9%

profile of v2, /device:TPU:0, one launch (start us, length us, event | category | flops | bytes accessed | tf_op | source)
XLA Modules:
  0.0 284.7 jit_solution(11482181310225681023)
XLA Ops:
  0.0 1.5 dynamic-slice_bitcast_fusion.1
  1.6 2.6 collective-permute-start.10
  4.1 4.1 %norm_rows.1 = bf16[192,3072]{1,0:T(8,128)(2,1)} custom-call(s32[1]{0:T(128)} %bitcast.17.half_ref, bf16[384,3072]{1,0:T(8,128)(2,1)} %x_ref.1, f32[1,3072]{1,0:T(1,128)} %bitcast.39, f32[1,3072]{1,0:T(1,128)} %bitcast.40), custom_call_target="tpu_custom_call" | custom-call | flops 5898240 | bytes 2359296 | tf_op jit(solution)/shard_map/norm_rows/pallas_call | solution.py:32
  9.9 4.9 %collective-permute-start.30 = (bf16[768,768]{1,0:T(8,128)(2,1)}, bf16[768,768]{1,0:T(8,128)(2,1)S(1)}, u32[]{:S(2)}, u32[]{:S(2)}) collective-permute-start(bf16[768,768]{1,0:T(8,128)(2,1)} %bitcast.30.refs_0_), channel_id=1, source_target_pairs={{0,8},{1,0},{2,10},{3,2},{4,9},{6,11},{8,4},{10,6},{12,5},{13,12},... | collective-permute-start | bytes 3538952 | tf_op jit(solution)/shard_map/ppermute | solution.py:332
  14.8 1.6 collective-permute-start.15
  16.4 8.6 %collective-permute-done.10.refs_10_ = bf16[3,3,384,128]{3,2,1,0:T(8,128)(2,1)} collective-permute-done((bf16[3,3,384,128]{3,2,1,0:T(8,128)(2,1)S(1)}, bf16[3,3,384,128]{3,2,1,0:T(8,128)(2,1)}, u32[]{:S(2)}, u32[]{:S(2)}) %collective-permute-start.10) | collective-permute-done | bytes 884768 | tf_op jit(solution)/shard_map/ppermute | solution.py:332
  25.0 11.7 %collective-permute-start.11 = (bf16[3,3,384,128]{3,2,1,0:T(8,128)(2,1)}, bf16[3,3,384,128]{3,2,1,0:T(8,128)(2,1)}, u32[]{:S(2)}, u32[]{:S(2)}) collective-permute-start(bf16[3,3,384,128]{3,2,1,0:T(8,128)(2,1)} %collective-permute-done.10.refs_10_), channel_id=1, source_target_pairs={{0,16},{1,17},{2,18},{3,19},{4,20},{5,21},{6,22},{7,23},{8,24},{9,... | collective-permute-start | bytes 2654216 | tf_op jit(solution)/shard_map/ppermute | solution.py:332
  36.7 9.7 %collective-permute-done.refs_0_ = bf16[192,3072]{1,0:T(8,128)(2,1)} collective-permute-done((bf16[192,3072]{1,0:T(8,128)(2,1)}, bf16[192,3072]{1,0:T(8,128)(2,1)}, u32[]{:S(2)}, u32[]{:S(2)}) %collective-permute-start) | collective-permute-done | bytes 1179680 | tf_op jit(solution)/shard_map/ppermute | solution.py:332
  46.4 1.6 collective-permute-start.16
  48.0 1.6 dynamic-slice_bitcast_fusion.refs_14_
  49.7 15.3 %collective-permute-start.12 = (bf16[3,3,384,128]{3,2,1,0:T(8,128)(2,1)}, bf16[3,3,384,128]{3,2,1,0:T(8,128)(2,1)S(1)}, u32[]{:S(2)}, u32[]{:S(2)}) collective-permute-start(bf16[3,3,384,128]{3,2,1,0:T(8,128)(2,1)} %collective-permute-done.10.refs_10_), channel_id=1, source_target_pairs={{0,1},{1,0},{2,3},{3,2},{4,5},{5,4},{6,7},{7,6},{8,9},{9,8},{10,11... | collective-permute-start | bytes 2654216 | tf_op jit(solution)/shard_map/ppermute | solution.py:332
  65.5 11.8 %collective-permute-start.4 = (bf16[192,3072]{1,0:T(8,128)(2,1)}, bf16[192,3072]{1,0:T(8,128)(2,1)}, u32[]{:S(2)}, u32[]{:S(2)}) collective-permute-start(bf16[192,3072]{1,0:T(8,128)(2,1)} %collective-permute-done.2.refs_2_), channel_id=1, source_target_pairs={{0,1},{2,3},{4,0},{5,4},{6,2},{7,6},{8,9},{9,13},{10,11},{11,15},{... | collective-permute-start | bytes 3538952 | tf_op jit(solution)/shard_map/ppermute | solution.py:332
  77.3 1.3 collective-permute-start.5
  79.5 1.5 collective-permute-start.1
  82.0 2.7 collective-permute-start.6
  84.7 1.2 copy-done.2
  86.0 1.9 collective-permute-start.7
  87.9 33.0 %collective-permute-done.4.refs_4_ = bf16[192,3072]{1,0:T(8,128)(2,1)} collective-permute-done((bf16[192,3072]{1,0:T(8,128)(2,1)}, bf16[192,3072]{1,0:T(8,128)(2,1)}, u32[]{:S(2)}, u32[]{:S(2)}) %collective-permute-start.4) | collective-permute-done | bytes 1179680 | tf_op jit(solution)/shard_map/ppermute | solution.py:332
  120.9 3.2 %collective-permute-start.8 = (bf16[192,3072]{1,0:T(8,128)(2,1)}, bf16[192,3072]{1,0:T(8,128)(2,1)}, u32[]{:S(2)}, u32[]{:S(2)}) collective-permute-start(bf16[192,3072]{1,0:T(8,128)(2,1)} %collective-permute-done.4.refs_4_), channel_id=1, source_target_pairs={{0,2},{2,0},{4,5},{5,4},{6,7},{7,6},{8,9},{9,8},{10,11},{11,10},{1... | collective-permute-start | bytes 3538952 | tf_op jit(solution)/shard_map/ppermute | solution.py:332
  124.1 1.7 collective-permute-start.9
  126.8 8.5 %collective-permute-start.13 = (bf16[3,3,384,128]{3,2,1,0:T(8,128)(2,1)}, bf16[3,3,384,128]{3,2,1,0:T(8,128)(2,1)}, u32[]{:S(2)}, u32[]{:S(2)}) collective-permute-start(bf16[3,3,384,128]{3,2,1,0:T(8,128)(2,1)} %collective-permute-done.11.refs_11_), channel_id=1, source_target_pairs={{0,1},{1,0},{2,3},{3,2},{4,5},{5,4},{6,7},{7,6},{8,9},{9,8},{10,11... | collective-permute-start | bytes 2654216 | tf_op jit(solution)/shard_map/ppermute | solution.py:332
  137.7 34.5 %collective-permute-start.28 = (bf16[768,768]{1,0:T(8,128)(2,1)}, bf16[768,768]{1,0:T(8,128)(2,1)}, u32[]{:S(2)}, u32[]{:S(2)}) collective-permute-start(bf16[768,768]{1,0:T(8,128)(2,1)} %bitcast.30.refs_0_), channel_id=1, source_target_pairs={{0,4},{1,0},{2,6},{3,2},{4,1},{6,3},{8,12},{9,8},{10,14},{11,10},{... | collective-permute-start | bytes 3538952 | tf_op jit(solution)/shard_map/ppermute | solution.py:332
  172.2 1.3 collective-permute-start.32
  173.7 1.5 copy-done.3
  175.2 1.3 copy-done.5
  176.4 1.3 copy-done.7
  177.7 1.2 copy-done.12
  180.0 11.3 %qkv_tiles.1 = (bf16[2,384,384]{2,1,0:T(8,128)(2,1)S(1)}, bf16[2,384,768]{2,1,0:T(8,128)(2,1)}) custom-call(s32[9]{0:T(128)S(1)} %stack.116.sc_ref, bf16[192,3072]{1,0:T(8,128)(2,1)} %collective-permute-done.refs_0_, bf16[192,3072]{1,0:T(8,128)(2,1)S(1)} %copy-done.5, bf16[192,3072]{1,0:T(8,128)(2,1)} %collective-permute-done.2.refs_2_, ...), custom_call_target="tpu_custom_call" | custom-call | flops 5435817984 | bytes 7077888 | tf_op jit(solution)/shard_map/qkv_tiles/pallas_call | solution.py:150
  192.6 3.6 %collective-permute-start.20 = (s32[1,512]{1,0:T(1,128)S(1)}, s32[1,512]{1,0:T(1,128)S(1)}, u32[]{:S(2)}, u32[]{:S(2)}) collective-permute-start(s32[1,512]{1,0:T(1,128)S(1)} %bitcast.41), channel_id=1, source_target_pairs={{0,4},{1,5},{2,6},{3,7},{4,0},{5,1},{6,2},{7,3},{8,12},{9,13},{10,... | collective-permute-start | bytes 6152 | tf_op jit(solution)/shard_map/ppermute | solution.py:332
  196.2 15.8 %collective-permute-done.20 = s32[1,512]{1,0:T(1,128)S(1)} collective-permute-done((s32[1,512]{1,0:T(1,128)S(1)}, s32[1,512]{1,0:T(1,128)S(1)}, u32[]{:S(2)}, u32[]{:S(2)}) %collective-permute-start.20) | collective-permute-done | bytes 2080 | tf_op jit(solution)/shard_map/ppermute | solution.py:332
  212.0 3.4 %collective-permute-start.21 = (s32[1,512]{1,0:T(1,128)S(1)}, s32[1,512]{1,0:T(1,128)S(1)}, u32[]{:S(2)}, u32[]{:S(2)}) collective-permute-start(s32[1,512]{1,0:T(1,128)S(1)} %bitcast.42), channel_id=1, source_target_pairs={{0,8},{1,9},{2,10},{3,11},{4,12},{5,13},{6,14},{7,15},{8,0},{9,1},... | collective-permute-start | bytes 6152 | tf_op jit(solution)/shard_map/ppermute | solution.py:332
  215.4 1.6 collective-permute-done.21
  216.9 4.8 %collective-permute-start.22 = (s32[1,512]{1,0:T(1,128)S(1)}, s32[1,512]{1,0:T(1,128)}, u32[]{:S(2)}, u32[]{:S(2)}) collective-permute-start(s32[1,512]{1,0:T(1,128)S(1)} %bitcast.43), channel_id=1, source_target_pairs={{0,12},{1,13},{2,14},{3,15},{4,8},{5,9},{6,10},{7,11},{8,4},{9,5},... | collective-permute-start | bytes 6152 | tf_op jit(solution)/shard_map/ppermute | solution.py:332
  221.7 1.7 collective-permute-done.22
  223.4 1.7 collective-permute-start.29
  225.1 1.9 collective-permute-start.33
  227.0 1.8 collective-permute-start.34
  230.6 1.3 copy-done.18
  233.0 7.1 %attend.1 = (bf16[384,384]{1,0:T(8,128)(2,1)S(1)}, bf16[384,384]{1,0:T(8,128)(2,1)S(1)}) custom-call(s32[8]{0:T(128)S(1)} %stack.107.sc_ref, bf16[2,384,384]{2,1,0:T(8,128)(2,1)S(1)} %copy-done.20, bf16[2,384,768]{2,1,0:T(8,128)(2,1)} %get-tuple-element.10.kv0, bf16[2,384,768]{2,1,0:T(8,128)(2,1)S(1)} %copy-done.18, s32[4,512]{1,0:T(4,128)S(1)} %pad_add_fusion.flags_ref), custom_call_target="tpu_custom_call" | custom-call | flops 1811939328 | bytes 2359296 | tf_op jit(solution)/shard_map/attend/pallas_call | solution.py:218
  241.1 5.4 %collective-permute-start.25 = (bf16[384,384]{1,0:T(8,128)(2,1)S(1)}, bf16[384,384]{1,0:T(8,128)(2,1)}, u32[]{:S(2)}, u32[]{:S(2)}) collective-permute-start(bf16[384,384]{1,0:T(8,128)(2,1)S(1)} %get-tuple-element.12), channel_id=1, source_target_pairs={{0,8},{1,12},{2,10},{3,14},{4,9},{5,13},{6,11},{7,15},{8,0},{9,4},... | collective-permute-start | bytes 884744 | tf_op jit(solution)/shard_map/ppermute | solution.py:332
  246.5 1.6 collective-permute-done.23.pn
  248.1 11.0 %collective-permute-done.25.f0 = bf16[384,384]{1,0:T(8,128)(2,1)} collective-permute-done((bf16[384,384]{1,0:T(8,128)(2,1)S(1)}, bf16[384,384]{1,0:T(8,128)(2,1)}, u32[]{:S(2)}, u32[]{:S(2)}) %collective-permute-start.25) | collective-permute-done | bytes 294944 | tf_op jit(solution)/shard_map/ppermute | solution.py:332
  259.2 1.8 collective-permute-done.26.f1
  262.0 4.6 %project.3 = bf16[384,768]{1,0:T(8,128)(2,1)} custom-call(s32[7]{0:T(128)S(1)} %stack.119.sc_ref, bf16[384,384]{1,0:T(8,128)(2,1)S(1)} %copy-done.9, bf16[384,384]{1,0:T(8,128)(2,1)} %collective-permute-done.23.pn, bf16[384,384]{1,0:T(8,128)(2,1)} %collective-permute-done.24.bp, bf16[384,384]{1,0:T(8,128)(2,1)} %collective-permute-done.25.f0, ...), custom_call_target="tpu_custom_call" | custom-call | flops 905969664 | bytes 4718592 | tf_op jit(solution)/shard_map/project/pallas_call | solution.py:282
  266.6 1.7 collective-permute-start.35
  270.1 4.0 %project.2 = f32[384,768]{1,0:T(8,128)S(1)} custom-call(s32[7]{0:T(128)S(1)} %stack.100.sc_ref, bf16[384,384]{1,0:T(8,128)(2,1)S(1)} %copy-done.10, bf16[384,384]{1,0:T(8,128)(2,1)} %collective-permute-done.23.pn, bf16[384,384]{1,0:T(8,128)(2,1)} %collective-permute-done.24.bp, bf16[384,384]{1,0:T(8,128)(2,1)} %collective-permute-done.25.f0, ...), custom_call_target="tpu_custom_call" | custom-call | flops 905969664 | bytes 4718592 | tf_op jit(solution)/shard_map/project/pallas_call | solution.py:282
  274.1 8.3 %collective-permute-done.35 = bf16[384,768]{1,0:T(8,128)(2,1)} collective-permute-done((bf16[384,768]{1,0:T(8,128)(2,1)}, bf16[384,768]{1,0:T(8,128)(2,1)}, u32[]{:S(2)}, u32[]{:S(2)}) %collective-permute-start.35) | collective-permute-done | bytes 589856 | tf_op jit(solution)/shard_map/ppermute | solution.py:332
  282.4 2.3 add_convert_fusion
  (90 shorter events, 16.9 us)
Async XLA Ops:
  1.6 23.5 %collective-permute-start.10 = (bf16[3,3,384,128]{3,2,1,0:T(8,128)(2,1)S(1)}, bf16[3,3,384,128]{3,2,1,0:T(8,128)(2,1)}, u32[]{:S(2)}, u32[]{:S(2)}) collective-permute-start(bf16[3,3,384,128]{3,2,1,0:T(8,128)(2,1)S(1)} %get-tuple-element.14), channel_id=1, source_target_pairs={{0,5},{1,8},{2,7},{3,10},{4,1},{5,12},{6,3},{7,14},{8,0},{9,13},{1... | collective-permute-start | bytes 2654216 | tf_op jit(solution)/shard_map/ppermute | solution.py:332
  8.2 38.2 %collective-permute-start = (bf16[192,3072]{1,0:T(8,128)(2,1)}, bf16[192,3072]{1,0:T(8,128)(2,1)}, u32[]{:S(2)}, u32[]{:S(2)}) collective-permute-start(bf16[192,3072]{1,0:T(8,128)(2,1)} %norm_rows.1), channel_id=1, source_target_pairs={{0,4},{1,0},{2,6},{3,2},{4,5},{5,1},{6,7},{7,3},{8,12},{9,8},{10,1... | collective-permute-start | bytes 3538952 | tf_op jit(solution)/shard_map/ppermute | solution.py:332
  8.8 40.9 %collective-permute-start.2 = (bf16[192,3072]{1,0:T(8,128)(2,1)}, bf16[192,3072]{1,0:T(8,128)(2,1)}, u32[]{:S(2)}, u32[]{:S(2)}) collective-permute-start(bf16[192,3072]{1,0:T(8,128)(2,1)} %norm_rows.1), channel_id=1, source_target_pairs={{0,1},{1,0},{2,3},{3,2},{4,5},{5,9},{6,7},{7,11},{8,4},{9,8},{10,6... | collective-permute-start | bytes 3538952 | tf_op jit(solution)/shard_map/ppermute | solution.py:332
  9.9 55.1 %collective-permute-start.30 = (bf16[768,768]{1,0:T(8,128)(2,1)}, bf16[768,768]{1,0:T(8,128)(2,1)S(1)}, u32[]{:S(2)}, u32[]{:S(2)}) collective-permute-start(bf16[768,768]{1,0:T(8,128)(2,1)} %bitcast.30.refs_0_), channel_id=1, source_target_pairs={{0,8},{1,0},{2,10},{3,2},{4,9},{6,11},{8,4},{10,6},{12,5},{13,12},... | collective-permute-start | bytes 3538952 | tf_op jit(solution)/shard_map/ppermute | solution.py:332
  14.8 31.6 %collective-permute-start.15 = (bf16[3,3,384,128]{3,2,1,0:T(8,128)(2,1)S(1)}, bf16[3,3,384,128]{3,2,1,0:T(8,128)(2,1)}, u32[]{:S(2)}, u32[]{:S(2)}) collective-permute-start(bf16[3,3,384,128]{3,2,1,0:T(8,128)(2,1)S(1)} %get-tuple-element.13), channel_id=1, source_target_pairs={{1,12},{3,14},{5,8},{7,10},{8,5},{10,7},{12,1},{14,3},{17,28},{19,... | collective-permute-start | bytes 2654216 | tf_op jit(solution)/shard_map/ppermute | solution.py:332
  25.0 40.0 %collective-permute-start.11 = (bf16[3,3,384,128]{3,2,1,0:T(8,128)(2,1)}, bf16[3,3,384,128]{3,2,1,0:T(8,128)(2,1)}, u32[]{:S(2)}, u32[]{:S(2)}) collective-permute-start(bf16[3,3,384,128]{3,2,1,0:T(8,128)(2,1)} %collective-permute-done.10.refs_10_), channel_id=1, source_target_pairs={{0,16},{1,17},{2,18},{3,19},{4,20},{5,21},{6,22},{7,23},{8,24},{9,... | collective-permute-start | bytes 2654216 | tf_op jit(solution)/shard_map/ppermute | solution.py:332
  46.4 30.9 %collective-permute-start.3 = (bf16[192,3072]{1,0:T(8,128)(2,1)}, bf16[192,3072]{1,0:T(8,128)(2,1)}, u32[]{:S(2)}, u32[]{:S(2)}) collective-permute-start(bf16[192,3072]{1,0:T(8,128)(2,1)} %collective-permute-done.refs_0_), channel_id=1, source_target_pairs={{0,1},{1,0},{2,3},{3,2},{4,8},{5,4},{6,10},{7,6},{8,9},{9,5},{10,1... | collective-permute-start | bytes 3538952 | tf_op jit(solution)/shard_map/ppermute | solution.py:332
  46.4 19.1 %collective-permute-start.16 = (bf16[3,3,384,128]{3,2,1,0:T(8,128)(2,1)}, bf16[3,3,384,128]{3,2,1,0:T(8,128)(2,1)}, u32[]{:S(2)}, u32[]{:S(2)}) collective-permute-start(bf16[3,3,384,128]{3,2,1,0:T(8,128)(2,1)} %collective-permute-done.15.refs_16_), channel_id=1, source_target_pairs={{1,17},{3,19},{5,21},{7,23},{8,24},{10,26},{12,28},{14,30},{17,1},... | collective-permute-start | bytes 2654216 | tf_op jit(solution)/shard_map/ppermute | solution.py:332
  48.0 88.5 %copy-start.22 = (s32[1,9]{1,0:T(1,128)S(1)}, s32[1,9]{1,0:T(1,128)}, u32[]{:S(2)}) copy-start(s32[1,9]{1,0:T(1,128)} %param.20) | copy-start | bytes 112
  48.0 88.5 %copy-start.23 = (s32[1,9]{1,0:T(1,128)S(1)}, s32[1,9]{1,0:T(1,128)}, u32[]{:S(2)}) copy-start(s32[1,9]{1,0:T(1,128)} %param.19) | copy-start | bytes 112
  48.0 125.7 %copy-start.15 = (f32[128]{0:T(128)S(1)}, f32[128]{0:T(128)}, u32[]{:S(2)}) copy-start(f32[128]{0:T(128)} %param.14) | copy-start | bytes 1540
  48.0 125.7 %copy-start.16 = (f32[128]{0:T(128)S(1)}, f32[128]{0:T(128)}, u32[]{:S(2)}) copy-start(f32[128]{0:T(128)} %param.15) | copy-start | bytes 1540
  49.7 28.9 %collective-permute-start.12 = (bf16[3,3,384,128]{3,2,1,0:T(8,128)(2,1)}, bf16[3,3,384,128]{3,2,1,0:T(8,128)(2,1)S(1)}, u32[]{:S(2)}, u32[]{:S(2)}) collective-permute-start(bf16[3,3,384,128]{3,2,1,0:T(8,128)(2,1)} %collective-permute-done.10.refs_10_), channel_id=1, source_target_pairs={{0,1},{1,0},{2,3},{3,2},{4,5},{5,4},{6,7},{7,6},{8,9},{9,8},{10,11... | collective-permute-start | bytes 2654216 | tf_op jit(solution)/shard_map/ppermute | solution.py:332
  64.9 107.3 %copy-start = (bf16[768,768]{1,0:T(8,128)(2,1)}, bf16[768,768]{1,0:T(8,128)(2,1)S(1)}, u32[]{:S(2)}) copy-start(bf16[768,768]{1,0:T(8,128)(2,1)S(1)} %collective-permute-done.30.refs_4_) | copy-start | bytes 3538948
  65.0 16.1 %collective-permute-start.17 = (bf16[3,3,384,128]{3,2,1,0:T(8,128)(2,1)}, bf16[3,3,384,128]{3,2,1,0:T(8,128)(2,1)S(1)}, u32[]{:S(2)}, u32[]{:S(2)}) collective-permute-start(bf16[3,3,384,128]{3,2,1,0:T(8,128)(2,1)} %collective-permute-done.15.refs_16_), channel_id=1, source_target_pairs={{0,1},{1,0},{2,3},{3,2},{4,5},{5,4},{6,7},{7,6},{8,9},{9,8},{10,11... | collective-permute-start | bytes 2654216 | tf_op jit(solution)/shard_map/ppermute | solution.py:332
  65.0 19.7 %collective-permute-start.14 = (bf16[3,3,768,128]{3,2,1,0:T(8,128)(2,1)S(1)}, bf16[3,3,768,128]{3,2,1,0:T(8,128)(2,1)S(1)}, u32[]{:S(2)}, u32[]{:S(2)}) collective-permute-start(bf16[3,3,768,128]{3,2,1,0:T(8,128)(2,1)S(1)} %dynamic-slice_bitcast_fusion.refs_14_), channel_id=1, source_target_pairs={{0,1},{1,0},{2,3},{3,2},{4,5},{5,4},{6,7},{7,6},{8,9},{9,8},{10,11... | collective-permute-start | bytes 5308424 | tf_op jit(solution)/shard_map/ppermute | solution.py:332
  65.5 55.4 %collective-permute-start.4 = (bf16[192,3072]{1,0:T(8,128)(2,1)}, bf16[192,3072]{1,0:T(8,128)(2,1)}, u32[]{:S(2)}, u32[]{:S(2)}) collective-permute-start(bf16[192,3072]{1,0:T(8,128)(2,1)} %collective-permute-done.2.refs_2_), channel_id=1, source_target_pairs={{0,1},{2,3},{4,0},{5,4},{6,2},{7,6},{8,9},{9,13},{10,11},{11,15},{... | collective-permute-start | bytes 3538952 | tf_op jit(solution)/shard_map/ppermute | solution.py:332
  77.3 46.8 %collective-permute-start.5 = (bf16[192,3072]{1,0:T(8,128)(2,1)}, bf16[192,3072]{1,0:T(8,128)(2,1)}, u32[]{:S(2)}, u32[]{:S(2)}) collective-permute-start(bf16[192,3072]{1,0:T(8,128)(2,1)} %collective-permute-done.3.refs_3_), channel_id=1, source_target_pairs={{1,0},{3,2},{4,5},{5,1},{6,7},{7,3},{8,12},{9,8},{10,14},{11,10},{... | collective-permute-start | bytes 3538952 | tf_op jit(solution)/shard_map/ppermute | solution.py:332
  79.5 46.2 %collective-permute-start.1 = (bf16[192,3072]{1,0:T(8,128)(2,1)}, bf16[192,3072]{1,0:T(8,128)(2,1)S(1)}, u32[]{:S(2)}, u32[]{:S(2)}) collective-permute-start(bf16[192,3072]{1,0:T(8,128)(2,1)} %collective-permute-done.refs_0_), channel_id=1, source_target_pairs={{0,2},{1,3},{2,0},{3,1},{4,6},{5,7},{6,4},{7,5},{8,10},{9,11},{10,... | collective-permute-start | bytes 3538952 | tf_op jit(solution)/shard_map/ppermute | solution.py:332
  82.0 53.4 %collective-permute-start.6 = (bf16[192,3072]{1,0:T(8,128)(2,1)}, bf16[192,3072]{1,0:T(8,128)(2,1)S(1)}, u32[]{:S(2)}, u32[]{:S(2)}) collective-permute-start(bf16[192,3072]{1,0:T(8,128)(2,1)} %collective-permute-done.2.refs_2_), channel_id=1, source_target_pairs={{0,1},{1,0},{2,3},{3,2},{4,6},{6,4},{9,11},{11,9},{12,13},{13,12},... | collective-permute-start | bytes 3538952 | tf_op jit(solution)/shard_map/ppermute | solution.py:332
  84.7 1.3 copy-start.2
  86.0 87.6 %collective-permute-start.7 = (bf16[192,3072]{1,0:T(8,128)(2,1)}, bf16[192,3072]{1,0:T(8,128)(2,1)}, u32[]{:S(2)}, u32[]{:S(2)}) collective-permute-start(bf16[192,3072]{1,0:T(8,128)(2,1)} %collective-permute-done.3.refs_3_), channel_id=1, source_target_pairs={{0,1},{1,0},{2,3},{3,2},{5,7},{7,5},{8,10},{10,8},{12,13},{13,12},... | collective-permute-start | bytes 3538952 | tf_op jit(solution)/shard_map/ppermute | solution.py:332
  120.9 52.8 %collective-permute-start.8 = (bf16[192,3072]{1,0:T(8,128)(2,1)}, bf16[192,3072]{1,0:T(8,128)(2,1)}, u32[]{:S(2)}, u32[]{:S(2)}) collective-permute-start(bf16[192,3072]{1,0:T(8,128)(2,1)} %collective-permute-done.4.refs_4_), channel_id=1, source_target_pairs={{0,2},{2,0},{4,5},{5,4},{6,7},{7,6},{8,9},{9,8},{10,11},{11,10},{1... | collective-permute-start | bytes 3538952 | tf_op jit(solution)/shard_map/ppermute | solution.py:332
  124.1 49.6 %collective-permute-start.9 = (bf16[192,3072]{1,0:T(8,128)(2,1)}, bf16[192,3072]{1,0:T(8,128)(2,1)}, u32[]{:S(2)}, u32[]{:S(2)}) collective-permute-start(bf16[192,3072]{1,0:T(8,128)(2,1)} %collective-permute-done.5.refs_5_), channel_id=1, source_target_pairs={{1,3},{3,1},{4,5},{5,4},{6,7},{7,6},{8,9},{9,8},{10,11},{11,10},{1... | collective-permute-start | bytes 3538952 | tf_op jit(solution)/shard_map/ppermute | solution.py:332
  126.8 10.9 %collective-permute-start.13 = (bf16[3,3,384,128]{3,2,1,0:T(8,128)(2,1)}, bf16[3,3,384,128]{3,2,1,0:T(8,128)(2,1)}, u32[]{:S(2)}, u32[]{:S(2)}) collective-permute-start(bf16[3,3,384,128]{3,2,1,0:T(8,128)(2,1)} %collective-permute-done.11.refs_11_), channel_id=1, source_target_pairs={{0,1},{1,0},{2,3},{3,2},{4,5},{5,4},{6,7},{7,6},{8,9},{9,8},{10,11... | collective-permute-start | bytes 2654216 | tf_op jit(solution)/shard_map/ppermute | solution.py:332
  136.4 35.9 %collective-permute-start.18 = (bf16[3,3,384,128]{3,2,1,0:T(8,128)(2,1)}, bf16[3,3,384,128]{3,2,1,0:T(8,128)(2,1)}, u32[]{:S(2)}, u32[]{:S(2)}) collective-permute-start(bf16[3,3,384,128]{3,2,1,0:T(8,128)(2,1)} %collective-permute-done.16.refs_17_), channel_id=1, source_target_pairs={{0,1},{1,0},{2,3},{3,2},{4,5},{5,4},{6,7},{7,6},{8,9},{9,8},{10,11... | collective-permute-start | bytes 2654216 | tf_op jit(solution)/shard_map/ppermute | solution.py:332
  137.7 85.7 %collective-permute-start.28 = (bf16[768,768]{1,0:T(8,128)(2,1)}, bf16[768,768]{1,0:T(8,128)(2,1)}, u32[]{:S(2)}, u32[]{:S(2)}) collective-permute-start(bf16[768,768]{1,0:T(8,128)(2,1)} %bitcast.30.refs_0_), channel_id=1, source_target_pairs={{0,4},{1,0},{2,6},{3,2},{4,1},{6,3},{8,12},{9,8},{10,14},{11,10},{... | collective-permute-start | bytes 3538952 | tf_op jit(solution)/shard_map/ppermute | solution.py:332
  172.2 52.8 %collective-permute-start.32 = (bf16[768,768]{1,0:T(8,128)(2,1)}, bf16[768,768]{1,0:T(8,128)(2,1)S(1)}, u32[]{:S(2)}, u32[]{:S(2)}) collective-permute-start(bf16[768,768]{1,0:T(8,128)(2,1)} %copy-done), channel_id=1, source_target_pairs={{4,0},{5,1},{6,2},{7,3},{8,12},{9,13},{10,14},{11,15},{20,16},{21,... | collective-permute-start | bytes 3538952 | tf_op jit(solution)/shard_map/ppermute | solution.py:332
  173.6 53.5 %collective-permute-start.31 = (bf16[768,768]{1,0:T(8,128)(2,1)}, bf16[768,768]{1,0:T(8,128)(2,1)}, u32[]{:S(2)}, u32[]{:S(2)}) collective-permute-start(bf16[768,768]{1,0:T(8,128)(2,1)} %copy-done), channel_id=1, source_target_pairs={{0,1},{1,0},{2,3},{3,2},{4,20},{5,21},{6,22},{7,23},{8,24},{9,25},... | collective-permute-start | bytes 3538952 | tf_op jit(solution)/shard_map/ppermute | solution.py:332
  173.7 1.5 copy-start.3
  175.2 1.3 copy-start.5
  176.4 1.3 copy-start.7
  180.0 12.5 %copy-start.21 = (s32[384]{0:T(512)S(1)}, s32[384]{0:T(512)}, u32[]{:S(2)}) copy-start(s32[384]{0:T(512)} %param.21) | copy-start | bytes 4612
  192.2 37.4 %collective-permute-start.19 = (bf16[2,384,768]{2,1,0:T(8,128)(2,1)}, bf16[2,384,768]{2,1,0:T(8,128)(2,1)S(1)}, u32[]{:S(2)}, u32[]{:S(2)}) collective-permute-start(bf16[2,384,768]{2,1,0:T(8,128)(2,1)} %get-tuple-element.10.kv0), channel_id=1, source_target_pairs={{0,1},{1,0},{2,3},{3,2},{4,5},{5,4},{6,7},{7,6},{8,9},{9,8},{10,11... | collective-permute-start | bytes 3538952 | tf_op jit(solution)/shard_map/ppermute | solution.py:332
  192.6 19.4 %collective-permute-start.20 = (s32[1,512]{1,0:T(1,128)S(1)}, s32[1,512]{1,0:T(1,128)S(1)}, u32[]{:S(2)}, u32[]{:S(2)}) collective-permute-start(s32[1,512]{1,0:T(1,128)S(1)} %bitcast.41), channel_id=1, source_target_pairs={{0,4},{1,5},{2,6},{3,7},{4,0},{5,1},{6,2},{7,3},{8,12},{9,13},{10,... | collective-permute-start | bytes 6152 | tf_op jit(solution)/shard_map/ppermute | solution.py:332
  212.0 5.0 %collective-permute-start.21 = (s32[1,512]{1,0:T(1,128)S(1)}, s32[1,512]{1,0:T(1,128)S(1)}, u32[]{:S(2)}, u32[]{:S(2)}) collective-permute-start(s32[1,512]{1,0:T(1,128)S(1)} %bitcast.42), channel_id=1, source_target_pairs={{0,8},{1,9},{2,10},{3,11},{4,12},{5,13},{6,14},{7,15},{8,0},{9,1},... | collective-permute-start | bytes 6152 | tf_op jit(solution)/shard_map/ppermute | solution.py:332
  216.9 6.4 %collective-permute-start.22 = (s32[1,512]{1,0:T(1,128)S(1)}, s32[1,512]{1,0:T(1,128)}, u32[]{:S(2)}, u32[]{:S(2)}) collective-permute-start(s32[1,512]{1,0:T(1,128)S(1)} %bitcast.43), channel_id=1, source_target_pairs={{0,12},{1,13},{2,14},{3,15},{4,8},{5,9},{6,10},{7,11},{8,4},{9,5},... | collective-permute-start | bytes 6152 | tf_op jit(solution)/shard_map/ppermute | solution.py:332
  223.4 17.8 %collective-permute-start.27 = (bf16[768,768]{1,0:T(8,128)(2,1)}, bf16[768,768]{1,0:T(8,128)(2,1)S(1)}, u32[]{:S(2)}, u32[]{:S(2)}) collective-permute-start(bf16[768,768]{1,0:T(8,128)(2,1)} %bitcast.30.refs_0_), channel_id=1, source_target_pairs={{0,1},{1,0},{2,3},{3,2},{4,5},{5,4},{6,7},{7,6},{8,9},{9,8},{10,11... | collective-permute-start | bytes 3538952 | tf_op jit(solution)/shard_map/ppermute | solution.py:332
  223.4 35.8 %collective-permute-start.29 = (bf16[768,768]{1,0:T(8,128)(2,1)}, bf16[768,768]{1,0:T(8,128)(2,1)}, u32[]{:S(2)}, u32[]{:S(2)}) collective-permute-start(bf16[768,768]{1,0:T(8,128)(2,1)} %collective-permute-done.28.refs_2_), channel_id=1, source_target_pairs={{1,17},{3,19},{4,20},{6,22},{9,25},{11,27},{12,28},{14,30},{17,1},... | collective-permute-start | bytes 3538952 | tf_op jit(solution)/shard_map/ppermute | solution.py:332
  225.1 34.1 %collective-permute-start.33 = (bf16[768,768]{1,0:T(8,128)(2,1)S(1)}, bf16[768,768]{1,0:T(8,128)(2,1)}, u32[]{:S(2)}, u32[]{:S(2)}) collective-permute-start(bf16[768,768]{1,0:T(8,128)(2,1)S(1)} %collective-permute-done.32.refs_6_.refs_8_), channel_id=1, source_target_pairs={{0,16},{2,18},{4,5},{5,4},{6,7},{7,6},{8,9},{9,8},{10,11},{11,10},... | collective-permute-start | bytes 3538952 | tf_op jit(solution)/shard_map/ppermute | solution.py:332
  227.0 32.2 %collective-permute-start.34 = (bf16[768,768]{1,0:T(8,128)(2,1)}, bf16[768,768]{1,0:T(8,128)(2,1)}, u32[]{:S(2)}, u32[]{:S(2)}) collective-permute-start(bf16[768,768]{1,0:T(8,128)(2,1)} %collective-permute-done.31.refs_5_), channel_id=1, source_target_pairs={{5,1},{7,3},{8,12},{10,14},{21,17},{23,19},{24,28},{26,30}} | collective-permute-start | bytes 3538952 | tf_op jit(solution)/shard_map/ppermute | solution.py:332
  230.6 1.3 copy-start.18
  233.0 28.1 %copy-start.1 = (bf16[768,768]{1,0:T(8,128)(2,1)S(1)}, bf16[768,768]{1,0:T(8,128)(2,1)}, u32[]{:S(2)}) copy-start(bf16[768,768]{1,0:T(8,128)(2,1)} %copy-done) | copy-start | bytes 3538948
  240.1 8.0 %collective-permute-start.23 = (bf16[384,384]{1,0:T(8,128)(2,1)S(1)}, bf16[384,384]{1,0:T(8,128)(2,1)}, u32[]{:S(2)}, u32[]{:S(2)}) collective-permute-start(bf16[384,384]{1,0:T(8,128)(2,1)S(1)} %get-tuple-element.11.an), channel_id=1, source_target_pairs={{0,1},{1,5},{2,3},{3,7},{4,0},{5,4},{6,2},{7,6},{8,9},{9,13},{10,1... | collective-permute-start | bytes 884744 | tf_op jit(solution)/shard_map/ppermute | solution.py:332
  241.1 18.0 %collective-permute-start.25 = (bf16[384,384]{1,0:T(8,128)(2,1)S(1)}, bf16[384,384]{1,0:T(8,128)(2,1)}, u32[]{:S(2)}, u32[]{:S(2)}) collective-permute-start(bf16[384,384]{1,0:T(8,128)(2,1)S(1)} %get-tuple-element.12), channel_id=1, source_target_pairs={{0,8},{1,12},{2,10},{3,14},{4,9},{5,13},{6,11},{7,15},{8,0},{9,4},... | collective-permute-start | bytes 884744 | tf_op jit(solution)/shard_map/ppermute | solution.py:332
  248.1 11.1 %collective-permute-start.24 = (bf16[384,384]{1,0:T(8,128)(2,1)}, bf16[384,384]{1,0:T(8,128)(2,1)}, u32[]{:S(2)}, u32[]{:S(2)}) collective-permute-start(bf16[384,384]{1,0:T(8,128)(2,1)} %collective-permute-done.23.pn), channel_id=1, source_target_pairs={{0,1},{1,0},{2,3},{3,2},{4,5},{5,4},{6,7},{7,6},{8,9},{9,8},{10,11... | collective-permute-start | bytes 884744 | tf_op jit(solution)/shard_map/ppermute | solution.py:332
  259.1 1.9 collective-permute-start.26
  266.6 15.8 %collective-permute-start.35 = (bf16[384,768]{1,0:T(8,128)(2,1)}, bf16[384,768]{1,0:T(8,128)(2,1)}, u32[]{:S(2)}, u32[]{:S(2)}) collective-permute-start(bf16[384,768]{1,0:T(8,128)(2,1)} %project.3), channel_id=1, source_target_pairs={{0,2},{1,3},{2,0},{3,1},{4,6},{5,7},{6,4},{7,5},{8,10},{9,11},{10,... | collective-permute-start | bytes 1769480 | tf_op jit(solution)/shard_map/ppermute | solution.py:332
  (12 other events, 12.0 us)

commit v3 on v2

--- a/solution.py
+++ b/solution.py
@@ -26,7 +26,7 @@
 
 def norm_rows(latents, mod_shift, mod_scale, half):
     rows, width = latents.shape
-    steps = 4
+    steps = 2
     block = rows // 2 // steps
     vector = pl.BlockSpec((1, width), lambda i, half_ref: (0, 0))
     return pl.pallas_call(
@@ -164,7 +164,7 @@
             pltpu.SemaphoreType.DMA((8,)),
             pltpu.SemaphoreType.DMA((2,)),
         ],
-        compiler_params=pltpu.CompilerParams(vmem_limit_bytes=28 << 20),
+        compiler_params=pltpu.CompilerParams(vmem_limit_bytes=24 << 20),
         cost_estimate=pl.CostEstimate(
             flops=12 * rows * width * out, bytes_accessed=width * 3 * out * 2, transcendentals=0
         ),
@@ -172,17 +172,16 @@
     )(scalars, *tokens, *weights, query_gain[None], key_gain[None])
 
 
-def attend_kernel(sc_ref, q_ref, kv0, kv1, flags_ref, near_ref, far_ref):
+def attend_kernel(sc_ref, q_ref, kv0, kv1, *refs):
     _, rows, width = q_ref.shape
     hd = 128
     heads = width // hd
     factor = math.log2(math.e) / math.sqrt(hd)
-    flags = flags_ref[...]
-    place = lax.broadcasted_iota(jnp.int32, flags.shape, 0)
+    flags, (near_ref, far_ref) = [r[...] for r in refs[:-2]], refs[-2:]
     segments = ((kv0, 0), (kv0, 1), (kv1, 0), (kv1, 1))
 
     def row(d):
-        return jnp.sum(jnp.where(place == d, flags, 0), axis=0, keepdims=True)
+        return functools.reduce(lambda a, i: jnp.where(d == i, flags[i], a), range(1, len(flags)), flags[0])
 
     rows_of = [row(sc_ref[4 + s]) for s in range(4)]
     biases = []
@@ -218,14 +217,14 @@
     return pl.pallas_call(
         attend_kernel,
         out_shape=(shape, shape),
-        in_specs=[smem] + [vmem] * 4,
+        in_specs=[smem] + [vmem] * (3 + len(flags)),
         out_specs=(vmem, vmem),
-        compiler_params=pltpu.CompilerParams(vmem_limit_bytes=24 << 20),
+        compiler_params=pltpu.CompilerParams(vmem_limit_bytes=16 << 20),
         cost_estimate=pl.CostEstimate(
             flops=8 * rows * keys * width, bytes_accessed=8 * rows * width * 2, transcendentals=2 * rows * keys * width // 128
         ),
         name="attend",
-    )(scalars, queries, kv, kv_other, flags)
+    )(scalars, queries, kv, kv_other, *flags)
 
 
 def project_kernel(sc_ref, an, pn, bp, f0, f1, *refs):
@@ -282,7 +281,7 @@
     return pl.pallas_call(
         project_kernel,
         out_shape=jax.ShapeDtypeStruct((rows, width), dtype),
-        in_specs=[smem] + [anywhere] * (len(pieces) + len(weights)),
+        in_specs=[smem, vmem] + [anywhere] * (len(pieces) - 1 + len(weights)),
         out_specs=vmem,
         scratch_shapes=[
             pltpu.VMEM((rows, 2 * depth), BF16),
@@ -290,7 +289,7 @@
             pltpu.SemaphoreType.DMA((4,)),
             pltpu.SemaphoreType.DMA((2,)),
         ],
-        compiler_params=pltpu.CompilerParams(vmem_limit_bytes=16 << 20),
+        compiler_params=pltpu.CompilerParams(vmem_limit_bytes=10 << 20),
         cost_estimate=pl.CostEstimate(
             flops=4 * rows * depth * width, bytes_accessed=4 * depth * width * 2, transcendentals=0
         ),
@@ -404,10 +403,7 @@
     tile_ids = jnp.arange(nz, dtype=jnp.int32)
     hits = jnp.any((block_list[0][:, None] == tile_ids[None]) & (block_live[0][:, None] > 0), axis=0)
     flags = jnp.concatenate([key_valid, jnp.pad(hits.astype(jnp.int32), (0, 128 - nz))])[None]
-    flags = jnp.concatenate(
-        [flags]
-        + [move(flags, lambda yy, zz, xx, cc, d=d: (yy, zz ^ d, xx, cc)) for d in range(1, nz)]
-    )
+    flags = [flags] + [move(flags, lambda yy, zz, xx, cc, d=d: (yy, zz ^ d, xx, cc)) for d in range(1, nz)]
 
     own_w = lax.dynamic_slice(w_t, (0, parity * heads, 0, 0), (3, heads, depth, hd))
 

time: 286 us -> 285 us (level)
    unnamed x48 -> x52, local copies, waits for them, and re-layouts: 18.5 us -> 19.2 us
where the time goes in v3:
time: 285 us; the launch traced here: 284 us
  starting transfers between devices  134 us (47%)
  waiting for transfers between devices  94.2 us (33%)
  Pallas kernels  29.6 us (10%)
  local copies, waits for them, and re-layouts  23.5 us (8%)
    ppermute x36, starting transfers between devices, move(): return lax.ppermute(array, AXES, pairs)  134 us
    ppermute x36, waiting for transfers between devices, move(): return lax.ppermute(array, AXES, pairs)  94.2 us
    unnamed x52, local copies, waits for them, and re-layouts  19.2 us
    pallas_call x1, Pallas kernels, qkv_tiles(): pl.pallas_call(functools.partial(qkv_kernel, counts), out_shape=(jax.Shap...  11.3 us
    pallas_call x2, Pallas kernels, project(): pl.pallas_call(project_kernel, out_shape=jax.ShapeDtypeStruct((rows, widt...  8.59 us
    pallas_call x1, Pallas kernels, attend(): pl.pallas_call(attend_kernel, out_shape=(shape, shape), in_specs=[smem] +...  6.85 us
  transfers between devices with their start and end apart: 36, of which 11 were waited for; matrix products, arithmetic and copies ran while one was open for 1% of the time, Pallas kernels for 9%

profile of v3, /device:TPU:0, one launch (start us, length us, event | category | flops | bytes accessed | tf_op | source)
XLA Modules:
  0.0 284.4 jit_solution(859839187238227369)
XLA Ops:
  0.0 1.5 dynamic-slice_bitcast_fusion.1
  1.6 2.6 collective-permute-start.10
  4.1 2.8 norm_rows.1
  8.6 4.9 %collective-permute-start.30 = (bf16[768,768]{1,0:T(8,128)(2,1)}, bf16[768,768]{1,0:T(8,128)(2,1)S(1)}, u32[]{:S(2)}, u32[]{:S(2)}) collective-permute-start(bf16[768,768]{1,0:T(8,128)(2,1)} %bitcast.30.refs_0_), channel_id=1, source_target_pairs={{0,8},{1,0},{2,10},{3,2},{4,9},{6,11},{8,4},{10,6},{12,5},{13,12},... | collective-permute-start | bytes 3538952 | tf_op jit(solution)/shard_map/ppermute | solution.py:331
  13.6 1.6 collective-permute-start.15
  15.1 9.9 %collective-permute-done.10.refs_10_ = bf16[3,3,384,128]{3,2,1,0:T(8,128)(2,1)} collective-permute-done((bf16[3,3,384,128]{3,2,1,0:T(8,128)(2,1)S(1)}, bf16[3,3,384,128]{3,2,1,0:T(8,128)(2,1)}, u32[]{:S(2)}, u32[]{:S(2)}) %collective-permute-start.10) | collective-permute-done | bytes 884768 | tf_op jit(solution)/shard_map/ppermute | solution.py:331
  25.0 12.9 %collective-permute-start.11 = (bf16[3,3,384,128]{3,2,1,0:T(8,128)(2,1)}, bf16[3,3,384,128]{3,2,1,0:T(8,128)(2,1)}, u32[]{:S(2)}, u32[]{:S(2)}) collective-permute-start(bf16[3,3,384,128]{3,2,1,0:T(8,128)(2,1)} %collective-permute-done.10.refs_10_), channel_id=1, source_target_pairs={{0,16},{1,17},{2,18},{3,19},{4,20},{5,21},{6,22},{7,23},{8,24},{9,... | collective-permute-start | bytes 2654216 | tf_op jit(solution)/shard_map/ppermute | solution.py:331
  37.9 8.5 %collective-permute-done.refs_0_ = bf16[192,3072]{1,0:T(8,128)(2,1)} collective-permute-done((bf16[192,3072]{1,0:T(8,128)(2,1)}, bf16[192,3072]{1,0:T(8,128)(2,1)}, u32[]{:S(2)}, u32[]{:S(2)}) %collective-permute-start) | collective-permute-done | bytes 1179680 | tf_op jit(solution)/shard_map/ppermute | solution.py:331
  46.4 1.6 collective-permute-start.16
  48.0 1.6 dynamic-slice_bitcast_fusion.refs_14_
  49.6 15.3 %collective-permute-start.12 = (bf16[3,3,384,128]{3,2,1,0:T(8,128)(2,1)}, bf16[3,3,384,128]{3,2,1,0:T(8,128)(2,1)S(1)}, u32[]{:S(2)}, u32[]{:S(2)}) collective-permute-start(bf16[3,3,384,128]{3,2,1,0:T(8,128)(2,1)} %collective-permute-done.10.refs_10_), channel_id=1, source_target_pairs={{0,1},{1,0},{2,3},{3,2},{4,5},{5,4},{6,7},{7,6},{8,9},{9,8},{10,11... | collective-permute-start | bytes 2654216 | tf_op jit(solution)/shard_map/ppermute | solution.py:331
  65.5 11.8 %collective-permute-start.4 = (bf16[192,3072]{1,0:T(8,128)(2,1)}, bf16[192,3072]{1,0:T(8,128)(2,1)}, u32[]{:S(2)}, u32[]{:S(2)}) collective-permute-start(bf16[192,3072]{1,0:T(8,128)(2,1)} %collective-permute-done.2.refs_2_), channel_id=1, source_target_pairs={{0,1},{2,3},{4,0},{5,4},{6,2},{7,6},{8,9},{9,13},{10,11},{11,15},{... | collective-permute-start | bytes 3538952 | tf_op jit(solution)/shard_map/ppermute | solution.py:331
  77.3 1.3 collective-permute-start.5
  79.5 1.5 collective-permute-start.1
  82.0 2.7 collective-permute-start.6
  84.7 1.2 copy-done.2
  86.0 1.9 collective-permute-start.7
  87.9 33.0 %collective-permute-done.4.refs_4_ = bf16[192,3072]{1,0:T(8,128)(2,1)} collective-permute-done((bf16[192,3072]{1,0:T(8,128)(2,1)}, bf16[192,3072]{1,0:T(8,128)(2,1)}, u32[]{:S(2)}, u32[]{:S(2)}) %collective-permute-start.4) | collective-permute-done | bytes 1179680 | tf_op jit(solution)/shard_map/ppermute | solution.py:331
  120.9 3.2 %collective-permute-start.8 = (bf16[192,3072]{1,0:T(8,128)(2,1)}, bf16[192,3072]{1,0:T(8,128)(2,1)}, u32[]{:S(2)}, u32[]{:S(2)}) collective-permute-start(bf16[192,3072]{1,0:T(8,128)(2,1)} %collective-permute-done.4.refs_4_), channel_id=1, source_target_pairs={{0,2},{2,0},{4,5},{5,4},{6,7},{7,6},{8,9},{9,8},{10,11},{11,10},{1... | collective-permute-start | bytes 3538952 | tf_op jit(solution)/shard_map/ppermute | solution.py:331
  124.1 1.7 collective-permute-start.9
  126.9 8.5 %collective-permute-start.13 = (bf16[3,3,384,128]{3,2,1,0:T(8,128)(2,1)}, bf16[3,3,384,128]{3,2,1,0:T(8,128)(2,1)}, u32[]{:S(2)}, u32[]{:S(2)}) collective-permute-start(bf16[3,3,384,128]{3,2,1,0:T(8,128)(2,1)} %collective-permute-done.11.refs_11_), channel_id=1, source_target_pairs={{0,1},{1,0},{2,3},{3,2},{4,5},{5,4},{6,7},{7,6},{8,9},{9,8},{10,11... | collective-permute-start | bytes 2654216 | tf_op jit(solution)/shard_map/ppermute | solution.py:331
  137.7 34.5 %collective-permute-start.28 = (bf16[768,768]{1,0:T(8,128)(2,1)}, bf16[768,768]{1,0:T(8,128)(2,1)}, u32[]{:S(2)}, u32[]{:S(2)}) collective-permute-start(bf16[768,768]{1,0:T(8,128)(2,1)} %bitcast.30.refs_0_), channel_id=1, source_target_pairs={{0,4},{1,0},{2,6},{3,2},{4,1},{6,3},{8,12},{9,8},{10,14},{11,10},{... | collective-permute-start | bytes 3538952 | tf_op jit(solution)/shard_map/ppermute | solution.py:331
  172.2 1.3 collective-permute-start.32
  173.7 1.5 copy-done.3
  175.1 1.3 copy-done.5
  176.4 1.3 copy-done.7
  177.7 1.2 copy-done.12
  180.0 11.3 %qkv_tiles.1 = (bf16[2,384,384]{2,1,0:T(8,128)(2,1)S(1)}, bf16[2,384,768]{2,1,0:T(8,128)(2,1)}) custom-call(s32[9]{0:T(128)S(1)} %stack.116.sc_ref, bf16[192,3072]{1,0:T(8,128)(2,1)} %collective-permute-done.refs_0_, bf16[192,3072]{1,0:T(8,128)(2,1)S(1)} %copy-done.5, bf16[192,3072]{1,0:T(8,128)(2,1)} %collective-permute-done.2.refs_2_, ...), custom_call_target="tpu_custom_call" | custom-call | flops 5435817984 | bytes 7077888 | tf_op jit(solution)/shard_map/qkv_tiles/pallas_call | solution.py:150
  192.6 3.6 %collective-permute-start.20 = (s32[1,512]{1,0:T(1,128)S(1)}, s32[1,512]{1,0:T(1,128)S(1)}, u32[]{:S(2)}, u32[]{:S(2)}) collective-permute-start(s32[1,512]{1,0:T(1,128)S(1)} %bitcast.37), channel_id=1, source_target_pairs={{0,4},{1,5},{2,6},{3,7},{4,0},{5,1},{6,2},{7,3},{8,12},{9,13},{10,... | collective-permute-start | bytes 6152 | tf_op jit(solution)/shard_map/ppermute | solution.py:331
  196.1 15.8 %collective-permute-done.20.refs_1_ = s32[1,512]{1,0:T(1,128)S(1)} collective-permute-done((s32[1,512]{1,0:T(1,128)S(1)}, s32[1,512]{1,0:T(1,128)S(1)}, u32[]{:S(2)}, u32[]{:S(2)}) %collective-permute-start.20) | collective-permute-done | bytes 2080 | tf_op jit(solution)/shard_map/ppermute | solution.py:331
  211.9 3.4 %collective-permute-start.21 = (s32[1,512]{1,0:T(1,128)S(1)}, s32[1,512]{1,0:T(1,128)S(1)}, u32[]{:S(2)}, u32[]{:S(2)}) collective-permute-start(s32[1,512]{1,0:T(1,128)S(1)} %bitcast.38), channel_id=1, source_target_pairs={{0,8},{1,9},{2,10},{3,11},{4,12},{5,13},{6,14},{7,15},{8,0},{9,1},... | collective-permute-start | bytes 6152 | tf_op jit(solution)/shard_map/ppermute | solution.py:331
  215.4 1.6 collective-permute-done.21.refs_2_
  216.9 4.8 %collective-permute-start.22 = (s32[1,512]{1,0:T(1,128)S(1)}, s32[1,512]{1,0:T(1,128)S(1)}, u32[]{:S(2)}, u32[]{:S(2)}) collective-permute-start(s32[1,512]{1,0:T(1,128)S(1)} %bitcast.39), channel_id=1, source_target_pairs={{0,12},{1,13},{2,14},{3,15},{4,8},{5,9},{6,10},{7,11},{8,4},{9,5},... | collective-permute-start | bytes 6152 | tf_op jit(solution)/shard_map/ppermute | solution.py:331
  221.7 1.6 collective-permute-done.22.refs_3_
  223.2 1.7 collective-permute-start.29
  225.0 1.9 collective-permute-start.33
  226.9 1.7 collective-permute-start.34
  229.9 1.3 copy-done.18
  232.9 6.9 %attend.1 = (bf16[384,384]{1,0:T(8,128)(2,1)S(1)}, bf16[384,384]{1,0:T(8,128)(2,1)S(1)}) custom-call(s32[8]{0:T(128)S(1)} %stack.107.sc_ref, bf16[2,384,384]{2,1,0:T(8,128)(2,1)S(1)} %copy-done.20, bf16[2,384,768]{2,1,0:T(8,128)(2,1)} %get-tuple-element.10.kv0, bf16[2,384,768]{2,1,0:T(8,128)(2,1)S(1)} %copy-done.18, s32[1,512]{1,0:T(1,128)S(1)} %bitcast.40, ...), custom_call_target="tpu_custom_call" | custom-call | flops 1811939328 | bytes 2359296 | tf_op jit(solution)/shard_map/attend/pallas_call | solution.py:217
  240.8 5.4 %collective-permute-start.25 = (bf16[384,384]{1,0:T(8,128)(2,1)S(1)}, bf16[384,384]{1,0:T(8,128)(2,1)}, u32[]{:S(2)}, u32[]{:S(2)}) collective-permute-start(bf16[384,384]{1,0:T(8,128)(2,1)S(1)} %get-tuple-element.12), channel_id=1, source_target_pairs={{0,8},{1,12},{2,10},{3,14},{4,9},{5,13},{6,11},{7,15},{8,0},{9,4},... | collective-permute-start | bytes 884744 | tf_op jit(solution)/shard_map/ppermute | solution.py:331
  246.1 1.8 collective-permute-done.23.pn
  248.0 10.7 %collective-permute-done.25.f0 = bf16[384,384]{1,0:T(8,128)(2,1)} collective-permute-done((bf16[384,384]{1,0:T(8,128)(2,1)S(1)}, bf16[384,384]{1,0:T(8,128)(2,1)}, u32[]{:S(2)}, u32[]{:S(2)}) %collective-permute-start.25) | collective-permute-done | bytes 294944 | tf_op jit(solution)/shard_map/ppermute | solution.py:331
  258.8 1.8 collective-permute-done.26.f1
  261.6 4.6 %project.3 = bf16[384,768]{1,0:T(8,128)(2,1)} custom-call(s32[7]{0:T(128)S(1)} %stack.119.sc_ref, bf16[384,384]{1,0:T(8,128)(2,1)S(1)} %copy-done.9, bf16[384,384]{1,0:T(8,128)(2,1)} %collective-permute-done.23.pn, bf16[384,384]{1,0:T(8,128)(2,1)} %collective-permute-done.24.bp, bf16[384,384]{1,0:T(8,128)(2,1)} %collective-permute-done.25.f0, ...), custom_call_target="tpu_custom_call" | custom-call | flops 905969664 | bytes 4718592 | tf_op jit(solution)/shard_map/project/pallas_call | solution.py:281
  266.3 1.7 collective-permute-start.35
  269.8 4.0 %project.2 = f32[384,768]{1,0:T(8,128)S(1)} custom-call(s32[7]{0:T(128)S(1)} %stack.100.sc_ref, bf16[384,384]{1,0:T(8,128)(2,1)S(1)} %copy-done.10, bf16[384,384]{1,0:T(8,128)(2,1)} %collective-permute-done.23.pn, bf16[384,384]{1,0:T(8,128)(2,1)} %collective-permute-done.24.bp, bf16[384,384]{1,0:T(8,128)(2,1)} %collective-permute-done.25.f0, ...), custom_call_target="tpu_custom_call" | custom-call | flops 905969664 | bytes 4718592 | tf_op jit(solution)/shard_map/project/pallas_call | solution.py:281
  273.7 8.3 %collective-permute-done.35 = bf16[384,768]{1,0:T(8,128)(2,1)} collective-permute-done((bf16[384,768]{1,0:T(8,128)(2,1)}, bf16[384,768]{1,0:T(8,128)(2,1)}, u32[]{:S(2)}, u32[]{:S(2)}) %collective-permute-start.35) | collective-permute-done | bytes 589856 | tf_op jit(solution)/shard_map/ppermute | solution.py:331
  282.1 2.3 add_convert_fusion
  (93 shorter events, 16.9 us)
Async XLA Ops:
  1.6 23.5 %collective-permute-start.10 = (bf16[3,3,384,128]{3,2,1,0:T(8,128)(2,1)S(1)}, bf16[3,3,384,128]{3,2,1,0:T(8,128)(2,1)}, u32[]{:S(2)}, u32[]{:S(2)}) collective-permute-start(bf16[3,3,384,128]{3,2,1,0:T(8,128)(2,1)S(1)} %get-tuple-element.14), channel_id=1, source_target_pairs={{0,5},{1,8},{2,7},{3,10},{4,1},{5,12},{6,3},{7,14},{8,0},{9,13},{1... | collective-permute-start | bytes 2654216 | tf_op jit(solution)/shard_map/ppermute | solution.py:331
  6.9 39.4 %collective-permute-start = (bf16[192,3072]{1,0:T(8,128)(2,1)}, bf16[192,3072]{1,0:T(8,128)(2,1)}, u32[]{:S(2)}, u32[]{:S(2)}) collective-permute-start(bf16[192,3072]{1,0:T(8,128)(2,1)} %norm_rows.1), channel_id=1, source_target_pairs={{0,4},{1,0},{2,6},{3,2},{4,5},{5,1},{6,7},{7,3},{8,12},{9,8},{10,1... | collective-permute-start | bytes 3538952 | tf_op jit(solution)/shard_map/ppermute | solution.py:331
  7.5 42.1 %collective-permute-start.2 = (bf16[192,3072]{1,0:T(8,128)(2,1)}, bf16[192,3072]{1,0:T(8,128)(2,1)}, u32[]{:S(2)}, u32[]{:S(2)}) collective-permute-start(bf16[192,3072]{1,0:T(8,128)(2,1)} %norm_rows.1), channel_id=1, source_target_pairs={{0,1},{1,0},{2,3},{3,2},{4,5},{5,9},{6,7},{7,11},{8,4},{9,8},{10,6... | collective-permute-start | bytes 3538952 | tf_op jit(solution)/shard_map/ppermute | solution.py:331
  8.6 56.3 %collective-permute-start.30 = (bf16[768,768]{1,0:T(8,128)(2,1)}, bf16[768,768]{1,0:T(8,128)(2,1)S(1)}, u32[]{:S(2)}, u32[]{:S(2)}) collective-permute-start(bf16[768,768]{1,0:T(8,128)(2,1)} %bitcast.30.refs_0_), channel_id=1, source_target_pairs={{0,8},{1,0},{2,10},{3,2},{4,9},{6,11},{8,4},{10,6},{12,5},{13,12},... | collective-permute-start | bytes 3538952 | tf_op jit(solution)/shard_map/ppermute | solution.py:331
  13.6 32.8 %collective-permute-start.15 = (bf16[3,3,384,128]{3,2,1,0:T(8,128)(2,1)S(1)}, bf16[3,3,384,128]{3,2,1,0:T(8,128)(2,1)}, u32[]{:S(2)}, u32[]{:S(2)}) collective-permute-start(bf16[3,3,384,128]{3,2,1,0:T(8,128)(2,1)S(1)} %get-tuple-element.13), channel_id=1, source_target_pairs={{1,12},{3,14},{5,8},{7,10},{8,5},{10,7},{12,1},{14,3},{17,28},{19,... | collective-permute-start | bytes 2654216 | tf_op jit(solution)/shard_map/ppermute | solution.py:331
  25.0 40.0 %collective-permute-start.11 = (bf16[3,3,384,128]{3,2,1,0:T(8,128)(2,1)}, bf16[3,3,384,128]{3,2,1,0:T(8,128)(2,1)}, u32[]{:S(2)}, u32[]{:S(2)}) collective-permute-start(bf16[3,3,384,128]{3,2,1,0:T(8,128)(2,1)} %collective-permute-done.10.refs_10_), channel_id=1, source_target_pairs={{0,16},{1,17},{2,18},{3,19},{4,20},{5,21},{6,22},{7,23},{8,24},{9,... | collective-permute-start | bytes 2654216 | tf_op jit(solution)/shard_map/ppermute | solution.py:331
  46.4 30.9 %collective-permute-start.3 = (bf16[192,3072]{1,0:T(8,128)(2,1)}, bf16[192,3072]{1,0:T(8,128)(2,1)}, u32[]{:S(2)}, u32[]{:S(2)}) collective-permute-start(bf16[192,3072]{1,0:T(8,128)(2,1)} %collective-permute-done.refs_0_), channel_id=1, source_target_pairs={{0,1},{1,0},{2,3},{3,2},{4,8},{5,4},{6,10},{7,6},{8,9},{9,5},{10,1... | collective-permute-start | bytes 3538952 | tf_op jit(solution)/shard_map/ppermute | solution.py:331
  46.4 19.1 %collective-permute-start.16 = (bf16[3,3,384,128]{3,2,1,0:T(8,128)(2,1)}, bf16[3,3,384,128]{3,2,1,0:T(8,128)(2,1)}, u32[]{:S(2)}, u32[]{:S(2)}) collective-permute-start(bf16[3,3,384,128]{3,2,1,0:T(8,128)(2,1)} %collective-permute-done.15.refs_16_), channel_id=1, source_target_pairs={{1,17},{3,19},{5,21},{7,23},{8,24},{10,26},{12,28},{14,30},{17,1},... | collective-permute-start | bytes 2654216 | tf_op jit(solution)/shard_map/ppermute | solution.py:331
  48.0 88.5 %copy-start.24 = (s32[1,9]{1,0:T(1,128)S(1)}, s32[1,9]{1,0:T(1,128)}, u32[]{:S(2)}) copy-start(s32[1,9]{1,0:T(1,128)} %param.20) | copy-start | bytes 112
  48.0 88.5 %copy-start.25 = (s32[1,9]{1,0:T(1,128)S(1)}, s32[1,9]{1,0:T(1,128)}, u32[]{:S(2)}) copy-start(s32[1,9]{1,0:T(1,128)} %param.19) | copy-start | bytes 112
  48.0 125.7 %copy-start.15 = (f32[128]{0:T(128)S(1)}, f32[128]{0:T(128)}, u32[]{:S(2)}) copy-start(f32[128]{0:T(128)} %param.14) | copy-start | bytes 1540
  48.0 125.7 %copy-start.16 = (f32[128]{0:T(128)S(1)}, f32[128]{0:T(128)}, u32[]{:S(2)}) copy-start(f32[128]{0:T(128)} %param.15) | copy-start | bytes 1540
  49.6 29.0 %collective-permute-start.12 = (bf16[3,3,384,128]{3,2,1,0:T(8,128)(2,1)}, bf16[3,3,384,128]{3,2,1,0:T(8,128)(2,1)S(1)}, u32[]{:S(2)}, u32[]{:S(2)}) collective-permute-start(bf16[3,3,384,128]{3,2,1,0:T(8,128)(2,1)} %collective-permute-done.10.refs_10_), channel_id=1, source_target_pairs={{0,1},{1,0},{2,3},{3,2},{4,5},{5,4},{6,7},{7,6},{8,9},{9,8},{10,11... | collective-permute-start | bytes 2654216 | tf_op jit(solution)/shard_map/ppermute | solution.py:331
  64.9 107.2 %copy-start = (bf16[768,768]{1,0:T(8,128)(2,1)}, bf16[768,768]{1,0:T(8,128)(2,1)S(1)}, u32[]{:S(2)}) copy-start(bf16[768,768]{1,0:T(8,128)(2,1)S(1)} %collective-permute-done.30.refs_4_) | copy-start | bytes 3538948
  65.0 16.1 %collective-permute-start.17 = (bf16[3,3,384,128]{3,2,1,0:T(8,128)(2,1)}, bf16[3,3,384,128]{3,2,1,0:T(8,128)(2,1)S(1)}, u32[]{:S(2)}, u32[]{:S(2)}) collective-permute-start(bf16[3,3,384,128]{3,2,1,0:T(8,128)(2,1)} %collective-permute-done.15.refs_16_), channel_id=1, source_target_pairs={{0,1},{1,0},{2,3},{3,2},{4,5},{5,4},{6,7},{7,6},{8,9},{9,8},{10,11... | collective-permute-start | bytes 2654216 | tf_op jit(solution)/shard_map/ppermute | solution.py:331
  65.0 19.7 %collective-permute-start.14 = (bf16[3,3,768,128]{3,2,1,0:T(8,128)(2,1)S(1)}, bf16[3,3,768,128]{3,2,1,0:T(8,128)(2,1)S(1)}, u32[]{:S(2)}, u32[]{:S(2)}) collective-permute-start(bf16[3,3,768,128]{3,2,1,0:T(8,128)(2,1)S(1)} %dynamic-slice_bitcast_fusion.refs_14_), channel_id=1, source_target_pairs={{0,1},{1,0},{2,3},{3,2},{4,5},{5,4},{6,7},{7,6},{8,9},{9,8},{10,11... | collective-permute-start | bytes 5308424 | tf_op jit(solution)/shard_map/ppermute | solution.py:331
  65.5 55.4 %collective-permute-start.4 = (bf16[192,3072]{1,0:T(8,128)(2,1)}, bf16[192,3072]{1,0:T(8,128)(2,1)}, u32[]{:S(2)}, u32[]{:S(2)}) collective-permute-start(bf16[192,3072]{1,0:T(8,128)(2,1)} %collective-permute-done.2.refs_2_), channel_id=1, source_target_pairs={{0,1},{2,3},{4,0},{5,4},{6,2},{7,6},{8,9},{9,13},{10,11},{11,15},{... | collective-permute-start | bytes 3538952 | tf_op jit(solution)/shard_map/ppermute | solution.py:331
  77.3 46.8 %collective-permute-start.5 = (bf16[192,3072]{1,0:T(8,128)(2,1)}, bf16[192,3072]{1,0:T(8,128)(2,1)}, u32[]{:S(2)}, u32[]{:S(2)}) collective-permute-start(bf16[192,3072]{1,0:T(8,128)(2,1)} %collective-permute-done.3.refs_3_), channel_id=1, source_target_pairs={{1,0},{3,2},{4,5},{5,1},{6,7},{7,3},{8,12},{9,8},{10,14},{11,10},{... | collective-permute-start | bytes 3538952 | tf_op jit(solution)/shard_map/ppermute | solution.py:331
  79.5 46.2 %collective-permute-start.1 = (bf16[192,3072]{1,0:T(8,128)(2,1)}, bf16[192,3072]{1,0:T(8,128)(2,1)S(1)}, u32[]{:S(2)}, u32[]{:S(2)}) collective-permute-start(bf16[192,3072]{1,0:T(8,128)(2,1)} %collective-permute-done.refs_0_), channel_id=1, source_target_pairs={{0,2},{1,3},{2,0},{3,1},{4,6},{5,7},{6,4},{7,5},{8,10},{9,11},{10,... | collective-permute-start | bytes 3538952 | tf_op jit(solution)/shard_map/ppermute | solution.py:331
  82.0 53.4 %collective-permute-start.6 = (bf16[192,3072]{1,0:T(8,128)(2,1)}, bf16[192,3072]{1,0:T(8,128)(2,1)S(1)}, u32[]{:S(2)}, u32[]{:S(2)}) collective-permute-start(bf16[192,3072]{1,0:T(8,128)(2,1)} %collective-permute-done.2.refs_2_), channel_id=1, source_target_pairs={{0,1},{1,0},{2,3},{3,2},{4,6},{6,4},{9,11},{11,9},{12,13},{13,12},... | collective-permute-start | bytes 3538952 | tf_op jit(solution)/shard_map/ppermute | solution.py:331
  86.0 87.5 %collective-permute-start.7 = (bf16[192,3072]{1,0:T(8,128)(2,1)}, bf16[192,3072]{1,0:T(8,128)(2,1)}, u32[]{:S(2)}, u32[]{:S(2)}) collective-permute-start(bf16[192,3072]{1,0:T(8,128)(2,1)} %collective-permute-done.3.refs_3_), channel_id=1, source_target_pairs={{0,1},{1,0},{2,3},{3,2},{5,7},{7,5},{8,10},{10,8},{12,13},{13,12},... | collective-permute-start | bytes 3538952 | tf_op jit(solution)/shard_map/ppermute | solution.py:331
  120.9 52.7 %collective-permute-start.8 = (bf16[192,3072]{1,0:T(8,128)(2,1)}, bf16[192,3072]{1,0:T(8,128)(2,1)}, u32[]{:S(2)}, u32[]{:S(2)}) collective-permute-start(bf16[192,3072]{1,0:T(8,128)(2,1)} %collective-permute-done.4.refs_4_), channel_id=1, source_target_pairs={{0,2},{2,0},{4,5},{5,4},{6,7},{7,6},{8,9},{9,8},{10,11},{11,10},{1... | collective-permute-start | bytes 3538952 | tf_op jit(solution)/shard_map/ppermute | solution.py:331
  124.1 49.5 %collective-permute-start.9 = (bf16[192,3072]{1,0:T(8,128)(2,1)}, bf16[192,3072]{1,0:T(8,128)(2,1)}, u32[]{:S(2)}, u32[]{:S(2)}) collective-permute-start(bf16[192,3072]{1,0:T(8,128)(2,1)} %collective-permute-done.5.refs_5_), channel_id=1, source_target_pairs={{1,3},{3,1},{4,5},{5,4},{6,7},{7,6},{8,9},{9,8},{10,11},{11,10},{1... | collective-permute-start | bytes 3538952 | tf_op jit(solution)/shard_map/ppermute | solution.py:331
  126.9 10.9 %collective-permute-start.13 = (bf16[3,3,384,128]{3,2,1,0:T(8,128)(2,1)}, bf16[3,3,384,128]{3,2,1,0:T(8,128)(2,1)}, u32[]{:S(2)}, u32[]{:S(2)}) collective-permute-start(bf16[3,3,384,128]{3,2,1,0:T(8,128)(2,1)} %collective-permute-done.11.refs_11_), channel_id=1, source_target_pairs={{0,1},{1,0},{2,3},{3,2},{4,5},{5,4},{6,7},{7,6},{8,9},{9,8},{10,11... | collective-permute-start | bytes 2654216 | tf_op jit(solution)/shard_map/ppermute | solution.py:331
  136.4 35.8 %collective-permute-start.18 = (bf16[3,3,384,128]{3,2,1,0:T(8,128)(2,1)}, bf16[3,3,384,128]{3,2,1,0:T(8,128)(2,1)}, u32[]{:S(2)}, u32[]{:S(2)}) collective-permute-start(bf16[3,3,384,128]{3,2,1,0:T(8,128)(2,1)} %collective-permute-done.16.refs_17_), channel_id=1, source_target_pairs={{0,1},{1,0},{2,3},{3,2},{4,5},{5,4},{6,7},{7,6},{8,9},{9,8},{10,11... | collective-permute-start | bytes 2654216 | tf_op jit(solution)/shard_map/ppermute | solution.py:331
  137.7 85.5 %collective-permute-start.28 = (bf16[768,768]{1,0:T(8,128)(2,1)}, bf16[768,768]{1,0:T(8,128)(2,1)}, u32[]{:S(2)}, u32[]{:S(2)}) collective-permute-start(bf16[768,768]{1,0:T(8,128)(2,1)} %bitcast.30.refs_0_), channel_id=1, source_target_pairs={{0,4},{1,0},{2,6},{3,2},{4,1},{6,3},{8,12},{9,8},{10,14},{11,10},{... | collective-permute-start | bytes 3538952 | tf_op jit(solution)/shard_map/ppermute | solution.py:331
  172.2 52.8 %collective-permute-start.32 = (bf16[768,768]{1,0:T(8,128)(2,1)}, bf16[768,768]{1,0:T(8,128)(2,1)S(1)}, u32[]{:S(2)}, u32[]{:S(2)}) collective-permute-start(bf16[768,768]{1,0:T(8,128)(2,1)} %copy-done), channel_id=1, source_target_pairs={{4,0},{5,1},{6,2},{7,3},{8,12},{9,13},{10,14},{11,15},{20,16},{21,... | collective-permute-start | bytes 3538952 | tf_op jit(solution)/shard_map/ppermute | solution.py:331
  173.5 53.4 %collective-permute-start.31 = (bf16[768,768]{1,0:T(8,128)(2,1)}, bf16[768,768]{1,0:T(8,128)(2,1)}, u32[]{:S(2)}, u32[]{:S(2)}) collective-permute-start(bf16[768,768]{1,0:T(8,128)(2,1)} %copy-done), channel_id=1, source_target_pairs={{0,1},{1,0},{2,3},{3,2},{4,20},{5,21},{6,22},{7,23},{8,24},{9,25},... | collective-permute-start | bytes 3538952 | tf_op jit(solution)/shard_map/ppermute | solution.py:331
  173.6 1.5 copy-start.3
  175.1 1.3 copy-start.5
  176.4 1.3 copy-start.7
  180.0 12.6 %copy-start.23 = (s32[384]{0:T(512)S(1)}, s32[384]{0:T(512)}, u32[]{:S(2)}) copy-start(s32[384]{0:T(512)} %param.21) | copy-start | bytes 4612
  192.1 36.6 %collective-permute-start.19 = (bf16[2,384,768]{2,1,0:T(8,128)(2,1)}, bf16[2,384,768]{2,1,0:T(8,128)(2,1)S(1)}, u32[]{:S(2)}, u32[]{:S(2)}) collective-permute-start(bf16[2,384,768]{2,1,0:T(8,128)(2,1)} %get-tuple-element.10.kv0), channel_id=1, source_target_pairs={{0,1},{1,0},{2,3},{3,2},{4,5},{5,4},{6,7},{7,6},{8,9},{9,8},{10,11... | collective-permute-start | bytes 3538952 | tf_op jit(solution)/shard_map/ppermute | solution.py:331
  192.6 19.4 %collective-permute-start.20 = (s32[1,512]{1,0:T(1,128)S(1)}, s32[1,512]{1,0:T(1,128)S(1)}, u32[]{:S(2)}, u32[]{:S(2)}) collective-permute-start(s32[1,512]{1,0:T(1,128)S(1)} %bitcast.37), channel_id=1, source_target_pairs={{0,4},{1,5},{2,6},{3,7},{4,0},{5,1},{6,2},{7,3},{8,12},{9,13},{10,... | collective-permute-start | bytes 6152 | tf_op jit(solution)/shard_map/ppermute | solution.py:331
  211.9 5.0 %collective-permute-start.21 = (s32[1,512]{1,0:T(1,128)S(1)}, s32[1,512]{1,0:T(1,128)S(1)}, u32[]{:S(2)}, u32[]{:S(2)}) collective-permute-start(s32[1,512]{1,0:T(1,128)S(1)} %bitcast.38), channel_id=1, source_target_pairs={{0,8},{1,9},{2,10},{3,11},{4,12},{5,13},{6,14},{7,15},{8,0},{9,1},... | collective-permute-start | bytes 6152 | tf_op jit(solution)/shard_map/ppermute | solution.py:331
  216.9 6.3 %collective-permute-start.22 = (s32[1,512]{1,0:T(1,128)S(1)}, s32[1,512]{1,0:T(1,128)S(1)}, u32[]{:S(2)}, u32[]{:S(2)}) collective-permute-start(s32[1,512]{1,0:T(1,128)S(1)} %bitcast.39), channel_id=1, source_target_pairs={{0,12},{1,13},{2,14},{3,15},{4,8},{5,9},{6,10},{7,11},{8,4},{9,5},... | collective-permute-start | bytes 6152 | tf_op jit(solution)/shard_map/ppermute | solution.py:331
  223.2 5.4 %copy-start.21 = (s32[1,512]{1,0:T(1,128)}, s32[1,512]{1,0:T(1,128)S(1)}, u32[]{:S(2)}) copy-start(s32[1,512]{1,0:T(1,128)S(1)} %collective-permute-done.22.refs_3_) | copy-start | bytes 6148
  223.2 17.5 %collective-permute-start.27 = (bf16[768,768]{1,0:T(8,128)(2,1)}, bf16[768,768]{1,0:T(8,128)(2,1)S(1)}, u32[]{:S(2)}, u32[]{:S(2)}) collective-permute-start(bf16[768,768]{1,0:T(8,128)(2,1)} %bitcast.30.refs_0_), channel_id=1, source_target_pairs={{0,1},{1,0},{2,3},{3,2},{4,5},{5,4},{6,7},{7,6},{8,9},{9,8},{10,11... | collective-permute-start | bytes 3538952 | tf_op jit(solution)/shard_map/ppermute | solution.py:331
  223.2 35.6 %collective-permute-start.29 = (bf16[768,768]{1,0:T(8,128)(2,1)}, bf16[768,768]{1,0:T(8,128)(2,1)}, u32[]{:S(2)}, u32[]{:S(2)}) collective-permute-start(bf16[768,768]{1,0:T(8,128)(2,1)} %collective-permute-done.28.refs_2_), channel_id=1, source_target_pairs={{1,17},{3,19},{4,20},{6,22},{9,25},{11,27},{12,28},{14,30},{17,1},... | collective-permute-start | bytes 3538952 | tf_op jit(solution)/shard_map/ppermute | solution.py:331
  225.0 33.8 %collective-permute-start.33 = (bf16[768,768]{1,0:T(8,128)(2,1)S(1)}, bf16[768,768]{1,0:T(8,128)(2,1)}, u32[]{:S(2)}, u32[]{:S(2)}) collective-permute-start(bf16[768,768]{1,0:T(8,128)(2,1)S(1)} %collective-permute-done.32.refs_6_.refs_8_), channel_id=1, source_target_pairs={{0,16},{2,18},{4,5},{5,4},{6,7},{7,6},{8,9},{9,8},{10,11},{11,10},... | collective-permute-start | bytes 3538952 | tf_op jit(solution)/shard_map/ppermute | solution.py:331
  226.9 31.9 %collective-permute-start.34 = (bf16[768,768]{1,0:T(8,128)(2,1)}, bf16[768,768]{1,0:T(8,128)(2,1)}, u32[]{:S(2)}, u32[]{:S(2)}) collective-permute-start(bf16[768,768]{1,0:T(8,128)(2,1)} %collective-permute-done.31.refs_5_), channel_id=1, source_target_pairs={{5,1},{7,3},{8,12},{10,14},{21,17},{23,19},{24,28},{26,30}} | collective-permute-start | bytes 3538952 | tf_op jit(solution)/shard_map/ppermute | solution.py:331
  229.9 1.3 copy-start.18
  232.9 27.8 %copy-start.1 = (bf16[768,768]{1,0:T(8,128)(2,1)S(1)}, bf16[768,768]{1,0:T(8,128)(2,1)}, u32[]{:S(2)}) copy-start(bf16[768,768]{1,0:T(8,128)(2,1)} %copy-done) | copy-start | bytes 3538948
  239.7 8.2 %collective-permute-start.23 = (bf16[384,384]{1,0:T(8,128)(2,1)S(1)}, bf16[384,384]{1,0:T(8,128)(2,1)}, u32[]{:S(2)}, u32[]{:S(2)}) collective-permute-start(bf16[384,384]{1,0:T(8,128)(2,1)S(1)} %get-tuple-element.11.an), channel_id=1, source_target_pairs={{0,1},{1,5},{2,3},{3,7},{4,0},{5,4},{6,2},{7,6},{8,9},{9,13},{10,1... | collective-permute-start | bytes 884744 | tf_op jit(solution)/shard_map/ppermute | solution.py:331
  240.8 18.0 %collective-permute-start.25 = (bf16[384,384]{1,0:T(8,128)(2,1)S(1)}, bf16[384,384]{1,0:T(8,128)(2,1)}, u32[]{:S(2)}, u32[]{:S(2)}) collective-permute-start(bf16[384,384]{1,0:T(8,128)(2,1)S(1)} %get-tuple-element.12), channel_id=1, source_target_pairs={{0,8},{1,12},{2,10},{3,14},{4,9},{5,13},{6,11},{7,15},{8,0},{9,4},... | collective-permute-start | bytes 884744 | tf_op jit(solution)/shard_map/ppermute | solution.py:331
  248.0 10.9 %collective-permute-start.24 = (bf16[384,384]{1,0:T(8,128)(2,1)}, bf16[384,384]{1,0:T(8,128)(2,1)}, u32[]{:S(2)}, u32[]{:S(2)}) collective-permute-start(bf16[384,384]{1,0:T(8,128)(2,1)} %collective-permute-done.23.pn), channel_id=1, source_target_pairs={{0,1},{1,0},{2,3},{3,2},{4,5},{5,4},{6,7},{7,6},{8,9},{9,8},{10,11... | collective-permute-start | bytes 884744 | tf_op jit(solution)/shard_map/ppermute | solution.py:331
  258.7 1.9 collective-permute-start.26
  266.3 15.8 %collective-permute-start.35 = (bf16[384,768]{1,0:T(8,128)(2,1)}, bf16[384,768]{1,0:T(8,128)(2,1)}, u32[]{:S(2)}, u32[]{:S(2)}) collective-permute-start(bf16[384,768]{1,0:T(8,128)(2,1)} %project.3), channel_id=1, source_target_pairs={{0,2},{1,3},{2,0},{3,1},{4,6},{5,7},{6,4},{7,5},{8,10},{9,11},{10,... | collective-permute-start | bytes 1769480 | tf_op jit(solution)/shard_map/ppermute | solution.py:331
  (14 other events, 13.9 us)

commit v4 on v3

--- a/solution.py
+++ b/solution.py
@@ -495,12 +495,12 @@
     send = project(project_block(jnp.logical_not(near_stays)), pieces, blocks, BF16)
     got = move(send, to_column())
     keep = project(project_block(near_stays), pieces, blocks, F32)
-    projected = keep + got.astype(F32)
-    out_width = projected.shape[1]
+    out_width = keep.shape[1]
     offset = (x * nc + c) * out_width
     latent_cols = lax.dynamic_slice_in_dim(latents, offset, out_width, 1).astype(F32)
     gate_cols = lax.dynamic_slice_in_dim(mod_gate, offset, out_width, 0)
-    return (latent_cols + gate_cols * projected).astype(BF16)
+    base = lax.optimization_barrier(latent_cols + gate_cols * keep)
+    return (base + gate_cols * got.astype(F32)).astype(BF16)
 
 
 def modulate(latents, mod_shift, mod_scale):

time: 285 us -> 285 us (level)
  no operation moved by 1% of the time
where the time goes in v4:
time: 285 us; the launch traced here: 284 us
  starting transfers between devices  134 us (47%)
  waiting for transfers between devices  93 us (33%)
  Pallas kernels  29.6 us (10%)
  local copies, waits for them, and re-layouts  23.5 us (8%)
  other arithmetic  3.34 us (1%)
    ppermute x36, starting transfers between devices, move(): return lax.ppermute(array, AXES, pairs)  134 us
    ppermute x36, waiting for transfers between devices, move(): return lax.ppermute(array, AXES, pairs)  93 us
    unnamed x52, local copies, waits for them, and re-layouts  19.2 us
    pallas_call x1, Pallas kernels, qkv_tiles(): pl.pallas_call(functools.partial(qkv_kernel, counts), out_shape=(jax.Shap...  11.3 us
    pallas_call x2, Pallas kernels, project(): pl.pallas_call(project_kernel, out_shape=jax.ShapeDtypeStruct((rows, widt...  8.59 us
    pallas_call x1, Pallas kernels, attend(): pl.pallas_call(attend_kernel, out_shape=(shape, shape), in_specs=[smem] +...  6.85 us
  transfers between devices with their start and end apart: 36, of which 11 were waited for; matrix products, arithmetic and copies ran while one was open for 1% of the time, Pallas kernels for 9%

profile of v4, /device:TPU:0, one launch (start us, length us, event | category | flops | bytes accessed | tf_op | source)
XLA Modules:
  0.0 284.1 jit_solution(4361775672239750826)
XLA Ops:
  0.0 1.5 dynamic-slice_bitcast_fusion.1
  1.6 2.6 collective-permute-start.10
  4.1 2.8 norm_rows.1
  8.6 4.9 %collective-permute-start.30 = (bf16[768,768]{1,0:T(8,128)(2,1)}, bf16[768,768]{1,0:T(8,128)(2,1)S(1)}, u32[]{:S(2)}, u32[]{:S(2)}) collective-permute-start(bf16[768,768]{1,0:T(8,128)(2,1)} %bitcast.30.refs_0_), channel_id=1, source_target_pairs={{0,8},{1,0},{2,10},{3,2},{4,9},{6,11},{8,4},{10,6},{12,5},{13,12},... | collective-permute-start | bytes 3538952 | tf_op jit(solution)/shard_map/ppermute | solution.py:331
  13.6 1.6 collective-permute-start.15
  15.1 9.9 %collective-permute-done.10.refs_10_ = bf16[3,3,384,128]{3,2,1,0:T(8,128)(2,1)} collective-permute-done((bf16[3,3,384,128]{3,2,1,0:T(8,128)(2,1)S(1)}, bf16[3,3,384,128]{3,2,1,0:T(8,128)(2,1)}, u32[]{:S(2)}, u32[]{:S(2)}) %collective-permute-start.10) | collective-permute-done | bytes 884768 | tf_op jit(solution)/shard_map/ppermute | solution.py:331
  25.0 12.9 %collective-permute-start.11 = (bf16[3,3,384,128]{3,2,1,0:T(8,128)(2,1)}, bf16[3,3,384,128]{3,2,1,0:T(8,128)(2,1)}, u32[]{:S(2)}, u32[]{:S(2)}) collective-permute-start(bf16[3,3,384,128]{3,2,1,0:T(8,128)(2,1)} %collective-permute-done.10.refs_10_), channel_id=1, source_target_pairs={{0,16},{1,17},{2,18},{3,19},{4,20},{5,21},{6,22},{7,23},{8,24},{9,... | collective-permute-start | bytes 2654216 | tf_op jit(solution)/shard_map/ppermute | solution.py:331
  37.9 8.5 %collective-permute-done.refs_0_ = bf16[192,3072]{1,0:T(8,128)(2,1)} collective-permute-done((bf16[192,3072]{1,0:T(8,128)(2,1)}, bf16[192,3072]{1,0:T(8,128)(2,1)}, u32[]{:S(2)}, u32[]{:S(2)}) %collective-permute-start) | collective-permute-done | bytes 1179680 | tf_op jit(solution)/shard_map/ppermute | solution.py:331
  46.4 1.6 collective-permute-start.16
  48.0 1.6 dynamic-slice_bitcast_fusion.refs_14_
  49.6 15.3 %collective-permute-start.12 = (bf16[3,3,384,128]{3,2,1,0:T(8,128)(2,1)}, bf16[3,3,384,128]{3,2,1,0:T(8,128)(2,1)S(1)}, u32[]{:S(2)}, u32[]{:S(2)}) collective-permute-start(bf16[3,3,384,128]{3,2,1,0:T(8,128)(2,1)} %collective-permute-done.10.refs_10_), channel_id=1, source_target_pairs={{0,1},{1,0},{2,3},{3,2},{4,5},{5,4},{6,7},{7,6},{8,9},{9,8},{10,11... | collective-permute-start | bytes 2654216 | tf_op jit(solution)/shard_map/ppermute | solution.py:331
  65.5 11.8 %collective-permute-start.4 = (bf16[192,3072]{1,0:T(8,128)(2,1)}, bf16[192,3072]{1,0:T(8,128)(2,1)}, u32[]{:S(2)}, u32[]{:S(2)}) collective-permute-start(bf16[192,3072]{1,0:T(8,128)(2,1)} %collective-permute-done.2.refs_2_), channel_id=1, source_target_pairs={{0,1},{2,3},{4,0},{5,4},{6,2},{7,6},{8,9},{9,13},{10,11},{11,15},{... | collective-permute-start | bytes 3538952 | tf_op jit(solution)/shard_map/ppermute | solution.py:331
  77.3 1.3 collective-permute-start.5
  79.5 1.5 collective-permute-start.1
  82.0 2.7 collective-permute-start.6
  84.7 1.2 copy-done.2
  86.0 1.9 collective-permute-start.7
  87.9 33.0 %collective-permute-done.4.refs_4_ = bf16[192,3072]{1,0:T(8,128)(2,1)} collective-permute-done((bf16[192,3072]{1,0:T(8,128)(2,1)}, bf16[192,3072]{1,0:T(8,128)(2,1)}, u32[]{:S(2)}, u32[]{:S(2)}) %collective-permute-start.4) | collective-permute-done | bytes 1179680 | tf_op jit(solution)/shard_map/ppermute | solution.py:331
  120.9 3.2 %collective-permute-start.8 = (bf16[192,3072]{1,0:T(8,128)(2,1)}, bf16[192,3072]{1,0:T(8,128)(2,1)}, u32[]{:S(2)}, u32[]{:S(2)}) collective-permute-start(bf16[192,3072]{1,0:T(8,128)(2,1)} %collective-permute-done.4.refs_4_), channel_id=1, source_target_pairs={{0,2},{2,0},{4,5},{5,4},{6,7},{7,6},{8,9},{9,8},{10,11},{11,10},{1... | collective-permute-start | bytes 3538952 | tf_op jit(solution)/shard_map/ppermute | solution.py:331
  124.1 1.7 collective-permute-start.9
  126.9 8.5 %collective-permute-start.13 = (bf16[3,3,384,128]{3,2,1,0:T(8,128)(2,1)}, bf16[3,3,384,128]{3,2,1,0:T(8,128)(2,1)}, u32[]{:S(2)}, u32[]{:S(2)}) collective-permute-start(bf16[3,3,384,128]{3,2,1,0:T(8,128)(2,1)} %collective-permute-done.11.refs_11_), channel_id=1, source_target_pairs={{0,1},{1,0},{2,3},{3,2},{4,5},{5,4},{6,7},{7,6},{8,9},{9,8},{10,11... | collective-permute-start | bytes 2654216 | tf_op jit(solution)/shard_map/ppermute | solution.py:331
  137.7 34.5 %collective-permute-start.28 = (bf16[768,768]{1,0:T(8,128)(2,1)}, bf16[768,768]{1,0:T(8,128)(2,1)}, u32[]{:S(2)}, u32[]{:S(2)}) collective-permute-start(bf16[768,768]{1,0:T(8,128)(2,1)} %bitcast.30.refs_0_), channel_id=1, source_target_pairs={{0,4},{1,0},{2,6},{3,2},{4,1},{6,3},{8,12},{9,8},{10,14},{11,10},{... | collective-permute-start | bytes 3538952 | tf_op jit(solution)/shard_map/ppermute | solution.py:331
  172.2 1.3 collective-permute-start.32
  173.7 1.5 copy-done.3
  175.1 1.3 copy-done.5
  176.4 1.3 copy-done.7
  180.0 11.3 %qkv_tiles.1 = (bf16[2,384,384]{2,1,0:T(8,128)(2,1)S(1)}, bf16[2,384,768]{2,1,0:T(8,128)(2,1)}) custom-call(s32[9]{0:T(128)S(1)} %stack.116.sc_ref, bf16[192,3072]{1,0:T(8,128)(2,1)} %collective-permute-done.refs_0_, bf16[192,3072]{1,0:T(8,128)(2,1)S(1)} %copy-done.5, bf16[192,3072]{1,0:T(8,128)(2,1)} %collective-permute-done.2.refs_2_, ...), custom_call_target="tpu_custom_call" | custom-call | flops 5435817984 | bytes 7077888 | tf_op jit(solution)/shard_map/qkv_tiles/pallas_call | solution.py:150
  192.6 3.6 %collective-permute-start.20 = (s32[1,512]{1,0:T(1,128)S(1)}, s32[1,512]{1,0:T(1,128)S(1)}, u32[]{:S(2)}, u32[]{:S(2)}) collective-permute-start(s32[1,512]{1,0:T(1,128)S(1)} %bitcast.37), channel_id=1, source_target_pairs={{0,4},{1,5},{2,6},{3,7},{4,0},{5,1},{6,2},{7,3},{8,12},{9,13},{10,... | collective-permute-start | bytes 6152 | tf_op jit(solution)/shard_map/ppermute | solution.py:331
  196.1 15.8 %collective-permute-done.20.refs_1_ = s32[1,512]{1,0:T(1,128)S(1)} collective-permute-done((s32[1,512]{1,0:T(1,128)S(1)}, s32[1,512]{1,0:T(1,128)S(1)}, u32[]{:S(2)}, u32[]{:S(2)}) %collective-permute-start.20) | collective-permute-done | bytes 2080 | tf_op jit(solution)/shard_map/ppermute | solution.py:331
  211.9 3.4 %collective-permute-start.21 = (s32[1,512]{1,0:T(1,128)S(1)}, s32[1,512]{1,0:T(1,128)S(1)}, u32[]{:S(2)}, u32[]{:S(2)}) collective-permute-start(s32[1,512]{1,0:T(1,128)S(1)} %bitcast.38), channel_id=1, source_target_pairs={{0,8},{1,9},{2,10},{3,11},{4,12},{5,13},{6,14},{7,15},{8,0},{9,1},... | collective-permute-start | bytes 6152 | tf_op jit(solution)/shard_map/ppermute | solution.py:331
  215.4 1.6 collective-permute-done.21.refs_2_
  216.9 4.8 %collective-permute-start.22 = (s32[1,512]{1,0:T(1,128)S(1)}, s32[1,512]{1,0:T(1,128)S(1)}, u32[]{:S(2)}, u32[]{:S(2)}) collective-permute-start(s32[1,512]{1,0:T(1,128)S(1)} %bitcast.39), channel_id=1, source_target_pairs={{0,12},{1,13},{2,14},{3,15},{4,8},{5,9},{6,10},{7,11},{8,4},{9,5},... | collective-permute-start | bytes 6152 | tf_op jit(solution)/shard_map/ppermute | solution.py:331
  221.7 1.6 collective-permute-done.22.refs_3_
  223.2 1.7 collective-permute-start.29
  225.0 1.9 collective-permute-start.33
  226.9 1.7 collective-permute-start.34
  229.9 1.3 copy-done.18
  232.9 6.9 %attend.1 = (bf16[384,384]{1,0:T(8,128)(2,1)S(1)}, bf16[384,384]{1,0:T(8,128)(2,1)S(1)}) custom-call(s32[8]{0:T(128)S(1)} %stack.107.sc_ref, bf16[2,384,384]{2,1,0:T(8,128)(2,1)S(1)} %copy-done.20, bf16[2,384,768]{2,1,0:T(8,128)(2,1)} %get-tuple-element.10.kv0, bf16[2,384,768]{2,1,0:T(8,128)(2,1)S(1)} %copy-done.18, s32[1,512]{1,0:T(1,128)S(1)} %bitcast.40, ...), custom_call_target="tpu_custom_call" | custom-call | flops 1811939328 | bytes 2359296 | tf_op jit(solution)/shard_map/attend/pallas_call | solution.py:217
  240.8 5.4 %collective-permute-start.25 = (bf16[384,384]{1,0:T(8,128)(2,1)S(1)}, bf16[384,384]{1,0:T(8,128)(2,1)}, u32[]{:S(2)}, u32[]{:S(2)}) collective-permute-start(bf16[384,384]{1,0:T(8,128)(2,1)S(1)} %get-tuple-element.12), channel_id=1, source_target_pairs={{0,8},{1,12},{2,10},{3,14},{4,9},{5,13},{6,11},{7,15},{8,0},{9,4},... | collective-permute-start | bytes 884744 | tf_op jit(solution)/shard_map/ppermute | solution.py:331
  246.1 1.8 collective-permute-done.23.pn
  248.0 10.7 %collective-permute-done.25.f0 = bf16[384,384]{1,0:T(8,128)(2,1)} collective-permute-done((bf16[384,384]{1,0:T(8,128)(2,1)S(1)}, bf16[384,384]{1,0:T(8,128)(2,1)}, u32[]{:S(2)}, u32[]{:S(2)}) %collective-permute-start.25) | collective-permute-done | bytes 294944 | tf_op jit(solution)/shard_map/ppermute | solution.py:331
  258.8 1.8 collective-permute-done.26.f1
  261.6 4.6 %project.3 = bf16[384,768]{1,0:T(8,128)(2,1)} custom-call(s32[7]{0:T(128)S(1)} %stack.119.sc_ref, bf16[384,384]{1,0:T(8,128)(2,1)S(1)} %copy-done.9, bf16[384,384]{1,0:T(8,128)(2,1)} %collective-permute-done.23.pn, bf16[384,384]{1,0:T(8,128)(2,1)} %collective-permute-done.24.bp, bf16[384,384]{1,0:T(8,128)(2,1)} %collective-permute-done.25.f0, ...), custom_call_target="tpu_custom_call" | custom-call | flops 905969664 | bytes 4718592 | tf_op jit(solution)/shard_map/project/pallas_call | solution.py:281
  266.3 1.7 collective-permute-start.35
  269.8 4.0 %project.2 = f32[384,768]{1,0:T(8,128)S(1)} custom-call(s32[7]{0:T(128)S(1)} %stack.100.sc_ref, bf16[384,384]{1,0:T(8,128)(2,1)S(1)} %copy-done.10, bf16[384,384]{1,0:T(8,128)(2,1)} %collective-permute-done.23.pn, bf16[384,384]{1,0:T(8,128)(2,1)} %collective-permute-done.24.bp, bf16[384,384]{1,0:T(8,128)(2,1)} %collective-permute-done.25.f0, ...), custom_call_target="tpu_custom_call" | custom-call | flops 905969664 | bytes 4718592 | tf_op jit(solution)/shard_map/project/pallas_call | solution.py:281
  273.7 1.2 multiply_add_fusion
  274.9 7.1 %collective-permute-done.35 = bf16[384,768]{1,0:T(8,128)(2,1)} collective-permute-done((bf16[384,768]{1,0:T(8,128)(2,1)}, bf16[384,768]{1,0:T(8,128)(2,1)}, u32[]{:S(2)}, u32[]{:S(2)}) %collective-permute-start.35) | collective-permute-done | bytes 589856 | tf_op jit(solution)/shard_map/ppermute | solution.py:331
  282.1 2.0 add_convert_fusion
  (94 shorter events, 18.0 us)
Async XLA Ops:
  1.6 23.5 %collective-permute-start.10 = (bf16[3,3,384,128]{3,2,1,0:T(8,128)(2,1)S(1)}, bf16[3,3,384,128]{3,2,1,0:T(8,128)(2,1)}, u32[]{:S(2)}, u32[]{:S(2)}) collective-permute-start(bf16[3,3,384,128]{3,2,1,0:T(8,128)(2,1)S(1)} %get-tuple-element.14), channel_id=1, source_target_pairs={{0,5},{1,8},{2,7},{3,10},{4,1},{5,12},{6,3},{7,14},{8,0},{9,13},{1... | collective-permute-start | bytes 2654216 | tf_op jit(solution)/shard_map/ppermute | solution.py:331
  6.9 39.4 %collective-permute-start = (bf16[192,3072]{1,0:T(8,128)(2,1)}, bf16[192,3072]{1,0:T(8,128)(2,1)}, u32[]{:S(2)}, u32[]{:S(2)}) collective-permute-start(bf16[192,3072]{1,0:T(8,128)(2,1)} %norm_rows.1), channel_id=1, source_target_pairs={{0,4},{1,0},{2,6},{3,2},{4,5},{5,1},{6,7},{7,3},{8,12},{9,8},{10,1... | collective-permute-start | bytes 3538952 | tf_op jit(solution)/shard_map/ppermute | solution.py:331
  7.5 42.1 %collective-permute-start.2 = (bf16[192,3072]{1,0:T(8,128)(2,1)}, bf16[192,3072]{1,0:T(8,128)(2,1)}, u32[]{:S(2)}, u32[]{:S(2)}) collective-permute-start(bf16[192,3072]{1,0:T(8,128)(2,1)} %norm_rows.1), channel_id=1, source_target_pairs={{0,1},{1,0},{2,3},{3,2},{4,5},{5,9},{6,7},{7,11},{8,4},{9,8},{10,6... | collective-permute-start | bytes 3538952 | tf_op jit(solution)/shard_map/ppermute | solution.py:331
  8.6 56.3 %collective-permute-start.30 = (bf16[768,768]{1,0:T(8,128)(2,1)}, bf16[768,768]{1,0:T(8,128)(2,1)S(1)}, u32[]{:S(2)}, u32[]{:S(2)}) collective-permute-start(bf16[768,768]{1,0:T(8,128)(2,1)} %bitcast.30.refs_0_), channel_id=1, source_target_pairs={{0,8},{1,0},{2,10},{3,2},{4,9},{6,11},{8,4},{10,6},{12,5},{13,12},... | collective-permute-start | bytes 3538952 | tf_op jit(solution)/shard_map/ppermute | solution.py:331
  13.6 32.8 %collective-permute-start.15 = (bf16[3,3,384,128]{3,2,1,0:T(8,128)(2,1)S(1)}, bf16[3,3,384,128]{3,2,1,0:T(8,128)(2,1)}, u32[]{:S(2)}, u32[]{:S(2)}) collective-permute-start(bf16[3,3,384,128]{3,2,1,0:T(8,128)(2,1)S(1)} %get-tuple-element.13), channel_id=1, source_target_pairs={{1,12},{3,14},{5,8},{7,10},{8,5},{10,7},{12,1},{14,3},{17,28},{19,... | collective-permute-start | bytes 2654216 | tf_op jit(solution)/shard_map/ppermute | solution.py:331
  25.0 40.0 %collective-permute-start.11 = (bf16[3,3,384,128]{3,2,1,0:T(8,128)(2,1)}, bf16[3,3,384,128]{3,2,1,0:T(8,128)(2,1)}, u32[]{:S(2)}, u32[]{:S(2)}) collective-permute-start(bf16[3,3,384,128]{3,2,1,0:T(8,128)(2,1)} %collective-permute-done.10.refs_10_), channel_id=1, source_target_pairs={{0,16},{1,17},{2,18},{3,19},{4,20},{5,21},{6,22},{7,23},{8,24},{9,... | collective-permute-start | bytes 2654216 | tf_op jit(solution)/shard_map/ppermute | solution.py:331
  46.4 30.9 %collective-permute-start.3 = (bf16[192,3072]{1,0:T(8,128)(2,1)}, bf16[192,3072]{1,0:T(8,128)(2,1)}, u32[]{:S(2)}, u32[]{:S(2)}) collective-permute-start(bf16[192,3072]{1,0:T(8,128)(2,1)} %collective-permute-done.refs_0_), channel_id=1, source_target_pairs={{0,1},{1,0},{2,3},{3,2},{4,8},{5,4},{6,10},{7,6},{8,9},{9,5},{10,1... | collective-permute-start | bytes 3538952 | tf_op jit(solution)/shard_map/ppermute | solution.py:331
  46.4 19.1 %collective-permute-start.16 = (bf16[3,3,384,128]{3,2,1,0:T(8,128)(2,1)}, bf16[3,3,384,128]{3,2,1,0:T(8,128)(2,1)}, u32[]{:S(2)}, u32[]{:S(2)}) collective-permute-start(bf16[3,3,384,128]{3,2,1,0:T(8,128)(2,1)} %collective-permute-done.15.refs_16_), channel_id=1, source_target_pairs={{1,17},{3,19},{5,21},{7,23},{8,24},{10,26},{12,28},{14,30},{17,1},... | collective-permute-start | bytes 2654216 | tf_op jit(solution)/shard_map/ppermute | solution.py:331
  48.0 88.5 %copy-start.24 = (s32[1,9]{1,0:T(1,128)S(1)}, s32[1,9]{1,0:T(1,128)}, u32[]{:S(2)}) copy-start(s32[1,9]{1,0:T(1,128)} %param.20) | copy-start | bytes 112
  48.0 88.5 %copy-start.25 = (s32[1,9]{1,0:T(1,128)S(1)}, s32[1,9]{1,0:T(1,128)}, u32[]{:S(2)}) copy-start(s32[1,9]{1,0:T(1,128)} %param.19) | copy-start | bytes 112
  48.0 125.7 %copy-start.15 = (f32[128]{0:T(128)S(1)}, f32[128]{0:T(128)}, u32[]{:S(2)}) copy-start(f32[128]{0:T(128)} %param.14) | copy-start | bytes 1540
  48.0 125.7 %copy-start.16 = (f32[128]{0:T(128)S(1)}, f32[128]{0:T(128)}, u32[]{:S(2)}) copy-start(f32[128]{0:T(128)} %param.15) | copy-start | bytes 1540
  49.6 29.0 %collective-permute-start.12 = (bf16[3,3,384,128]{3,2,1,0:T(8,128)(2,1)}, bf16[3,3,384,128]{3,2,1,0:T(8,128)(2,1)S(1)}, u32[]{:S(2)}, u32[]{:S(2)}) collective-permute-start(bf16[3,3,384,128]{3,2,1,0:T(8,128)(2,1)} %collective-permute-done.10.refs_10_), channel_id=1, source_target_pairs={{0,1},{1,0},{2,3},{3,2},{4,5},{5,4},{6,7},{7,6},{8,9},{9,8},{10,11... | collective-permute-start | bytes 2654216 | tf_op jit(solution)/shard_map/ppermute | solution.py:331
  64.9 107.2 %copy-start = (bf16[768,768]{1,0:T(8,128)(2,1)}, bf16[768,768]{1,0:T(8,128)(2,1)S(1)}, u32[]{:S(2)}) copy-start(bf16[768,768]{1,0:T(8,128)(2,1)S(1)} %collective-permute-done.30.refs_4_) | copy-start | bytes 3538948
  65.0 16.1 %collective-permute-start.17 = (bf16[3,3,384,128]{3,2,1,0:T(8,128)(2,1)}, bf16[3,3,384,128]{3,2,1,0:T(8,128)(2,1)S(1)}, u32[]{:S(2)}, u32[]{:S(2)}) collective-permute-start(bf16[3,3,384,128]{3,2,1,0:T(8,128)(2,1)} %collective-permute-done.15.refs_16_), channel_id=1, source_target_pairs={{0,1},{1,0},{2,3},{3,2},{4,5},{5,4},{6,7},{7,6},{8,9},{9,8},{10,11... | collective-permute-start | bytes 2654216 | tf_op jit(solution)/shard_map/ppermute | solution.py:331
  65.0 19.7 %collective-permute-start.14 = (bf16[3,3,768,128]{3,2,1,0:T(8,128)(2,1)S(1)}, bf16[3,3,768,128]{3,2,1,0:T(8,128)(2,1)S(1)}, u32[]{:S(2)}, u32[]{:S(2)}) collective-permute-start(bf16[3,3,768,128]{3,2,1,0:T(8,128)(2,1)S(1)} %dynamic-slice_bitcast_fusion.refs_14_), channel_id=1, source_target_pairs={{0,1},{1,0},{2,3},{3,2},{4,5},{5,4},{6,7},{7,6},{8,9},{9,8},{10,11... | collective-permute-start | bytes 5308424 | tf_op jit(solution)/shard_map/ppermute | solution.py:331
  65.5 55.4 %collective-permute-start.4 = (bf16[192,3072]{1,0:T(8,128)(2,1)}, bf16[192,3072]{1,0:T(8,128)(2,1)}, u32[]{:S(2)}, u32[]{:S(2)}) collective-permute-start(bf16[192,3072]{1,0:T(8,128)(2,1)} %collective-permute-done.2.refs_2_), channel_id=1, source_target_pairs={{0,1},{2,3},{4,0},{5,4},{6,2},{7,6},{8,9},{9,13},{10,11},{11,15},{... | collective-permute-start | bytes 3538952 | tf_op jit(solution)/shard_map/ppermute | solution.py:331
  77.3 46.8 %collective-permute-start.5 = (bf16[192,3072]{1,0:T(8,128)(2,1)}, bf16[192,3072]{1,0:T(8,128)(2,1)}, u32[]{:S(2)}, u32[]{:S(2)}) collective-permute-start(bf16[192,3072]{1,0:T(8,128)(2,1)} %collective-permute-done.3.refs_3_), channel_id=1, source_target_pairs={{1,0},{3,2},{4,5},{5,1},{6,7},{7,3},{8,12},{9,8},{10,14},{11,10},{... | collective-permute-start | bytes 3538952 | tf_op jit(solution)/shard_map/ppermute | solution.py:331
  79.5 46.2 %collective-permute-start.1 = (bf16[192,3072]{1,0:T(8,128)(2,1)}, bf16[192,3072]{1,0:T(8,128)(2,1)S(1)}, u32[]{:S(2)}, u32[]{:S(2)}) collective-permute-start(bf16[192,3072]{1,0:T(8,128)(2,1)} %collective-permute-done.refs_0_), channel_id=1, source_target_pairs={{0,2},{1,3},{2,0},{3,1},{4,6},{5,7},{6,4},{7,5},{8,10},{9,11},{10,... | collective-permute-start | bytes 3538952 | tf_op jit(solution)/shard_map/ppermute | solution.py:331
  82.0 53.4 %collective-permute-start.6 = (bf16[192,3072]{1,0:T(8,128)(2,1)}, bf16[192,3072]{1,0:T(8,128)(2,1)S(1)}, u32[]{:S(2)}, u32[]{:S(2)}) collective-permute-start(bf16[192,3072]{1,0:T(8,128)(2,1)} %collective-permute-done.2.refs_2_), channel_id=1, source_target_pairs={{0,1},{1,0},{2,3},{3,2},{4,6},{6,4},{9,11},{11,9},{12,13},{13,12},... | collective-permute-start | bytes 3538952 | tf_op jit(solution)/shard_map/ppermute | solution.py:331
  86.0 87.5 %collective-permute-start.7 = (bf16[192,3072]{1,0:T(8,128)(2,1)}, bf16[192,3072]{1,0:T(8,128)(2,1)}, u32[]{:S(2)}, u32[]{:S(2)}) collective-permute-start(bf16[192,3072]{1,0:T(8,128)(2,1)} %collective-permute-done.3.refs_3_), channel_id=1, source_target_pairs={{0,1},{1,0},{2,3},{3,2},{5,7},{7,5},{8,10},{10,8},{12,13},{13,12},... | collective-permute-start | bytes 3538952 | tf_op jit(solution)/shard_map/ppermute | solution.py:331
  120.9 52.7 %collective-permute-start.8 = (bf16[192,3072]{1,0:T(8,128)(2,1)}, bf16[192,3072]{1,0:T(8,128)(2,1)}, u32[]{:S(2)}, u32[]{:S(2)}) collective-permute-start(bf16[192,3072]{1,0:T(8,128)(2,1)} %collective-permute-done.4.refs_4_), channel_id=1, source_target_pairs={{0,2},{2,0},{4,5},{5,4},{6,7},{7,6},{8,9},{9,8},{10,11},{11,10},{1... | collective-permute-start | bytes 3538952 | tf_op jit(solution)/shard_map/ppermute | solution.py:331
  124.1 49.5 %collective-permute-start.9 = (bf16[192,3072]{1,0:T(8,128)(2,1)}, bf16[192,3072]{1,0:T(8,128)(2,1)}, u32[]{:S(2)}, u32[]{:S(2)}) collective-permute-start(bf16[192,3072]{1,0:T(8,128)(2,1)} %collective-permute-done.5.refs_5_), channel_id=1, source_target_pairs={{1,3},{3,1},{4,5},{5,4},{6,7},{7,6},{8,9},{9,8},{10,11},{11,10},{1... | collective-permute-start | bytes 3538952 | tf_op jit(solution)/shard_map/ppermute | solution.py:331
  126.9 10.9 %collective-permute-start.13 = (bf16[3,3,384,128]{3,2,1,0:T(8,128)(2,1)}, bf16[3,3,384,128]{3,2,1,0:T(8,128)(2,1)}, u32[]{:S(2)}, u32[]{:S(2)}) collective-permute-start(bf16[3,3,384,128]{3,2,1,0:T(8,128)(2,1)} %collective-permute-done.11.refs_11_), channel_id=1, source_target_pairs={{0,1},{1,0},{2,3},{3,2},{4,5},{5,4},{6,7},{7,6},{8,9},{9,8},{10,11... | collective-permute-start | bytes 2654216 | tf_op jit(solution)/shard_map/ppermute | solution.py:331
  136.4 35.8 %collective-permute-start.18 = (bf16[3,3,384,128]{3,2,1,0:T(8,128)(2,1)}, bf16[3,3,384,128]{3,2,1,0:T(8,128)(2,1)}, u32[]{:S(2)}, u32[]{:S(2)}) collective-permute-start(bf16[3,3,384,128]{3,2,1,0:T(8,128)(2,1)} %collective-permute-done.16.refs_17_), channel_id=1, source_target_pairs={{0,1},{1,0},{2,3},{3,2},{4,5},{5,4},{6,7},{7,6},{8,9},{9,8},{10,11... | collective-permute-start | bytes 2654216 | tf_op jit(solution)/shard_map/ppermute | solution.py:331
  137.7 85.5 %collective-permute-start.28 = (bf16[768,768]{1,0:T(8,128)(2,1)}, bf16[768,768]{1,0:T(8,128)(2,1)}, u32[]{:S(2)}, u32[]{:S(2)}) collective-permute-start(bf16[768,768]{1,0:T(8,128)(2,1)} %bitcast.30.refs_0_), channel_id=1, source_target_pairs={{0,4},{1,0},{2,6},{3,2},{4,1},{6,3},{8,12},{9,8},{10,14},{11,10},{... | collective-permute-start | bytes 3538952 | tf_op jit(solution)/shard_map/ppermute | solution.py:331
  172.2 52.8 %collective-permute-start.32 = (bf16[768,768]{1,0:T(8,128)(2,1)}, bf16[768,768]{1,0:T(8,128)(2,1)S(1)}, u32[]{:S(2)}, u32[]{:S(2)}) collective-permute-start(bf16[768,768]{1,0:T(8,128)(2,1)} %copy-done), channel_id=1, source_target_pairs={{4,0},{5,1},{6,2},{7,3},{8,12},{9,13},{10,14},{11,15},{20,16},{21,... | collective-permute-start | bytes 3538952 | tf_op jit(solution)/shard_map/ppermute | solution.py:331
  173.5 53.4 %collective-permute-start.31 = (bf16[768,768]{1,0:T(8,128)(2,1)}, bf16[768,768]{1,0:T(8,128)(2,1)}, u32[]{:S(2)}, u32[]{:S(2)}) collective-permute-start(bf16[768,768]{1,0:T(8,128)(2,1)} %copy-done), channel_id=1, source_target_pairs={{0,1},{1,0},{2,3},{3,2},{4,20},{5,21},{6,22},{7,23},{8,24},{9,25},... | collective-permute-start | bytes 3538952 | tf_op jit(solution)/shard_map/ppermute | solution.py:331
  173.6 1.5 copy-start.3
  175.1 1.3 copy-start.5
  176.4 1.3 copy-start.7
  180.0 12.6 %copy-start.23 = (s32[384]{0:T(512)S(1)}, s32[384]{0:T(512)}, u32[]{:S(2)}) copy-start(s32[384]{0:T(512)} %param.21) | copy-start | bytes 4612
  192.1 36.6 %collective-permute-start.19 = (bf16[2,384,768]{2,1,0:T(8,128)(2,1)}, bf16[2,384,768]{2,1,0:T(8,128)(2,1)S(1)}, u32[]{:S(2)}, u32[]{:S(2)}) collective-permute-start(bf16[2,384,768]{2,1,0:T(8,128)(2,1)} %get-tuple-element.10.kv0), channel_id=1, source_target_pairs={{0,1},{1,0},{2,3},{3,2},{4,5},{5,4},{6,7},{7,6},{8,9},{9,8},{10,11... | collective-permute-start | bytes 3538952 | tf_op jit(solution)/shard_map/ppermute | solution.py:331
  192.6 19.4 %collective-permute-start.20 = (s32[1,512]{1,0:T(1,128)S(1)}, s32[1,512]{1,0:T(1,128)S(1)}, u32[]{:S(2)}, u32[]{:S(2)}) collective-permute-start(s32[1,512]{1,0:T(1,128)S(1)} %bitcast.37), channel_id=1, source_target_pairs={{0,4},{1,5},{2,6},{3,7},{4,0},{5,1},{6,2},{7,3},{8,12},{9,13},{10,... | collective-permute-start | bytes 6152 | tf_op jit(solution)/shard_map/ppermute | solution.py:331
  211.9 5.0 %collective-permute-start.21 = (s32[1,512]{1,0:T(1,128)S(1)}, s32[1,512]{1,0:T(1,128)S(1)}, u32[]{:S(2)}, u32[]{:S(2)}) collective-permute-start(s32[1,512]{1,0:T(1,128)S(1)} %bitcast.38), channel_id=1, source_target_pairs={{0,8},{1,9},{2,10},{3,11},{4,12},{5,13},{6,14},{7,15},{8,0},{9,1},... | collective-permute-start | bytes 6152 | tf_op jit(solution)/shard_map/ppermute | solution.py:331
  216.9 6.3 %collective-permute-start.22 = (s32[1,512]{1,0:T(1,128)S(1)}, s32[1,512]{1,0:T(1,128)S(1)}, u32[]{:S(2)}, u32[]{:S(2)}) collective-permute-start(s32[1,512]{1,0:T(1,128)S(1)} %bitcast.39), channel_id=1, source_target_pairs={{0,12},{1,13},{2,14},{3,15},{4,8},{5,9},{6,10},{7,11},{8,4},{9,5},... | collective-permute-start | bytes 6152 | tf_op jit(solution)/shard_map/ppermute | solution.py:331
  223.2 5.4 %copy-start.21 = (s32[1,512]{1,0:T(1,128)}, s32[1,512]{1,0:T(1,128)S(1)}, u32[]{:S(2)}) copy-start(s32[1,512]{1,0:T(1,128)S(1)} %collective-permute-done.22.refs_3_) | copy-start | bytes 6148
  223.2 17.5 %collective-permute-start.27 = (bf16[768,768]{1,0:T(8,128)(2,1)}, bf16[768,768]{1,0:T(8,128)(2,1)S(1)}, u32[]{:S(2)}, u32[]{:S(2)}) collective-permute-start(bf16[768,768]{1,0:T(8,128)(2,1)} %bitcast.30.refs_0_), channel_id=1, source_target_pairs={{0,1},{1,0},{2,3},{3,2},{4,5},{5,4},{6,7},{7,6},{8,9},{9,8},{10,11... | collective-permute-start | bytes 3538952 | tf_op jit(solution)/shard_map/ppermute | solution.py:331
  223.2 35.6 %collective-permute-start.29 = (bf16[768,768]{1,0:T(8,128)(2,1)}, bf16[768,768]{1,0:T(8,128)(2,1)}, u32[]{:S(2)}, u32[]{:S(2)}) collective-permute-start(bf16[768,768]{1,0:T(8,128)(2,1)} %collective-permute-done.28.refs_2_), channel_id=1, source_target_pairs={{1,17},{3,19},{4,20},{6,22},{9,25},{11,27},{12,28},{14,30},{17,1},... | collective-permute-start | bytes 3538952 | tf_op jit(solution)/shard_map/ppermute | solution.py:331
  225.0 33.8 %collective-permute-start.33 = (bf16[768,768]{1,0:T(8,128)(2,1)S(1)}, bf16[768,768]{1,0:T(8,128)(2,1)}, u32[]{:S(2)}, u32[]{:S(2)}) collective-permute-start(bf16[768,768]{1,0:T(8,128)(2,1)S(1)} %collective-permute-done.32.refs_6_.refs_8_), channel_id=1, source_target_pairs={{0,16},{2,18},{4,5},{5,4},{6,7},{7,6},{8,9},{9,8},{10,11},{11,10},... | collective-permute-start | bytes 3538952 | tf_op jit(solution)/shard_map/ppermute | solution.py:331
  226.9 31.9 %collective-permute-start.34 = (bf16[768,768]{1,0:T(8,128)(2,1)}, bf16[768,768]{1,0:T(8,128)(2,1)}, u32[]{:S(2)}, u32[]{:S(2)}) collective-permute-start(bf16[768,768]{1,0:T(8,128)(2,1)} %collective-permute-done.31.refs_5_), channel_id=1, source_target_pairs={{5,1},{7,3},{8,12},{10,14},{21,17},{23,19},{24,28},{26,30}} | collective-permute-start | bytes 3538952 | tf_op jit(solution)/shard_map/ppermute | solution.py:331
  229.9 1.3 copy-start.18
  232.9 27.8 %copy-start.1 = (bf16[768,768]{1,0:T(8,128)(2,1)S(1)}, bf16[768,768]{1,0:T(8,128)(2,1)}, u32[]{:S(2)}) copy-start(bf16[768,768]{1,0:T(8,128)(2,1)} %copy-done) | copy-start | bytes 3538948
  239.7 8.2 %collective-permute-start.23 = (bf16[384,384]{1,0:T(8,128)(2,1)S(1)}, bf16[384,384]{1,0:T(8,128)(2,1)}, u32[]{:S(2)}, u32[]{:S(2)}) collective-permute-start(bf16[384,384]{1,0:T(8,128)(2,1)S(1)} %get-tuple-element.11.an), channel_id=1, source_target_pairs={{0,1},{1,5},{2,3},{3,7},{4,0},{5,4},{6,2},{7,6},{8,9},{9,13},{10,1... | collective-permute-start | bytes 884744 | tf_op jit(solution)/shard_map/ppermute | solution.py:331
  240.8 18.0 %collective-permute-start.25 = (bf16[384,384]{1,0:T(8,128)(2,1)S(1)}, bf16[384,384]{1,0:T(8,128)(2,1)}, u32[]{:S(2)}, u32[]{:S(2)}) collective-permute-start(bf16[384,384]{1,0:T(8,128)(2,1)S(1)} %get-tuple-element.12), channel_id=1, source_target_pairs={{0,8},{1,12},{2,10},{3,14},{4,9},{5,13},{6,11},{7,15},{8,0},{9,4},... | collective-permute-start | bytes 884744 | tf_op jit(solution)/shard_map/ppermute | solution.py:331
  248.0 10.9 %collective-permute-start.24 = (bf16[384,384]{1,0:T(8,128)(2,1)}, bf16[384,384]{1,0:T(8,128)(2,1)}, u32[]{:S(2)}, u32[]{:S(2)}) collective-permute-start(bf16[384,384]{1,0:T(8,128)(2,1)} %collective-permute-done.23.pn), channel_id=1, source_target_pairs={{0,1},{1,0},{2,3},{3,2},{4,5},{5,4},{6,7},{7,6},{8,9},{9,8},{10,11... | collective-permute-start | bytes 884744 | tf_op jit(solution)/shard_map/ppermute | solution.py:331
  258.7 1.9 collective-permute-start.26
  266.3 15.8 %collective-permute-start.35 = (bf16[384,768]{1,0:T(8,128)(2,1)}, bf16[384,768]{1,0:T(8,128)(2,1)}, u32[]{:S(2)}, u32[]{:S(2)}) collective-permute-start(bf16[384,768]{1,0:T(8,128)(2,1)} %project.3), channel_id=1, source_target_pairs={{0,2},{1,3},{2,0},{3,1},{4,6},{5,7},{6,4},{7,5},{8,10},{9,11},{10,... | collective-permute-start | bytes 1769480 | tf_op jit(solution)/shard_map/ppermute | solution.py:331
  (14 other events, 13.9 us)
